TPU v7x, 32 devices: a whole 2x2x4 slice. The times are simulated.
32 devices in a mesh: grp: 2 (over y), gx: 4 (over x, core), gy: 4 (over z).
Axes of the slice: x: 2, y: 2, z: 4, core: 2. Of those that a mesh axis runs over, the one named last changes fastest.
Arguments:
- ensemble: float32 [128, 3, 32, 1024], P('grp', None, 'gx', 'gy'), parts along dimension 0, may hold values from -16 to 16
- diffusivity: float32 [6, 32, 1024], P('grp', 'gx', 'gy'), parts along dimension 0, may hold values from 0.03 to 0.24
- mixing: float32 [3, 3], replicated, may hold values from -0.6 to 0.6
- obs_cell: int32 [4, 4, 4096], P('gx', 'gy', 'grp'), parts along dimension 2, may hold values from 0 to 2047
- obs_var: int32 [4, 4, 4096], P('gx', 'gy', 'grp'), parts along dimension 2, may hold values from 0 to 2
- obs_value: float32 [4, 4, 4096], P('gx', 'gy', 'grp'), parts along dimension 2, may hold values from -5 to 5
- obs_weight: float32 [4, 4, 4096], P('gx', 'gy', 'grp'), parts along dimension 2, may hold values from 0.5 to 6
Outputs:
- analysis: float32 [128, 3, 32, 1024], P('grp', None, 'gx', 'gy'), parts along dimension 0
There are 2 independent parts, one for each index of `grp`. A program takes and returns all parts, laid end to end along the dimension named above; an argument that names none is the same for every part. Nothing has to cross between parts.
All inputs are finite; a program needn't handle non-finite values.
Results may differ from a plain program's by a relative error of at most 0.0001.
Values sent between devices are 32-bit elements; how exact they have to be, the bound alone decides.
No kernel may reach another device: no remote copies, remote signals or barrier semaphores. Data moves between devices by JAX's collectives and lax.ppermute only.
A program may use at most 64 MiB of HBM per device.

v0:
```python
import math

import jax
import jax.numpy as jnp
from jax import lax
from jax.sharding import PartitionSpec as P

NS_ITERS = 5


def padded_2(cells, sides, width):
    for axis, dim in sides:
        count = lax.axis_size(axis)
        ends = count - 1
        head = lax.slice_in_dim(cells, 0, width, axis=dim)
        tail = lax.slice_in_dim(cells, cells.shape[dim] - width, cells.shape[dim], axis=dim)
        cells = jnp.concatenate(
            [
                lax.ppermute(tail, axis, [(i, (i + 1) % count) for i in range(ends)]),
                cells,
                lax.ppermute(head, axis, [((i + 1) % count, i) for i in range(ends)]),
            ],
            axis=dim,
        )
    return cells


def advance(padded, kappa_field, mixing):
    center = padded[:, :, 1:-1, 1:-1]
    beside = padded[:, :, 2:, 1:-1] + padded[:, :, :-2, 1:-1]
    beside = beside + padded[:, :, 1:-1, 2:] + padded[:, :, 1:-1, :-2]
    coupled = jnp.zeros_like(center)
    for source in range(3):
        coupled = coupled + mixing[:, source][None, :, None, None] * center[:, source][:, None]
    return center + kappa_field[None] * (beside - 4.0 * center) + coupled


def pad_faces(state):
    return padded_2(state, (("gx", 2), ("gy", 3)), 1)


def transform(gram, pull):
    identity = jnp.eye(gram.shape[0], dtype=jnp.float32)
    matrix = identity + gram
    frob_norm = jnp.sqrt(jnp.sum(matrix * matrix))

    def ns_step(step, carry):
        sqrt_iter, inv_iter = carry
        correction = 1.5 * identity - 0.5 * jnp.dot(
            inv_iter, sqrt_iter, precision=lax.Precision.HIGHEST
        )
        return (
            jnp.dot(sqrt_iter, correction, precision=lax.Precision.HIGHEST),
            jnp.dot(correction, inv_iter, precision=lax.Precision.HIGHEST),
        )

    sqrt_iter, inv_iter = lax.fori_loop(0, NS_ITERS, ns_step, (matrix / frob_norm, identity))
    root_inv = inv_iter / jnp.sqrt(frob_norm)
    inverse = jnp.dot(root_inv, root_inv, precision=lax.Precision.HIGHEST)
    mean_shift = jnp.dot(inverse, pull, precision=lax.Precision.HIGHEST)
    return mean_shift[:, None] + root_inv


def local(ensemble, diffusivity, mixing, obs_cell, obs_var, obs_value, obs_weight):
    members = ensemble.shape[0]
    first_state = advance(pad_faces(ensemble), diffusivity, mixing)
    second_state = advance(pad_faces(first_state), diffusivity, mixing)
    cell_count = second_state.shape[2] * second_state.shape[3]
    flat_state = second_state.reshape(members, -1)
    obs_index = obs_var[0, 0] * cell_count + obs_cell[0, 0]
    observed = jnp.take(flat_state, obs_index, axis=1)
    obs_mean = jnp.mean(observed, axis=0)
    obs_total = obs_cell.shape[2] * lax.axis_size("gx") * lax.axis_size("gy")
    factor = 1.0 / math.sqrt((members - 1) * obs_total)
    weight = obs_weight[0, 0]
    spread = (observed - obs_mean) * (weight * factor)
    departure = weight * (obs_value[0, 0] - obs_mean)
    gram_part = jnp.dot(spread, spread.T, precision=lax.Precision.HIGHEST)
    pull_part = jnp.dot(spread, departure, precision=lax.Precision.HIGHEST)
    gram, pull = lax.psum((gram_part, pull_part), ("gx", "gy"))
    state_mean = jnp.mean(second_state, axis=0)
    anomalies = (second_state - state_mean).reshape(members, -1)
    weights = transform(gram, pull)
    moved = jnp.dot(weights.T, anomalies, precision=lax.Precision.HIGHEST)
    return state_mean + moved.reshape(second_state.shape)


def solution(mesh):
    return jax.shard_map(
        local,
        mesh=mesh,
        in_specs=(
            P("grp", None, "gx", "gy"),
            P("grp", "gx", "gy"),
            P(),
            P("gx", "gy", "grp"),
            P("gx", "gy", "grp"),
            P("gx", "gy", "grp"),
            P("gx", "gy", "grp"),
        ),
        out_specs=P("grp", None, "gx", "gy"),
        check_vma=False,
    )
```

profile of v0, /device:TPU:0, one launch (start us, length us, event | category | flops | bytes accessed | tf_op | source)
XLA Modules:
  0.0 146.7 jit_solution(570074319774280910)
XLA Ops:
  0.0 2.0 %copy.48 = f32[64,3,8,256]{3,0,2,1:T(8,128)S(1)} copy(f32[64,3,8,256]{3,2,1,0:T(8,128)} %param.9) | data formatting | bytes 3145728 | tf_op args[0]
  2.1 2.4 %collective-permute-start.1 = (f32[64,3,1,256]{3,0,2,1:T(8,128)S(1)}, f32[64,3,1,256]{3,0,2,1:T(8,128)S(1)}, u32[]{:S(2)}, u32[]{:S(2)}) collective-permute-start(f32[64,3,1,256]{3,0,2,1:T(8,128)S(1)} %get-tuple-element.73), channel_id=1, source_target_pairs={{0,4},{4,8},{8,12},{1,5},{5,9},{9,13},{2,6},{6,10},{10,14},{3,7},{... | collective-permute-start | bytes 589832 | tf_op jit(solution)/shard_map/ppermute | solution.py:19
  4.5 1.3 collective-permute-start
  5.8 1.1 slice_bitcast_fusion.5
  8.2 1.7 %collective-permute-done = f32[64,3,1,256]{3,0,2,1:T(8,128)S(1)} collective-permute-done((f32[64,3,1,256]{3,0,2,1:T(8,128)S(1)}, f32[64,3,1,256]{3,0,2,1:T(8,128)S(1)}, u32[]{:S(2)}, u32[]{:S(2)}) %collective-permute-start) | collective-permute-done | bytes 196640 | tf_op jit(solution)/shard_map/ppermute | solution.py:21
  9.9 1.3 fusion.44
  11.2 1.6 %copy.43 = f32[64,3,10,1]{0,3,2,1:T(1,128)S(1)} copy(f32[64,3,10,1]{3,0,2,1:T(8,128)} %get-tuple-element.62) | data formatting | bytes 15360 | tf_op jit(solution)/shard_map/slice | solution.py:15
  12.8 1.3 collective-permute-start.2
  14.4 4.6 %collective-permute-start.3 = (f32[64,3,10,1]{0,3,2,1:T(1,128)S(1)}, f32[64,3,10,1]{0,3,2,1:T(1,128)S(1)}, u32[]{:S(2)}, u32[]{:S(2)}) collective-permute-start(f32[64,3,10,1]{0,3,2,1:T(1,128)S(1)} %copy.45), channel_id=1, source_target_pairs={{0,1},{1,2},{2,3},{4,5},{5,6},{6,7},{8,9},{9,10},{10,11},{12,13},{... | collective-permute-start | bytes 23048 | tf_op jit(solution)/shard_map/ppermute | solution.py:19
  19.7 2.0 %copy.49 = f32[64,8,256]{2,0,1:T(8,128)} copy(f32[64,8,256]{2,1,0:T(8,128)} %get-tuple-element.69) | data formatting | bytes 1048576 | tf_op jit(solution)/shard_map/mul | solution.py:34
  21.8 2.0 %copy.50 = f32[64,8,256]{2,0,1:T(8,128)} copy(f32[64,8,256]{2,1,0:T(8,128)} %get-tuple-element.71) | data formatting | bytes 1048576 | tf_op jit(solution)/shard_map/mul | solution.py:34
  23.8 1.0 copy.51
  24.8 1.4 copy.44
  26.1 1.3 copy.46
  27.5 5.0 %fusion.14 = f32[64,3,8,256]{3,0,2,1:T(8,128)S(1)} fusion(f32[64,3,8,256]{3,0,2,1:T(8,128)} %copy-done.2, f32[64,3,10,256]{3,0,2,1:T(8,128)S(1)} %constant_dynamic-update-slice_fusion, f32[64,3,10,1]{3,0,2,1:T(8,128)} %copy.46, f32[64,3,10,1]{3,0,2,1:T(8,128)} %copy.44, f32[64,3,1,256]{3,0,2,1:T(8,128)} %copy-done.5, f32[64,3,1,256]{3,0,2,1:T(8,128)} %copy-done.6, ...), kind=kLoop, calls=%fused_computation.27 | loop fusion | flops 6684672 | bytes 7117860 | tf_op jit(solution)/shard_map/add | solution.py:35
  32.5 1.3 collective-permute-start.4
  33.8 6.1 %collective-permute-start.5 = (f32[64,3,1,256]{3,0,2,1:T(8,128)S(1)}, f32[64,3,1,256]{3,0,2,1:T(8,128)S(1)}, u32[]{:S(2)}, u32[]{:S(2)}) collective-permute-start(f32[64,3,1,256]{3,0,2,1:T(8,128)S(1)} %get-tuple-element.64), channel_id=1, source_target_pairs={{0,4},{4,8},{8,12},{1,5},{5,9},{9,13},{2,6},{6,10},{10,14},{3,7},{... | collective-permute-start | bytes 589832 | tf_op jit(solution)/shard_map/ppermute | solution.py:19
  42.0 1.0 copy.52
  43.0 1.3 collective-permute-start.6
  44.6 5.2 %collective-permute-start.7 = (f32[64,3,10,1]{0,3,2,1:T(1,128)S(1)}, f32[64,3,10,1]{0,3,2,1:T(1,128)}, u32[]{:S(2)}, u32[]{:S(2)}) collective-permute-start(f32[64,3,10,1]{0,3,2,1:T(1,128)S(1)} %copy.54), channel_id=1, source_target_pairs={{0,1},{1,2},{2,3},{4,5},{5,6},{6,7},{8,9},{9,10},{10,11},{12,13},{... | collective-permute-start | bytes 23048 | tf_op jit(solution)/shard_map/ppermute | solution.py:19
  49.7 1.2 slice_bitcast_fusion.2
  51.3 1.1 copy.55
  52.5 4.6 %fusion.41 = (f32[3,8,256]{2,1,0:T(8,128)}, f32[64,3,8,256]{3,0,2,1:T(8,128)}) fusion(f32[64,8,256]{2,0,1:T(8,128)} %get-tuple-element.68, f32[3]{0:T(128)S(1)} %copy-done.17, f32[64,8,256]{2,0,1:T(8,128)} %get-tuple-element.67, f32[3]{0:T(128)} %get-tuple-element.47, f32[64,8,256]{2,0,1:T(8,128)} %get-tuple-element.66, f32[3]{0:T(128)S(1)} %copy-done.16, ...), kind=kLoop, calls=%fused_computation.85 | loop fusion | flops 8644608 | bytes 5176356 | tf_op jit(solution)/shard_map/reduce_sum | solution.py:81
  57.1 2.1 %copy.64 = f32[64,3,8,256]{0,3,2,1:T(8,128)S(1)} copy(f32[64,3,8,256]{3,0,2,1:T(8,128)} %get-tuple-element.59) | data formatting | bytes 3145728 | tf_op jit(solution)/shard_map/reshape | solution.py:69
  59.2 7.6 %gather_fusion = f32[2048,64]{1,0:T(8,128)} fusion(f32[64,6144]{0,1:T(8,128)S(1)} %bitcast.68, s32[2048]{0:T(1024)S(1)} %broadcast_clamp_fusion), kind=kCustom, calls=%fused_computation | custom fusion | bytes 1056768 | tf_op jit(solution)/shard_map/jit(_take)/gather | solution.py:71
  66.9 1.9 %select_reduce_fusion = f32[2048]{0:T(1024)S(1)} fusion(f32[2048,64]{1,0:T(8,128)} %gather_fusion, pred[2048]{0:T(1024)(128)(4,1)S(1)} %copy-done.11), kind=kLoop, calls=%fused_computation.40 | loop fusion | flops 260096 | bytes 534528 | tf_op jit(solution)/shard_map/reduce_sum | solution.py:72
  68.8 5.4 %fusion.23 = f32[64,64]{1,0:T(8,128)S(1)} fusion(f32[2048,64]{1,0:T(8,128)} %gather_fusion, f32[2048]{0:T(1024)S(1)} %get-tuple-element.76, f32[2048]{0:T(1024)S(1)} %get-tuple-element.75, pred[2048]{0:T(1024)(128)(4,1)S(1)} %copy-done.11), kind=kOutput, calls=%fused_computation.41 | convolution fusion | flops 101056512 | bytes 559104 | tf_op jit(solution)/shard_map/dot_general | solution.py:78
  74.3 1.3 convolution_bitcast_fusion.1
  75.6 61.1 %all-reduce = (f32[64,64]{1,0:T(8,128)S(1)}, f32[64]{0:T(128)S(1)}) all-reduce(f32[64,64]{1,0:T(8,128)S(1)} %fusion.23, f32[64]{0:T(128)S(1)} %convolution_bitcast_fusion.1), channel_id=1, replica_groups=mesh['grp'=2,'gx'=4,'gy'=4] {'gx','gy'}, use_global_device_ids=true, to_apply=%region_2.3 | all-reduce | flops 4160 | bytes 33280 | tf_op jit(solution)/shard_map/psum | solution.py:80
  138.1 3.2 %while.13 = (s32[]{:T(128)}, f32[64,64]{0,1:T(8,128)S(1)}, f32[64,64]{1,0:T(8,128)S(1)}, s32[]{:T(128)}) while((s32[]{:T(128)}, f32[64,64]{0,1:T(8,128)S(1)}, f32[64,64]{1,0:T(8,128)S(1)}, s32[]{:T(128)}) %tuple.41), condition=%wide.region_5.6_spmd.clone, body=%wide.region_4.5_spmd.clone.sunk | while | flops 9453570 | bytes 213045 | solution.py:57
  142.7 2.0 %fusion.19 = f32[64,3,8,256]{3,0,2,1:T(8,128)S(1)} fusion(f32[3,8,256,64]{2,1,0,3:T(8,128)S(1)} %bitcast.69, f32[3,8,256]{2,1,0:T(8,128)S(1)} %broadcast_multiply_fusion, f32[64]{0:T(128)S(1)} %convolution_bitcast_fusion.2, f32[64,64]{1,0:T(8,128)S(1)} %get-tuple-element.27, f32[]{:T(128)S(6)} %sqrt.7), kind=kOutput, calls=%fused_computation.35 | convolution fusion | flops 302391296 | bytes 3186948 | tf_op jit(solution)/shard_map/dot_general | solution.py:84
  144.7 2.1 %copy.62 = f32[64,3,8,256]{3,2,1,0:T(8,128)} copy(f32[64,3,8,256]{3,0,2,1:T(8,128)S(1)} %fusion.19) | data formatting | bytes 3145728 | tf_op jit(solution)/shard_map/add | solution.py:85
  (92 shorter events, 10.3 us)
Async XLA Ops:
  0.0 5.8 %copy-start = (f32[64,3,8,256]{3,2,1,0:T(8,128)S(1)}, f32[64,3,8,256]{3,2,1,0:T(8,128)}, u32[]{:S(2)}) copy-start(f32[64,3,8,256]{3,2,1,0:T(8,128)} %param.9) | copy-start | bytes 4718596
  2.0 4.9 %copy-start.2 = (f32[64,3,8,256]{3,0,2,1:T(8,128)}, f32[64,3,8,256]{3,0,2,1:T(8,128)S(1)}, u32[]{:S(2)}) copy-start(f32[64,3,8,256]{3,0,2,1:T(8,128)S(1)} %copy.48) | copy-start | bytes 4718596
  2.1 5.5 %collective-permute-start.1 = (f32[64,3,1,256]{3,0,2,1:T(8,128)S(1)}, f32[64,3,1,256]{3,0,2,1:T(8,128)S(1)}, u32[]{:S(2)}, u32[]{:S(2)}) collective-permute-start(f32[64,3,1,256]{3,0,2,1:T(8,128)S(1)} %get-tuple-element.73), channel_id=1, source_target_pairs={{0,4},{4,8},{8,12},{1,5},{5,9},{9,13},{2,6},{6,10},{10,14},{3,7},{... | collective-permute-start | bytes 589832 | tf_op jit(solution)/shard_map/ppermute | solution.py:19
  4.5 3.1 %copy-start.12 = (s32[1,1,2048]{2,1,0:T(1,128)S(1)}, s32[1,1,2048]{2,1,0:T(1,128)}, u32[]{:S(2)}) copy-start(s32[1,1,2048]{2,1,0:T(1,128)} %param.12) | copy-start | bytes 24580
  4.5 3.1 %copy-start.13 = (s32[1,1,2048]{2,1,0:T(1,128)S(1)}, s32[1,1,2048]{2,1,0:T(1,128)}, u32[]{:S(2)}) copy-start(s32[1,1,2048]{2,1,0:T(1,128)} %param.13) | copy-start | bytes 24580
  4.5 5.4 %collective-permute-start = (f32[64,3,1,256]{3,0,2,1:T(8,128)S(1)}, f32[64,3,1,256]{3,0,2,1:T(8,128)S(1)}, u32[]{:S(2)}, u32[]{:S(2)}) collective-permute-start(f32[64,3,1,256]{3,0,2,1:T(8,128)S(1)} %get-tuple-element.72), channel_id=1, source_target_pairs={{4,0},{8,4},{12,8},{5,1},{9,5},{13,9},{6,2},{10,6},{14,10},{7,3},{... | collective-permute-start | bytes 589832 | tf_op jit(solution)/shard_map/ppermute | solution.py:21
  7.6 0.7 copy-start.5
  9.9 1.3 copy-start.6
  11.2 7.8 %copy-start.10 = (f32[3,3]{1,0:T(4,128)S(1)}, f32[3,3]{1,0:T(4,128)}, u32[]{:S(2)}) copy-start(f32[3,3]{1,0:T(4,128)} %param.11) | copy-start | bytes 112
  12.8 12.0 %collective-permute-start.2 = (f32[64,3,10,1]{0,3,2,1:T(1,128)S(1)}, f32[64,3,10,1]{0,3,2,1:T(1,128)S(1)}, u32[]{:S(2)}, u32[]{:S(2)}) collective-permute-start(f32[64,3,10,1]{0,3,2,1:T(1,128)S(1)} %copy.43), channel_id=1, source_target_pairs={{1,0},{2,1},{3,2},{5,4},{6,5},{7,6},{9,8},{10,9},{11,10},{13,12},{... | collective-permute-start | bytes 23048 | tf_op jit(solution)/shard_map/ppermute | solution.py:21
  14.4 11.7 %collective-permute-start.3 = (f32[64,3,10,1]{0,3,2,1:T(1,128)S(1)}, f32[64,3,10,1]{0,3,2,1:T(1,128)S(1)}, u32[]{:S(2)}, u32[]{:S(2)}) collective-permute-start(f32[64,3,10,1]{0,3,2,1:T(1,128)S(1)} %copy.45), channel_id=1, source_target_pairs={{0,1},{1,2},{2,3},{4,5},{5,6},{6,7},{8,9},{9,10},{10,11},{12,13},{... | collective-permute-start | bytes 23048 | tf_op jit(solution)/shard_map/ppermute | solution.py:19
  32.5 8.0 %collective-permute-start.4 = (f32[64,3,1,256]{3,0,2,1:T(8,128)S(1)}, f32[64,3,1,256]{3,0,2,1:T(8,128)S(1)}, u32[]{:S(2)}, u32[]{:S(2)}) collective-permute-start(f32[64,3,1,256]{3,0,2,1:T(8,128)S(1)} %get-tuple-element.65), channel_id=1, source_target_pairs={{4,0},{8,4},{12,8},{5,1},{9,5},{13,9},{6,2},{10,6},{14,10},{7,3},{... | collective-permute-start | bytes 589832 | tf_op jit(solution)/shard_map/ppermute | solution.py:21
  33.8 7.2 %collective-permute-start.5 = (f32[64,3,1,256]{3,0,2,1:T(8,128)S(1)}, f32[64,3,1,256]{3,0,2,1:T(8,128)S(1)}, u32[]{:S(2)}, u32[]{:S(2)}) collective-permute-start(f32[64,3,1,256]{3,0,2,1:T(8,128)S(1)} %get-tuple-element.64), channel_id=1, source_target_pairs={{0,4},{4,8},{8,12},{1,5},{5,9},{9,13},{2,6},{6,10},{10,14},{3,7},{... | collective-permute-start | bytes 589832 | tf_op jit(solution)/shard_map/ppermute | solution.py:19
  40.5 0.7 copy-start.7
  41.0 0.7 copy-start.8
  43.0 8.0 %collective-permute-start.6 = (f32[64,3,10,1]{0,3,2,1:T(1,128)}, f32[64,3,10,1]{0,3,2,1:T(1,128)S(1)}, u32[]{:S(2)}, u32[]{:S(2)}) collective-permute-start(f32[64,3,10,1]{0,3,2,1:T(1,128)} %copy.52), channel_id=1, source_target_pairs={{1,0},{2,1},{3,2},{5,4},{6,5},{7,6},{9,8},{10,9},{11,10},{13,12},{... | collective-permute-start | bytes 23048 | tf_op jit(solution)/shard_map/ppermute | solution.py:21
  44.6 6.7 %collective-permute-start.7 = (f32[64,3,10,1]{0,3,2,1:T(1,128)S(1)}, f32[64,3,10,1]{0,3,2,1:T(1,128)}, u32[]{:S(2)}, u32[]{:S(2)}) collective-permute-start(f32[64,3,10,1]{0,3,2,1:T(1,128)S(1)} %copy.54), channel_id=1, source_target_pairs={{0,1},{1,2},{2,3},{4,5},{5,6},{6,7},{8,9},{9,10},{10,11},{12,13},{... | collective-permute-start | bytes 23048 | tf_op jit(solution)/shard_map/ppermute | solution.py:19
  50.9 1.5 %copy-start.16 = (f32[3]{0:T(128)S(1)}, f32[3]{0:T(128)}, u32[]{:S(2)}) copy-start(f32[3]{0:T(128)} %get-tuple-element.45) | copy-start | bytes 40
  50.9 1.5 %copy-start.17 = (f32[3]{0:T(128)S(1)}, f32[3]{0:T(128)}, u32[]{:S(2)}) copy-start(f32[3]{0:T(128)} %get-tuple-element.46) | copy-start | bytes 40
  59.2 7.7 %copy-start.11 = (pred[2048]{0:T(1024)(128)(4,1)S(1)}, pred[2048]{0:T(1024)(128)(4,1)}, u32[]{:S(2)}) copy-start(pred[2048]{0:T(1024)(128)(4,1)} %compare_and_fusion) | copy-start | bytes 6148
  59.2 9.6 %copy-start.14 = (f32[1,1,2048]{2,1,0:T(1,128)S(1)}, f32[1,1,2048]{2,1,0:T(1,128)}, u32[]{:S(2)}) copy-start(f32[1,1,2048]{2,1,0:T(1,128)} %param.15) | copy-start | bytes 24580
  59.2 9.6 %copy-start.15 = (f32[1,1,2048]{2,1,0:T(1,128)S(1)}, f32[1,1,2048]{2,1,0:T(1,128)}, u32[]{:S(2)}) copy-start(f32[1,1,2048]{2,1,0:T(1,128)} %param.14) | copy-start | bytes 24580
  66.9 7.4 %copy-start.3 = (f32[2048,64]{1,0:T(8,128)S(1)}, f32[2048,64]{1,0:T(8,128)}, u32[]{:S(2)}) copy-start(f32[2048,64]{1,0:T(8,128)} %gather_fusion) | copy-start | bytes 1572868
  66.9 71.2 %copy-start.4 = (f32[64,64]{1,0:T(8,128)S(1)}, f32[64,64]{1,0:T(8,128)}, u32[]{:S(2)}) copy-start(f32[64,64]{1,0:T(8,128)} %fusion.34) | copy-start | bytes 49156
  74.3 67.0 %copy-start.9 = (f32[3,8,256]{2,1,0:T(8,128)S(1)}, f32[3,8,256]{2,1,0:T(8,128)}, u32[]{:S(2)}) copy-start(f32[3,8,256]{2,1,0:T(8,128)} %get-tuple-element.58) | copy-start | bytes 73732
  74.3 67.0 %copy-start.1 = (f32[64,3,8,256]{3,0,2,1:T(8,128)S(1)}, f32[64,3,8,256]{3,0,2,1:T(8,128)}, u32[]{:S(2)}) copy-start(f32[64,3,8,256]{3,0,2,1:T(8,128)} %get-tuple-element.59) | copy-start | bytes 4718596
where the time goes:
time: 148 us; the launch traced here: 147 us
  blocking collectives  61.1 us (41%)
  local copies, waits for them, and re-layouts  33.2 us (22%)
  starting transfers between devices  23.4 us (16%)
  other arithmetic  13.7 us (9%)
  matrix products  11.9 us (8%)
  waiting for transfers between devices  2.14 us (1%)
    psum x1, blocking collectives, local(): gram, pull = lax.psum((gram_part, pull_part), ('gx', 'gy'))  61.1 us
    ppermute x4, starting transfers between devices, padded_2(): lax.ppermute(tail, axis, [(i, (i + 1) % count) for i in range(ends)])  18.2 us
    gather x1, local copies, waits for them, and re-layouts, local(): observed = jnp.take(flat_state, obs_index, axis=1)  7.62 us
    mul x5, local copies, waits for them, and re-layouts, advance(): mixing[:, source][None, :, None, None] * center[:, source][:, None]  7.33 us
    dot_general x1, matrix products, local(): gram_part = jnp.dot(spread, spread.T, precision=lax.Precision.HIGHEST)  5.4 us
    ppermute x4, starting transfers between devices, padded_2(): lax.ppermute(head, axis, [((i + 1) % count, i) for i in range(ends)])  5.16 us
    add x1, other arithmetic, advance(): return center + kappa_field[None] * (beside - 4.0 * center) + coupled  4.97 us
    reduce_sum x1, other arithmetic, local(): state_mean = jnp.mean(second_state, axis=0)  4.63 us
  transfers between devices with their start and end apart: 8, of which 2 were waited for; matrix products, arithmetic and copies ran while one was open for 8% of the time, Pallas kernels for 0%

commit v1 on v0

v1 whole, which is shorter than its diff:
```python
import functools
import math

import jax
import jax.numpy as jnp
from jax import lax
from jax.experimental import pallas as pl
from jax.experimental.pallas import tpu as pltpu
from jax.sharding import PartitionSpec as P

NS_ITERS = 5
LANES = 128
HIGHEST = lax.Precision.HIGHEST
F32 = jnp.float32
BF16 = jnp.bfloat16


def vmem():
    return pl.BlockSpec(memory_space=pltpu.VMEM)


def smem():
    return pl.BlockSpec(memory_space=pltpu.SMEM)


def nt(a, b):
    return lax.dot_general(a, b, (((1,), (1,)), ((), ())), preferred_element_type=F32)


def split_2(x):
    high = x.astype(BF16)
    return high, (x - high.astype(F32)).astype(BF16)


def split_3(x):
    high = x.astype(BF16)
    rest = x - high.astype(F32)
    middle = rest.astype(BF16)
    return high, middle, (rest - middle.astype(F32)).astype(BF16)


def pair_swap(partner, sizes):
    grp, nx, ny = sizes
    pairs = []
    for g in range(grp):
        for x in range(nx):
            for y in range(ny):
                there = partner(g, x, y)
                if there is not None:
                    tg, tx, ty = there
                    pairs.append(((g * nx + x) * ny + y, (tg * nx + tx) * ny + ty))
    return lambda value: lax.ppermute(value, ("grp", "gx", "gy"), pairs)


def along(place, count, phase):
    first = place - (place - phase) % 2
    if first < 0 or first + 1 >= count:
        return None
    return first + 1 if place == first else first


def x_swap(phase, sizes):
    def partner(g, x, y):
        there = along(x, sizes[1], phase)
        if there is not None:
            return g, there, y
        return (g ^ 1, x, y) if sizes[0] % 2 == 0 else None

    return pair_swap(partner, sizes)


def y_swap(phase, sizes):
    def partner(g, x, y):
        there = along(y, sizes[2], phase)
        if there is not None:
            return g, x, there
        return (g, x ^ 1, y) if sizes[1] % 2 == 0 else None

    return pair_swap(partner, sizes)


def all_sum(value, sizes):
    grp, nx, ny = sizes
    if nx & (nx - 1) or ny & (ny - 1) or nx < 2:
        return lax.psum(value, ("gx", "gy"))

    def chip_swap(mask_0, mask_1):
        def partner(g, x, y):
            chip = ((x >> 1) * ny + y) ^ (mask_1 if x & 1 else mask_0)
            return g, ((chip // ny) << 1) | (x & 1), chip % ny

        return pair_swap(partner, sizes)

    core_swap = pair_swap(lambda g, x, y: (g, x ^ 1, y), sizes)
    chips = nx // 2 * ny
    value = value + core_swap(value)
    if chips == 8:
        parts = [chip_swap(a, b)(value) for a, b in ((4, 4), (1, 5), (2, 6), (3, 7))]
        core_1 = lax.axis_index("gx") % 2 == 1
        own = jnp.where(core_1, 0.0, value + parts[0])
        value = own + parts[1] + parts[2] + parts[3]
        return value + core_swap(value)
    step = 1
    while step < chips:
        value = value + chip_swap(step, step)(value)
        step *= 2
    return value


def load_kernel(dims, ens, kappa, state, send_a, send_b, sides, buf, sems):
    k, nv, cx, cy = dims
    rows = nv * cx
    chunks = 4
    part = k // chunks
    copies = []
    half = cy // LANES
    for c in range(chunks):
        span = pl.ds(c * part * rows, part * rows)
        for h in range(half):
            lanes = slice(h * LANES, (h + 1) * LANES)
            copies.append(pltpu.make_async_copy(ens.at[span, lanes], buf.at[h, span], sems.at[c, h]))
            copies[-1].start()
    for c in range(chunks):
        for h in range(half):
            copies[c * half + h].wait()
            for r in range(cx):
                for v in range(nv):
                    value = buf[h, pl.ds(c * part * rows + v * cx + r, part, stride=rows), :]
                    at = pl.ds(((r + 2) * nv + v) * k + c * part, part)
                    state[at, h * LANES : (h + 1) * LANES] = value
    block = nv * k
    even_x = lax.axis_index("gx") % 2 == 0
    top = 2 * block
    bottom = (cx + 1) * block
    for ref, near_top in ((send_a, jnp.logical_not(even_x)), (send_b, even_x)):
        near = jnp.where(near_top, top, bottom)
        second = jnp.where(near_top, top + block, bottom - block)
        for j in range(0, block, 64):
            ref[pl.ds(j, 64), :] = state[pl.ds(pl.multiple_of(near + j, 64), 64), :]
            ref[pl.ds(block + j, 64), :] = state[pl.ds(pl.multiple_of(second + j, 64), 64), :]
        for v in range(nv):
            edge = jnp.where(near_top, kappa[v, 0:1, :], kappa[v, cx - 1 : cx, :])
            ref[pl.ds(2 * block + v, 1), :] = edge
        ref[pl.ds(2 * block + nv, 8 - nv), :] = jnp.zeros((8 - nv, cy), F32)

    lane = lax.broadcasted_iota(jnp.int32, (1, LANES), 1)
    total = jnp.zeros((k, LANES), F32)
    total_k = jnp.zeros((8, LANES), F32)
    for r in range(cx):
        for v in range(nv):
            place = 2 * (nv * (r + 1) + v)
            base = ((r + 2) * nv + v) * k
            low = (lane >= place) & (lane < place + 2)
            high = (lane >= 64 + place) & (lane < 64 + place + 2)

            def add(acc, right, left):
                acc = jnp.where(low, pltpu.roll(right, (place + 2) % LANES, 1), acc)
                return jnp.where(high, pltpu.roll(left, 64 + place, 1), acc)

            total = add(total, state[pl.ds(base, k), cy - LANES :], state[pl.ds(base, k), :LANES])
            row = kappa[v, r : r + 1, :]
            total_k = add(
                total_k,
                jnp.broadcast_to(row[:, cy - LANES :], (8, LANES)),
                jnp.broadcast_to(row[:, :LANES], (8, LANES)),
            )
    sides[0:k, :] = total
    sides[k : k + 8, :] = total_k


def scatter_kernel(dims, cell, var, value, weight, out):
    k, nv, cx, cy = dims
    count = cell.shape[1]
    row = cell[...] // cy * nv + var[...]
    column = cell[...] % cy
    square = weight[...] * weight[...]
    rows = 32
    hit = lax.broadcasted_iota(jnp.int32, (rows, count), 0) == row
    parts = split_3(square) + split_3(square * value[...])
    left = [jnp.where(hit, p.astype(F32), 0.0).astype(BF16) for p in parts]
    one = (lax.broadcasted_iota(jnp.int32, (cy, count), 0) == column).astype(F32).astype(BF16)
    got = nt(jnp.concatenate(left, axis=0), one)
    piece = [got[i * rows : (i + 1) * rows] for i in range(6)]
    out[0:rows, :] = piece[0] + piece[1] + piece[2]
    out[rows : 2 * rows, :] = piece[3] + piece[4] + piece[5]


def forecast_kernel(
    dims, factor, mixing, state_in, recv_a, recv_b, sides, halo, corner_a, corner_b, kappa, cells,
    state, anomalies, means, gram, first, kext, spread, moved,
):
    k, nv, cx, cy = dims
    block = nv * k
    gx = lax.axis_index("gx")
    nx = lax.axis_size("gx")
    even_x = gx % 2 == 0
    has_up = gx > 0
    has_down = gx < nx - 1
    up_is_a = jnp.logical_not(even_x)

    def pick(ref_is_a, has, a, b):
        return jnp.where(has, jnp.where(ref_is_a, a, b), 0.0)

    for j in range(0, 2 * block, 64):
        a = recv_a[pl.ds(j, 64), :]
        b = recv_b[pl.ds(j, 64), :]
        up_at = (block if j < block else -block) + j
        state[pl.ds(up_at, 64), :] = pick(up_is_a, has_up, a, b)
        state[pl.ds((cx + 2) * block + j, 64), :] = pick(even_x, has_down, a, b)
    for v in range(nv):
        a = recv_a[pl.ds(2 * block + v, 1), :]
        b = recv_b[pl.ds(2 * block + v, 1), :]
        kext[pl.ds(v, 1), :] = pick(up_is_a, has_up, a, b)
        kext[pl.ds((cx + 1) * 8 + v, 1), :] = pick(even_x, has_down, a, b)
        for r in range(cx):
            kext[pl.ds((r + 1) * 8 + v, 1), :] = kappa[v, r : r + 1, :]
            spread[pl.ds(r * 8 + v, 1), :] = cells[pl.ds(r * nv + v, 1), :]
            spread[pl.ds(r * 8 + nv + v, 1), :] = cells[pl.ds(32 + r * nv + v, 1), :]

    lane = lax.broadcasted_iota(jnp.int32, (1, LANES), 1)
    slot = lane % 64
    inside = (slot >= 2 * nv) & (slot < 2 * nv * (cx + 1))
    up_corner = pick(up_is_a, has_up, corner_a[...], corner_b[...])
    down_corner = pick(even_x, has_down, corner_a[...], corner_b[...])
    far = 2 * nv * cx
    columns = jnp.where(slot < 2 * nv, pltpu.roll(up_corner, LANES - far, 1), halo[...])
    columns = jnp.where(
        (slot >= 2 * nv * (cx + 1)) & (slot < 2 * nv * (cx + 2)), pltpu.roll(down_corner, far, 1), columns
    )
    kcol = columns[k : k + 1, :]
    columns = columns[0:k, :]

    own = sides[0:k, :]
    beside = jnp.where(
        lane < 64,
        pltpu.roll(columns, 1, 1) + pltpu.roll(own, 65, 1),
        pltpu.roll(columns, LANES - 1, 1) + pltpu.roll(own, 63, 1),
    )
    step = 2 * nv
    beside = beside + pltpu.roll(columns, step, 1) + pltpu.roll(columns, LANES - step, 1)
    which = slot // 2 % nv
    mixed = jnp.zeros((k, LANES), F32)
    for shift in range(1 - nv, nv):
        coef = jnp.zeros((1, LANES), F32)
        for v in range(nv):
            if 0 <= v + shift < nv:
                coef = jnp.where(which == v, mixing[v, v + shift], coef)
        source = pltpu.roll(columns, (-2 * shift) % LANES, 1) if shift else columns
        mixed = mixed + coef * source
    first_columns = jnp.where(inside, columns + kcol * (beside - 4.0 * columns) + mixed, 0.0)

    half = cy // LANES

    def advance(source, side, r, store):
        eight = pl.ds(pl.multiple_of(r * 8, 8), 8)
        kappas = [kext[eight, h * LANES : (h + 1) * LANES] for h in range(half)]
        for v in range(nv):
            at = 2 * (nv * r + v)
            left_edge = pltpu.roll(side, (LANES - 1 - at) & (LANES - 1), 1)
            right_edge = pltpu.roll(side, (2 * LANES - 1 - 64 - at) & (LANES - 1), 1)
            base = (r + 1) * block

            def load(row, w, h):
                return source[pl.ds(pl.multiple_of(base + row * block + w * k, k), k), h * LANES : (h + 1) * LANES]

            center = [load(0, v, h) for h in range(half)]
            ahead = [pltpu.roll(c, 1, 1) for c in center]
            behind = [pltpu.roll(c, LANES - 1, 1) for c in center]
            for h in range(half):
                kap = kappas[h][v : v + 1]
                left = jnp.where(lane == 0, left_edge if h == 0 else ahead[h - 1], ahead[h])
                right = jnp.where(lane == LANES - 1, right_edge if h == half - 1 else behind[h + 1], behind[h])
                around = (load(-1, v, h) + load(1, v, h)) + (left + right)
                out = (1.0 - 4.0 * kap + mixing[v, v]) * center[h] + kap * around
                for w in range(nv):
                    if w != v:
                        out = out + mixing[v, w] * load(0, w, h)
                store(v, h, out)

    def step_1(r, carry):
        def store(v, h, out):
            first[pl.ds(pl.multiple_of(r * block + v * k, k), k), h * LANES : (h + 1) * LANES] = out

        advance(state, columns, r, store)
        return carry

    lax.fori_loop(0, cx + 2, step_1, 0)

    sub = lax.broadcasted_iota(jnp.int32, (8, 1), 0)

    def step_2(r, carry):
        eight = pl.ds(pl.multiple_of((r - 1) * 8, 8), 8)
        spreads = [spread[eight, h * LANES : (h + 1) * LANES] for h in range(half)]
        found = [jnp.zeros((8, LANES), F32) for h in range(half)]

        def store(v, h, out):
            q = (r - 1) * nv + v
            mean = jnp.sum(out, axis=0, keepdims=True) * (1.0 / k)
            found[h] = jnp.where(sub == v, mean, found[h])
            part = out - mean
            s2 = spreads[h][v : v + 1]
            s1 = spreads[h][nv + v : nv + v + 1]
            at = pl.ds(pl.multiple_of(q * cy + h * LANES, LANES), LANES)
            high, low = split_2(part)
            anomalies[0:k, at] = high
            anomalies[k : 2 * k, at] = low
            high, low = split_2(part * (s2 * (factor * factor)))
            moved[0:k, at] = high
            moved[k : 2 * k, at] = low
            pull = jnp.broadcast_to((s1 - mean * s2) * factor, (16, LANES))
            high, low = split_2(pull)
            moved[2 * k : 2 * k + 16, at] = high
            moved[2 * k + 16 : 2 * k + 32, at] = low

        advance(first_view(), first_columns, r, store)
        for h in range(half):
            means[eight, h * LANES : (h + 1) * LANES] = found[h]
        return carry

    class first_view:
        def __getitem__(self, index):
            return first[pl.ds(pl.multiple_of(index[0].start - block, k), k), index[1]]

    lax.fori_loop(1, cx + 1, step_2, 0)

    got = nt(moved[...], anomalies[...])
    whole = got[:, 0:k] + got[:, k : 2 * k]
    matrix = whole[0:k] + whole[k : 2 * k]
    pull = whole[2 * k : 2 * k + 8] + whole[2 * k + 16 : 2 * k + 24]
    gram[0 : k // 2, :] = jnp.concatenate([matrix[0 : k // 2], matrix[k // 2 :]], axis=1)
    gram[k // 2 : k // 2 + 8, :] = jnp.concatenate([pull, pull], axis=1)


def apply_kernel(dims, gram, anomalies, means, out, buf, sems):
    k, nv, cx, cy = dims
    rows = nv * cx
    row = lax.broadcasted_iota(jnp.int32, (k, k), 0)
    col = lax.broadcasted_iota(jnp.int32, (k, k), 1)
    eye = (row == col).astype(F32)
    both = gram[...]
    matrix = jnp.concatenate([both[0 : k // 2, 0:k], both[0 : k // 2, k : 2 * k]], axis=0) + eye
    pull = both[k // 2 : k // 2 + 8, 0:k]
    norm = jnp.sqrt(jnp.sum(jnp.sum(matrix * matrix, axis=1, keepdims=True), axis=0, keepdims=True))

    def dot(a, b):
        return jnp.dot(a, b, precision=HIGHEST, preferred_element_type=F32)

    root = matrix / norm
    correction = 1.5 * eye - 0.5 * root
    carried = jnp.concatenate([correction, dot(pull, correction)], axis=0)
    root = dot(root, correction)
    for i in range(1, NS_ITERS):
        correction = 1.5 * eye - 0.5 * dot(carried[0:k], root)
        if i < NS_ITERS - 1:
            root = dot(root, correction)
        carried = dot(carried, correction)
    shift = dot(carried[k:], carried[0:k]) / norm
    weights = carried[0:k] / jnp.sqrt(norm) + shift[0:1, :]
    high, low = split_2(weights)
    high_2 = jnp.concatenate([high, high], axis=1)
    for v in range(nv):
        for r in range(cx):
            q = r * nv + v
            at = slice(q * cy, (q + 1) * cy)
            value = jnp.dot(high_2, anomalies[:, at], preferred_element_type=F32)
            value = value + jnp.dot(low, anomalies[0:k, at], preferred_element_type=F32)
            value = value + means[r * 8 + v : r * 8 + v + 1, :]
            for h in range(cy // LANES):
                buf[h, pl.ds(v * cx + r, k, stride=rows), :] = value[:, h * LANES : (h + 1) * LANES]
    copies = []
    for h in range(cy // LANES):
        copies.append(pltpu.make_async_copy(buf.at[h], out.at[:, h * LANES : (h + 1) * LANES], sems.at[h]))
        copies[-1].start()
    for copy in copies:
        copy.wait()


def local(sizes, ensemble, diffusivity, mixing, obs_cell, obs_var, obs_value, obs_weight):
    k, nv, cx, cy = ensemble.shape
    dims = (k, nv, cx, cy)
    assert k == 64 and nv == 3 and cx == 8 and cy % LANES == 0
    block = nv * k
    rows = nv * cx
    grp, nx, ny = sizes
    count = obs_cell.shape[2]
    factor = 1.0 / math.sqrt((k - 1) * count * nx * ny)
    limits = pltpu.CompilerParams(vmem_limit_bytes=48 << 20)

    def shape(*dims, dtype=F32):
        return jax.ShapeDtypeStruct(dims, dtype)

    state, send_a, send_b, sides = pl.pallas_call(
        functools.partial(load_kernel, dims),
        name="load",
        in_specs=[pl.BlockSpec(memory_space=pl.ANY), vmem()],
        out_specs=[vmem()] * 4,
        out_shape=[
            shape((cx + 4) * block, cy),
            shape(2 * block + 8, cy),
            shape(2 * block + 8, cy),
            shape(k + 8, LANES),
        ],
        scratch_shapes=[pltpu.VMEM((cy // LANES, k * rows, LANES), F32), pltpu.SemaphoreType.DMA((4, cy // LANES))],
        compiler_params=limits,
    )(ensemble.reshape(k * rows, cy), diffusivity)

    recv_b = x_swap(1, sizes)(send_b)
    recv_a = x_swap(0, sizes)(send_a)
    side_a = y_swap(0, sizes)(sides)
    side_b = y_swap(1, sizes)(sides)

    cells = pl.pallas_call(
        functools.partial(scatter_kernel, dims),
        name="scatter",
        in_specs=[vmem()] * 4,
        out_specs=vmem(),
        out_shape=shape(64, cy),
        compiler_params=limits,
    )(*(a.reshape(1, count) for a in (obs_cell, obs_var, obs_value, obs_weight)))

    gy = lax.axis_index("gy")
    lane = lax.broadcasted_iota(jnp.int32, (1, LANES), 1)
    from_a = (gy % 2 == 1) == (lane < 64)
    there = jnp.where(lane < 64, gy > 0, gy < ny - 1)
    halo = jnp.where(there, jnp.where(from_a, side_a, side_b), 0.0)
    corner_b = x_swap(1, sizes)(halo)
    corner_a = x_swap(0, sizes)(halo)

    _, anomalies, means, gram = pl.pallas_call(
        functools.partial(forecast_kernel, dims, factor),
        name="forecast",
        in_specs=[smem()] + [vmem()] * 9,
        out_specs=[vmem()] * 4,
        out_shape=[
            shape((cx + 4) * block, cy),
            shape(2 * k, rows * cy, dtype=BF16),
            shape(cx * 8, cy),
            shape(k // 2 + 8, 2 * k),
        ],
        scratch_shapes=[
            pltpu.VMEM(((cx + 2) * block, cy), F32),
            pltpu.VMEM(((cx + 2) * 8, cy), F32),
            pltpu.VMEM((cx * 8, cy), F32),
            pltpu.VMEM((2 * k + 32, rows * cy), BF16),
        ],
        input_output_aliases={1: 0},
        compiler_params=limits,
    )(mixing, state, recv_a, recv_b, sides, halo, corner_a, corner_b, diffusivity, cells)

    gram = all_sum(gram, sizes)

    out = pl.pallas_call(
        functools.partial(apply_kernel, dims),
        name="apply",
        in_specs=[vmem()] * 3,
        out_specs=pl.BlockSpec(memory_space=pl.ANY),
        out_shape=shape(k * rows, cy),
        scratch_shapes=[pltpu.VMEM((cy // LANES, k * rows, LANES), F32), pltpu.SemaphoreType.DMA((cy // LANES,))],
        compiler_params=limits,
    )(gram, anomalies, means)
    return out.reshape(k, nv, cx, cy)


def solution(mesh):
    sizes = tuple(mesh.shape[a] for a in ("grp", "gx", "gy"))
    return jax.shard_map(
        functools.partial(local, sizes),
        mesh=mesh,
        in_specs=(
            P("grp", None, "gx", "gy"),
            P("grp", "gx", "gy"),
            P(),
            P("gx", "gy", "grp"),
            P("gx", "gy", "grp"),
            P("gx", "gy", "grp"),
            P("gx", "gy", "grp"),
        ),
        out_specs=P("grp", None, "gx", "gy"),
        check_vma=False,
    )
```

time: 148 us -> 40.5 us (0.27)
  blocking collectives: 61.1 us -> 0 us
  local copies, waits for them, and re-layouts: 33.2 us -> 4.73 us
  other arithmetic: 13.7 us -> 0.03 us
  Pallas kernels: 0 us -> 13.1 us
  matrix products: 11.9 us -> 0 us
  starting transfers between devices: 23.4 us -> 11.9 us
  waiting for transfers between devices: 2.14 us -> 10.3 us
    psum x1 -> x0, blocking collectives: 61.1 us -> none  [local(): gram, pull = lax.psum((gram_part, pull_part), ('gx', 'gy'))]
    pallas_call x0 -> x4, Pallas kernels: none -> 13.1 us  [the longest x1 6.8 us: local(): pl.pallas_call(functools.partial(forecast_kernel, dims, factor), name='fo...]
    dot_general x20 -> x0, matrix products: 11.9 us -> none  [the longest x1 5.4 us: local(): gram_part = jnp.dot(spread, spread.T, precision=lax.Precision.HIGHEST)]
    ppermute x8 -> x12, starting transfers between devices: 23.4 us -> 11.9 us  [pair_swap(): return lambda value: lax.ppermute(value, ('grp', 'gx', 'gy'), pairs)]
    ppermute x8 -> x12, waiting for transfers between devices: 2.14 us -> 10.3 us  [pair_swap(): return lambda value: lax.ppermute(value, ('grp', 'gx', 'gy'), pairs)]
    gather x1 -> x0, local copies, waits for them, and re-layouts: 7.62 us -> none  [local(): observed = jnp.take(flat_state, obs_index, axis=1)]
    mul x5 -> x0, local copies, waits for them, and re-layouts: 7.33 us -> none  [advance(): mixing[:, source][None, :, None, None] * center[:, source][:, None]]
    reduce_sum x3 -> x0, other arithmetic: 7.19 us -> none  [the longest x1 4.63 us: local(): state_mean = jnp.mean(second_state, axis=0)]
  transfers between devices with their start and end apart: 8 -> 12, of which waited for: 2 -> 8; matrix products, arithmetic and copies ran while one was open for 8% -> 0% of each run, Pallas kernels for 0% -> 1%
where the time goes in v1:
time: 40.5 us; the launch traced here: 40.2 us
  Pallas kernels  13.1 us (32%)
  starting transfers between devices  11.9 us (29%)
  waiting for transfers between devices  10.3 us (25%)
  local copies, waits for them, and re-layouts  4.73 us (12%)
    ppermute x12, starting transfers between devices, pair_swap(): return lambda value: lax.ppermute(value, ('grp', 'gx', 'gy'), pairs)  11.9 us
    ppermute x12, waiting for transfers between devices, pair_swap(): return lambda value: lax.ppermute(value, ('grp', 'gx', 'gy'), pairs)  10.3 us
    pallas_call x1, Pallas kernels, local(): pl.pallas_call(functools.partial(forecast_kernel, dims, factor), name='fo...  6.8 us
    unnamed x20, local copies, waits for them, and re-layouts  4.73 us
    pallas_call x1, Pallas kernels, local(): pl.pallas_call(functools.partial(apply_kernel, dims), name='apply', in_sp...  3.98 us
    pallas_call x1, Pallas kernels, local(): pl.pallas_call(functools.partial(load_kernel, dims), name='load', in_spec...  1.8 us
  transfers between devices with their start and end apart: 12, of which 8 were waited for; matrix products, arithmetic and copies ran while one was open for 0% of the time, Pallas kernels for 1%

profile of v1, /device:TPU:0, one launch (start us, length us, event | category | flops | bytes accessed | tf_op | source)
XLA Modules:
  0.0 40.2 jit_solution(11368998605439317068)
XLA Ops:
  0.0 1.4 %copy-done = f32[64,3,8,256]{3,2,1,0:T(8,128)S(1)} copy-done((f32[64,3,8,256]{3,2,1,0:T(8,128)S(1)}, f32[64,3,8,256]{3,2,1,0:T(8,128)}, u32[]{:S(2)}) %copy-start) | copy-done | bytes 1572888
  1.4 0.7 %copy-done.3 = f32[3,8,256]{2,1,0:T(8,128)S(1)} copy-done((f32[3,8,256]{2,1,0:T(8,128)S(1)}, f32[3,8,256]{2,1,0:T(8,128)}, u32[]{:S(2)}) %copy-start.3) | copy-done | bytes 24600
  2.2 1.8 %load.1 = (f32[2304,256]{1,0:T(8,128)S(1)}, f32[392,256]{1,0:T(8,128)}, f32[392,256]{1,0:T(8,128)}, f32[72,128]{1,0:T(8,128)S(1)}) custom-call(f32[1536,256]{1,0:T(8,128)S(1)} %bitcast.6, f32[3,8,256]{2,1,0:T(8,128)S(1)} %copy-done.3), custom_call_target="tpu_custom_call" | custom-call | tf_op jit(solution)/shard_map/load/pallas_call | solution.py:392
  4.0 0.5 %collective-permute-start = (f32[392,256]{1,0:T(8,128)}, f32[392,256]{1,0:T(8,128)S(1)}, u32[]{:S(2)}, u32[]{:S(2)}) collective-permute-start(f32[392,256]{1,0:T(8,128)} %get-tuple-element.13), channel_id=1, source_target_pairs={{0,4},{1,5},{2,6},{3,7},{4,0},{5,1},{6,2},{7,3},{8,12},{9,13},{10,... | collective-permute-start | bytes 1204232 | tf_op jit(solution)/shard_map/ppermute | solution.py:52
  4.5 2.6 %collective-permute-start.1 = (f32[392,256]{1,0:T(8,128)}, f32[392,256]{1,0:T(8,128)S(1)}, u32[]{:S(2)}, u32[]{:S(2)}) collective-permute-start(f32[392,256]{1,0:T(8,128)} %get-tuple-element.14), channel_id=1, source_target_pairs={{0,16},{1,17},{2,18},{3,19},{4,8},{5,9},{6,10},{7,11},{8,4},{9,5},... | collective-permute-start | bytes 1204232 | tf_op jit(solution)/shard_map/ppermute | solution.py:52
  7.1 0.1 collective-permute-start.3
  7.2 3.1 %collective-permute-start.2 = (f32[72,128]{1,0:T(8,128)S(1)}, f32[72,128]{1,0:T(8,128)S(1)}, u32[]{:S(2)}, u32[]{:S(2)}) collective-permute-start(f32[72,128]{1,0:T(8,128)S(1)} %get-tuple-element.15.sides), channel_id=1, source_target_pairs={{0,1},{1,0},{2,3},{3,2},{4,5},{5,4},{6,7},{7,6},{8,9},{9,8},{10,11... | collective-permute-start | bytes 110600 | tf_op jit(solution)/shard_map/ppermute | solution.py:52
  10.3 0.0 collective-permute-done.3
  10.3 1.9 %collective-permute-done.2 = f32[72,128]{1,0:T(8,128)S(1)} collective-permute-done((f32[72,128]{1,0:T(8,128)S(1)}, f32[72,128]{1,0:T(8,128)S(1)}, u32[]{:S(2)}, u32[]{:S(2)}) %collective-permute-start.2) | collective-permute-done | bytes 36896 | tf_op jit(solution)/shard_map/ppermute | solution.py:52
  12.2 0.8 %collective-permute-start.5 = (f32[72,128]{1,0:T(8,128)S(1)}, f32[72,128]{1,0:T(8,128)S(1)}, u32[]{:S(2)}, u32[]{:S(2)}) collective-permute-start(f32[72,128]{1,0:T(8,128)S(1)} %select_select_fusion.halo), channel_id=1, source_target_pairs={{0,16},{1,17},{2,18},{3,19},{4,8},{5,9},{6,10},{7,11},{8,4},{9,5},... | collective-permute-start | bytes 110600 | tf_op jit(solution)/shard_map/ppermute | solution.py:52
  13.0 0.2 collective-permute-start.4
  13.2 0.5 %scatter.1.cells = f32[64,256]{1,0:T(8,128)S(1)} custom-call(s32[1,2048]{1,0:T(1,128)S(1)} %bitcast.7, s32[1,2048]{1,0:T(1,128)S(1)} %bitcast.8, f32[1,2048]{1,0:T(1,128)S(1)} %bitcast.9, f32[1,2048]{1,0:T(1,128)S(1)} %bitcast.10), custom_call_target="tpu_custom_call" | custom-call | tf_op jit(solution)/shard_map/scatter/pallas_call | solution.py:412
  13.7 2.5 %collective-permute-done.5.corner_b = f32[72,128]{1,0:T(8,128)S(1)} collective-permute-done((f32[72,128]{1,0:T(8,128)S(1)}, f32[72,128]{1,0:T(8,128)S(1)}, u32[]{:S(2)}, u32[]{:S(2)}) %collective-permute-start.5) | collective-permute-done | bytes 36896 | tf_op jit(solution)/shard_map/ppermute | solution.py:52
  16.2 0.0 collective-permute-done.4.corner_a
  16.2 0.0 collective-permute-done.recv_a
  16.2 0.0 collective-permute-done.1.recv_b
  16.2 6.8 %forecast.1 = (f32[2304,256]{1,0:T(8,128)S(1)}, bf16[128,6144]{1,0:T(8,128)(2,1)S(1)}, f32[64,256]{1,0:T(8,128)S(1)}, f32[40,128]{1,0:T(8,128)S(1)}) custom-call(f32[3,3]{1,0:T(4,128)S(1)} %copy-done.9, f32[2304,256]{1,0:T(8,128)S(1)} %get-tuple-element.12.state_in, f32[392,256]{1,0:T(8,128)S(1)} %collective-permute-done.recv_a, ...), custom_call_target="tpu_custom_call", output_to_operand_aliasing={{0}: (1, {})} | custom-call | tf_op jit(solution)/shard_map/forecast/pallas_call | solution.py:429
  23.0 1.1 %copy-done.1 = bf16[128,6144]{1,0:T(8,128)(2,1)} copy-done((bf16[128,6144]{1,0:T(8,128)(2,1)}, bf16[128,6144]{1,0:T(8,128)(2,1)S(1)}, u32[]{:S(2)}) %copy-start.1) | copy-done | bytes 1572888
  24.2 0.0 collective-permute-start.6
  24.2 1.2 %collective-permute-done.6 = f32[40,128]{1,0:T(8,128)S(1)} collective-permute-done((f32[40,128]{1,0:T(8,128)S(1)}, f32[40,128]{1,0:T(8,128)S(1)}, u32[]{:S(2)}, u32[]{:S(2)}) %collective-permute-start.6) | collective-permute-done | bytes 20512 | tf_op jit(solution)/shard_map/ppermute | solution.py:52
  25.4 2.6 %collective-permute-start.10 = (f32[40,128]{1,0:T(8,128)S(1)}, f32[40,128]{1,0:T(8,128)S(1)}, u32[]{:S(2)}, u32[]{:S(2)}) collective-permute-start(f32[40,128]{1,0:T(8,128)S(1)} %add.27), channel_id=1, source_target_pairs={{0,3},{1,2},{2,1},{3,0},{4,15},{5,14},{6,13},{7,12},{8,11},{9,10},... | collective-permute-start | bytes 61448 | tf_op jit(solution)/shard_map/ppermute | solution.py:52
  28.0 0.9 %collective-permute-start.9 = (f32[40,128]{1,0:T(8,128)S(1)}, f32[40,128]{1,0:T(8,128)S(1)}, u32[]{:S(2)}, u32[]{:S(2)}) collective-permute-start(f32[40,128]{1,0:T(8,128)S(1)} %add.27), channel_id=1, source_target_pairs={{0,2},{1,3},{2,0},{3,1},{4,14},{5,15},{6,12},{7,13},{8,10},{9,11},... | collective-permute-start | bytes 61448 | tf_op jit(solution)/shard_map/ppermute | solution.py:52
  28.9 0.9 %collective-permute-start.8 = (f32[40,128]{1,0:T(8,128)S(1)}, f32[40,128]{1,0:T(8,128)S(1)}, u32[]{:S(2)}, u32[]{:S(2)}) collective-permute-start(f32[40,128]{1,0:T(8,128)S(1)} %add.27), channel_id=1, source_target_pairs={{0,1},{1,0},{2,3},{3,2},{4,13},{5,12},{6,15},{7,14},{8,9},{9,8},{1... | collective-permute-start | bytes 61448 | tf_op jit(solution)/shard_map/ppermute | solution.py:52
  29.8 0.2 collective-permute-start.7
  30.0 1.0 %collective-permute-done.10 = f32[40,128]{1,0:T(8,128)S(1)} collective-permute-done((f32[40,128]{1,0:T(8,128)S(1)}, f32[40,128]{1,0:T(8,128)S(1)}, u32[]{:S(2)}, u32[]{:S(2)}) %collective-permute-start.10) | collective-permute-done | bytes 20512 | tf_op jit(solution)/shard_map/ppermute | solution.py:52
  31.0 1.7 %collective-permute-done.9 = f32[40,128]{1,0:T(8,128)S(1)} collective-permute-done((f32[40,128]{1,0:T(8,128)S(1)}, f32[40,128]{1,0:T(8,128)S(1)}, u32[]{:S(2)}, u32[]{:S(2)}) %collective-permute-start.9) | collective-permute-done | bytes 20512 | tf_op jit(solution)/shard_map/ppermute | solution.py:52
  32.7 0.2 collective-permute-done.8
  32.9 0.7 %collective-permute-done.7 = f32[40,128]{1,0:T(8,128)S(1)} collective-permute-done((f32[40,128]{1,0:T(8,128)S(1)}, f32[40,128]{1,0:T(8,128)S(1)}, u32[]{:S(2)}, u32[]{:S(2)}) %collective-permute-start.7) | collective-permute-done | bytes 20512 | tf_op jit(solution)/shard_map/ppermute | solution.py:52
  33.6 0.1 collective-permute-start.11
  33.7 1.2 %collective-permute-done.11 = f32[40,128]{1,0:T(8,128)S(1)} collective-permute-done((f32[40,128]{1,0:T(8,128)S(1)}, f32[40,128]{1,0:T(8,128)S(1)}, u32[]{:S(2)}, u32[]{:S(2)}) %collective-permute-start.11) | collective-permute-done | bytes 20512 | tf_op jit(solution)/shard_map/ppermute | solution.py:52
  34.8 1.4 %copy-done.2 = bf16[128,6144]{1,0:T(8,128)(2,1)S(1)} copy-done((bf16[128,6144]{1,0:T(8,128)(2,1)S(1)}, bf16[128,6144]{1,0:T(8,128)(2,1)}, u32[]{:S(2)}) %copy-start.2) | copy-done | bytes 1572888
  36.2 4.0 %apply.1 = f32[1536,256]{1,0:T(8,128)} custom-call(f32[40,128]{1,0:T(8,128)S(1)} %add.32.gram, bf16[128,6144]{1,0:T(8,128)(2,1)S(1)} %copy-done.2, f32[64,256]{1,0:T(8,128)S(1)} %get-tuple-element.18.means), custom_call_target="tpu_custom_call" | custom-call | tf_op jit(solution)/shard_map/apply/pallas_call | solution.py:452
  (21 shorter events, 0.1 us)
Async XLA Ops:
  0.0 1.4 %copy-start = (f32[64,3,8,256]{3,2,1,0:T(8,128)S(1)}, f32[64,3,8,256]{3,2,1,0:T(8,128)}, u32[]{:S(2)}) copy-start(f32[64,3,8,256]{3,2,1,0:T(8,128)} %param.7) | copy-start | bytes 4718596
  1.4 0.7 %copy-start.3 = (f32[3,8,256]{2,1,0:T(8,128)S(1)}, f32[3,8,256]{2,1,0:T(8,128)}, u32[]{:S(2)}) copy-start(f32[3,8,256]{2,1,0:T(8,128)} %kappa.3) | copy-start | bytes 73732
  2.1 11.0 %copy-start.5 = (s32[1,1,2048]{2,1,0:T(1,128)S(1)}, s32[1,1,2048]{2,1,0:T(1,128)}, u32[]{:S(2)}) copy-start(s32[1,1,2048]{2,1,0:T(1,128)} %param.10) | copy-start | bytes 24580
  2.1 11.0 %copy-start.6 = (s32[1,1,2048]{2,1,0:T(1,128)S(1)}, s32[1,1,2048]{2,1,0:T(1,128)}, u32[]{:S(2)}) copy-start(s32[1,1,2048]{2,1,0:T(1,128)} %param.11) | copy-start | bytes 24580
  2.2 11.0 %copy-start.7 = (f32[1,1,2048]{2,1,0:T(1,128)S(1)}, f32[1,1,2048]{2,1,0:T(1,128)}, u32[]{:S(2)}) copy-start(f32[1,1,2048]{2,1,0:T(1,128)} %param.12) | copy-start | bytes 24580
  2.2 11.0 %copy-start.8 = (f32[1,1,2048]{2,1,0:T(1,128)S(1)}, f32[1,1,2048]{2,1,0:T(1,128)}, u32[]{:S(2)}) copy-start(f32[1,1,2048]{2,1,0:T(1,128)} %param.13) | copy-start | bytes 24580
  2.2 14.1 %copy-start.4 = (f32[3,8,256]{2,1,0:T(8,128)S(1)}, f32[3,8,256]{2,1,0:T(8,128)}, u32[]{:S(2)}) copy-start(f32[3,8,256]{2,1,0:T(8,128)} %kappa.3) | copy-start | bytes 73732
  2.2 14.1 %copy-start.9 = (f32[3,3]{1,0:T(4,128)S(1)}, f32[3,3]{1,0:T(4,128)}, u32[]{:S(2)}) copy-start(f32[3,3]{1,0:T(4,128)} %mixing.1) | copy-start | bytes 112
  4.0 12.2 %collective-permute-start = (f32[392,256]{1,0:T(8,128)}, f32[392,256]{1,0:T(8,128)S(1)}, u32[]{:S(2)}, u32[]{:S(2)}) collective-permute-start(f32[392,256]{1,0:T(8,128)} %get-tuple-element.13), channel_id=1, source_target_pairs={{0,4},{1,5},{2,6},{3,7},{4,0},{5,1},{6,2},{7,3},{8,12},{9,13},{10,... | collective-permute-start | bytes 1204232 | tf_op jit(solution)/shard_map/ppermute | solution.py:52
  4.5 11.7 %collective-permute-start.1 = (f32[392,256]{1,0:T(8,128)}, f32[392,256]{1,0:T(8,128)S(1)}, u32[]{:S(2)}, u32[]{:S(2)}) collective-permute-start(f32[392,256]{1,0:T(8,128)} %get-tuple-element.14), channel_id=1, source_target_pairs={{0,16},{1,17},{2,18},{3,19},{4,8},{5,9},{6,10},{7,11},{8,4},{9,5},... | collective-permute-start | bytes 1204232 | tf_op jit(solution)/shard_map/ppermute | solution.py:52
  7.1 3.2 %collective-permute-start.3 = (f32[72,128]{1,0:T(8,128)S(1)}, f32[72,128]{1,0:T(8,128)S(1)}, u32[]{:S(2)}, u32[]{:S(2)}) collective-permute-start(f32[72,128]{1,0:T(8,128)S(1)} %get-tuple-element.15.sides), channel_id=1, source_target_pairs={{0,4},{1,2},{2,1},{3,7},{4,0},{5,6},{6,5},{7,3},{8,12},{9,10},{10,... | collective-permute-start | bytes 110600 | tf_op jit(solution)/shard_map/ppermute | solution.py:52
  7.2 5.0 %collective-permute-start.2 = (f32[72,128]{1,0:T(8,128)S(1)}, f32[72,128]{1,0:T(8,128)S(1)}, u32[]{:S(2)}, u32[]{:S(2)}) collective-permute-start(f32[72,128]{1,0:T(8,128)S(1)} %get-tuple-element.15.sides), channel_id=1, source_target_pairs={{0,1},{1,0},{2,3},{3,2},{4,5},{5,4},{6,7},{7,6},{8,9},{9,8},{10,11... | collective-permute-start | bytes 110600 | tf_op jit(solution)/shard_map/ppermute | solution.py:52
  12.2 4.0 %collective-permute-start.5 = (f32[72,128]{1,0:T(8,128)S(1)}, f32[72,128]{1,0:T(8,128)S(1)}, u32[]{:S(2)}, u32[]{:S(2)}) collective-permute-start(f32[72,128]{1,0:T(8,128)S(1)} %select_select_fusion.halo), channel_id=1, source_target_pairs={{0,16},{1,17},{2,18},{3,19},{4,8},{5,9},{6,10},{7,11},{8,4},{9,5},... | collective-permute-start | bytes 110600 | tf_op jit(solution)/shard_map/ppermute | solution.py:52
  13.0 3.2 %collective-permute-start.4 = (f32[72,128]{1,0:T(8,128)S(1)}, f32[72,128]{1,0:T(8,128)S(1)}, u32[]{:S(2)}, u32[]{:S(2)}) collective-permute-start(f32[72,128]{1,0:T(8,128)S(1)} %select_select_fusion.halo), channel_id=1, source_target_pairs={{0,4},{1,5},{2,6},{3,7},{4,0},{5,1},{6,2},{7,3},{8,12},{9,13},{10,... | collective-permute-start | bytes 110600 | tf_op jit(solution)/shard_map/ppermute | solution.py:52
  23.0 1.2 %copy-start.1 = (bf16[128,6144]{1,0:T(8,128)(2,1)}, bf16[128,6144]{1,0:T(8,128)(2,1)S(1)}, u32[]{:S(2)}) copy-start(bf16[128,6144]{1,0:T(8,128)(2,1)S(1)} %get-tuple-element.17.anomalies) | copy-start | bytes 4718596
  24.2 1.2 %collective-permute-start.6 = (f32[40,128]{1,0:T(8,128)S(1)}, f32[40,128]{1,0:T(8,128)S(1)}, u32[]{:S(2)}, u32[]{:S(2)}) collective-permute-start(f32[40,128]{1,0:T(8,128)S(1)} %get-tuple-element.16), channel_id=1, source_target_pairs={{0,4},{1,5},{2,6},{3,7},{4,0},{5,1},{6,2},{7,3},{8,12},{9,13},{10,... | collective-permute-start | bytes 61448 | tf_op jit(solution)/shard_map/ppermute | solution.py:52
  25.4 5.6 %collective-permute-start.10 = (f32[40,128]{1,0:T(8,128)S(1)}, f32[40,128]{1,0:T(8,128)S(1)}, u32[]{:S(2)}, u32[]{:S(2)}) collective-permute-start(f32[40,128]{1,0:T(8,128)S(1)} %add.27), channel_id=1, source_target_pairs={{0,3},{1,2},{2,1},{3,0},{4,15},{5,14},{6,13},{7,12},{8,11},{9,10},... | collective-permute-start | bytes 61448 | tf_op jit(solution)/shard_map/ppermute | solution.py:52
  28.0 4.7 %collective-permute-start.9 = (f32[40,128]{1,0:T(8,128)S(1)}, f32[40,128]{1,0:T(8,128)S(1)}, u32[]{:S(2)}, u32[]{:S(2)}) collective-permute-start(f32[40,128]{1,0:T(8,128)S(1)} %add.27), channel_id=1, source_target_pairs={{0,2},{1,3},{2,0},{3,1},{4,14},{5,15},{6,12},{7,13},{8,10},{9,11},... | collective-permute-start | bytes 61448 | tf_op jit(solution)/shard_map/ppermute | solution.py:52
  28.9 4.0 %collective-permute-start.8 = (f32[40,128]{1,0:T(8,128)S(1)}, f32[40,128]{1,0:T(8,128)S(1)}, u32[]{:S(2)}, u32[]{:S(2)}) collective-permute-start(f32[40,128]{1,0:T(8,128)S(1)} %add.27), channel_id=1, source_target_pairs={{0,1},{1,0},{2,3},{3,2},{4,13},{5,12},{6,15},{7,14},{8,9},{9,8},{1... | collective-permute-start | bytes 61448 | tf_op jit(solution)/shard_map/ppermute | solution.py:52
  29.8 3.8 %collective-permute-start.7 = (f32[40,128]{1,0:T(8,128)S(1)}, f32[40,128]{1,0:T(8,128)S(1)}, u32[]{:S(2)}, u32[]{:S(2)}) collective-permute-start(f32[40,128]{1,0:T(8,128)S(1)} %add.27), channel_id=1, source_target_pairs={{0,8},{1,9},{2,10},{3,11},{4,12},{5,13},{6,14},{7,15},{8,0},{9,1},... | collective-permute-start | bytes 61448 | tf_op jit(solution)/shard_map/ppermute | solution.py:52
  33.6 1.3 %collective-permute-start.11 = (f32[40,128]{1,0:T(8,128)S(1)}, f32[40,128]{1,0:T(8,128)S(1)}, u32[]{:S(2)}, u32[]{:S(2)}) collective-permute-start(f32[40,128]{1,0:T(8,128)S(1)} %add_add_fusion), channel_id=1, source_target_pairs={{0,4},{1,5},{2,6},{3,7},{4,0},{5,1},{6,2},{7,3},{8,12},{9,13},{10,... | collective-permute-start | bytes 61448 | tf_op jit(solution)/shard_map/ppermute | solution.py:52
  34.8 1.4 %copy-start.2 = (bf16[128,6144]{1,0:T(8,128)(2,1)S(1)}, bf16[128,6144]{1,0:T(8,128)(2,1)}, u32[]{:S(2)}) copy-start(bf16[128,6144]{1,0:T(8,128)(2,1)} %copy-done.1) | copy-start | bytes 4718596

commit v2 on v1

--- a/solution.py
+++ b/solution.py
@@ -96,9 +96,7 @@
     value = value + core_swap(value)
     if chips == 8:
         parts = [chip_swap(a, b)(value) for a, b in ((4, 4), (1, 5), (2, 6), (3, 7))]
-        core_1 = lax.axis_index("gx") % 2 == 1
-        own = jnp.where(core_1, 0.0, value + parts[0])
-        value = own + parts[1] + parts[2] + parts[3]
+        value = 0.5 * (value + parts[0]) + parts[1] + parts[2] + parts[3]
         return value + core_swap(value)
     step = 1
     while step < chips:
@@ -107,7 +105,10 @@
     return value
 
 
-def load_kernel(dims, ens, kappa, state, send_a, send_b, sides, buf, sems):
+def load_kernel(dims, ens, *refs):
+    small_in, (state, send_a, send_b, sides, side_a, side_b) = refs[:6], refs[6:12]
+    small, (buf, sems, small_sems) = refs[12:18], refs[18:]
+    kappa = small[0]
     k, nv, cx, cy = dims
     rows = nv * cx
     chunks = 4
@@ -120,6 +121,9 @@
             lanes = slice(h * LANES, (h + 1) * LANES)
             copies.append(pltpu.make_async_copy(ens.at[span, lanes], buf.at[h, span], sems.at[c, h]))
             copies[-1].start()
+    small_copies = [pltpu.make_async_copy(a, b, small_sems.at[i]) for i, (a, b) in enumerate(zip(small_in, small))]
+    for copy in small_copies:
+        copy.start()
     for c in range(chunks):
         for h in range(half):
             copies[c * half + h].wait()
@@ -128,6 +132,8 @@
                     value = buf[h, pl.ds(c * part * rows + v * cx + r, part, stride=rows), :]
                     at = pl.ds(((r + 2) * nv + v) * k + c * part, part)
                     state[at, h * LANES : (h + 1) * LANES] = value
+    for copy in small_copies:
+        copy.wait()
     block = nv * k
     even_x = lax.axis_index("gx") % 2 == 0
     top = 2 * block
@@ -166,6 +172,15 @@
             )
     sides[0:k, :] = total
     sides[k : k + 8, :] = total_k
+    gy = lax.axis_index("gy")
+    even_y = gy % 2 == 0
+    has_left = gy > 0
+    has_right = gy < lax.axis_size("gy") - 1
+    for ref, to_right in ((side_a, even_y), (side_b, jnp.logical_not(even_y))):
+        start = jnp.where(jnp.where(to_right, has_right, has_left), jnp.where(to_right, 0, 64), LANES)
+        wanted = (lane >= start) & (lane < start + 64)
+        ref[0:k, :] = jnp.where(wanted, total, 0.0)
+        ref[k : k + 8, :] = jnp.where(wanted, total_k, 0.0)
 
 
 def scatter_kernel(dims, cell, var, value, weight, out):
@@ -185,52 +200,10 @@
     out[rows : 2 * rows, :] = piece[3] + piece[4] + piece[5]
 
 
-def forecast_kernel(
-    dims, factor, mixing, state_in, recv_a, recv_b, sides, halo, corner_a, corner_b, kappa, cells,
-    state, anomalies, means, gram, first, kext, spread, moved,
-):
-    k, nv, cx, cy = dims
-    block = nv * k
-    gx = lax.axis_index("gx")
-    nx = lax.axis_size("gx")
-    even_x = gx % 2 == 0
-    has_up = gx > 0
-    has_down = gx < nx - 1
-    up_is_a = jnp.logical_not(even_x)
-
-    def pick(ref_is_a, has, a, b):
-        return jnp.where(has, jnp.where(ref_is_a, a, b), 0.0)
-
-    for j in range(0, 2 * block, 64):
-        a = recv_a[pl.ds(j, 64), :]
-        b = recv_b[pl.ds(j, 64), :]
-        up_at = (block if j < block else -block) + j
-        state[pl.ds(up_at, 64), :] = pick(up_is_a, has_up, a, b)
-        state[pl.ds((cx + 2) * block + j, 64), :] = pick(even_x, has_down, a, b)
-    for v in range(nv):
-        a = recv_a[pl.ds(2 * block + v, 1), :]
-        b = recv_b[pl.ds(2 * block + v, 1), :]
-        kext[pl.ds(v, 1), :] = pick(up_is_a, has_up, a, b)
-        kext[pl.ds((cx + 1) * 8 + v, 1), :] = pick(even_x, has_down, a, b)
-        for r in range(cx):
-            kext[pl.ds((r + 1) * 8 + v, 1), :] = kappa[v, r : r + 1, :]
-            spread[pl.ds(r * 8 + v, 1), :] = cells[pl.ds(r * nv + v, 1), :]
-            spread[pl.ds(r * 8 + nv + v, 1), :] = cells[pl.ds(32 + r * nv + v, 1), :]
-
-    lane = lax.broadcasted_iota(jnp.int32, (1, LANES), 1)
+def first_columns_of(dims, mixing, columns, kcol, own, lane):
+    k, nv, cx, cy = dims
     slot = lane % 64
     inside = (slot >= 2 * nv) & (slot < 2 * nv * (cx + 1))
-    up_corner = pick(up_is_a, has_up, corner_a[...], corner_b[...])
-    down_corner = pick(even_x, has_down, corner_a[...], corner_b[...])
-    far = 2 * nv * cx
-    columns = jnp.where(slot < 2 * nv, pltpu.roll(up_corner, LANES - far, 1), halo[...])
-    columns = jnp.where(
-        (slot >= 2 * nv * (cx + 1)) & (slot < 2 * nv * (cx + 2)), pltpu.roll(down_corner, far, 1), columns
-    )
-    kcol = columns[k : k + 1, :]
-    columns = columns[0:k, :]
-
-    own = sides[0:k, :]
     beside = jnp.where(
         lane < 64,
         pltpu.roll(columns, 1, 1) + pltpu.roll(own, 65, 1),
@@ -247,83 +220,177 @@
                 coef = jnp.where(which == v, mixing[v, v + shift], coef)
         source = pltpu.roll(columns, (-2 * shift) % LANES, 1) if shift else columns
         mixed = mixed + coef * source
-    first_columns = jnp.where(inside, columns + kcol * (beside - 4.0 * columns) + mixed, 0.0)
-
+    return jnp.where(inside, columns + kcol * (beside - 4.0 * columns) + mixed, 0.0)
+
+
+def advance(dims, mixing, kext, load, side, e, lane, store):
+    k, nv, cx, cy = dims
     half = cy // LANES
-
-    def advance(source, side, r, store):
-        eight = pl.ds(pl.multiple_of(r * 8, 8), 8)
-        kappas = [kext[eight, h * LANES : (h + 1) * LANES] for h in range(half)]
-        for v in range(nv):
-            at = 2 * (nv * r + v)
-            left_edge = pltpu.roll(side, (LANES - 1 - at) & (LANES - 1), 1)
-            right_edge = pltpu.roll(side, (2 * LANES - 1 - 64 - at) & (LANES - 1), 1)
-            base = (r + 1) * block
-
-            def load(row, w, h):
-                return source[pl.ds(pl.multiple_of(base + row * block + w * k, k), k), h * LANES : (h + 1) * LANES]
-
-            center = [load(0, v, h) for h in range(half)]
+    eight = pl.ds(pl.multiple_of(e * 8, 8), 8)
+    kappas = [kext[eight, h * LANES : (h + 1) * LANES] for h in range(half)]
+    first_lane = lane == 0
+    last_lane = lane == LANES - 1
+    for v in range(nv):
+        at = 2 * (nv * e + v)
+        to_left = (LANES - 1 - at) & (LANES - 1)
+        to_right = (2 * LANES - 1 - 64 - at) & (LANES - 1)
+        kap = [jnp.broadcast_to(kappas[h][v : v + 1], (8, LANES)) for h in range(half)]
+        own = [1.0 - 4.0 * kap[h] + mixing[v, v] for h in range(half)]
+        others = [(w, mixing[v, w]) for w in range(nv) if w != v]
+        for j in range(0, k, 8):
+            edge = side[pl.ds(j, 8), :]
+            left_edge = pltpu.roll(edge, to_left, 1)
+            right_edge = pltpu.roll(edge, to_right, 1)
+            center = [load(0, v, j, h) for h in range(half)]
             ahead = [pltpu.roll(c, 1, 1) for c in center]
             behind = [pltpu.roll(c, LANES - 1, 1) for c in center]
             for h in range(half):
-                kap = kappas[h][v : v + 1]
-                left = jnp.where(lane == 0, left_edge if h == 0 else ahead[h - 1], ahead[h])
-                right = jnp.where(lane == LANES - 1, right_edge if h == half - 1 else behind[h + 1], behind[h])
-                around = (load(-1, v, h) + load(1, v, h)) + (left + right)
-                out = (1.0 - 4.0 * kap + mixing[v, v]) * center[h] + kap * around
-                for w in range(nv):
-                    if w != v:
-                        out = out + mixing[v, w] * load(0, w, h)
-                store(v, h, out)
-
-    def step_1(r, carry):
-        def store(v, h, out):
-            first[pl.ds(pl.multiple_of(r * block + v * k, k), k), h * LANES : (h + 1) * LANES] = out
-
-        advance(state, columns, r, store)
+                left = jnp.where(first_lane, left_edge if h == 0 else ahead[h - 1], ahead[h])
+                right = jnp.where(last_lane, right_edge if h == half - 1 else behind[h + 1], behind[h])
+                around = (load(-1, v, j, h) + load(1, v, j, h)) + (left + right)
+                out = own[h] * center[h] + kap[h] * around
+                for w, factor in others:
+                    out = out + factor * load(0, w, j, h)
+                store(v, j, h, out)
+
+
+def rows_forecast(
+    dims, factor, mixing, kext, spread, state, first, side, first_side, rows_1, rows_2, outs, lane
+):
+    k, nv, cx, cy = dims
+    block = nv * k
+    half = cy // LANES
+    anomalies, means, moved, kept = outs
+
+    def loader(ref, base):
+        def load(row, w, j, h):
+            at = pl.multiple_of(base + row * block + w * k + j, 8)
+            return ref[pl.ds(at, 8), h * LANES : (h + 1) * LANES]
+
+        return load
+
+    def step_1(i, carry):
+        e = rows_1[1](i)
+
+        def store(v, j, h, out):
+            first[pl.ds(pl.multiple_of(e * block + v * k + j, 8), 8), h * LANES : (h + 1) * LANES] = out
+
+        advance(dims, mixing, kext, loader(state, (e + 1) * block), side, e, lane, store)
         return carry
 
-    lax.fori_loop(0, cx + 2, step_1, 0)
-
+    lax.fori_loop(0, rows_1[0], step_1, 0)
     sub = lax.broadcasted_iota(jnp.int32, (8, 1), 0)
 
-    def step_2(r, carry):
-        eight = pl.ds(pl.multiple_of((r - 1) * 8, 8), 8)
+    def step_2(i, carry):
+        e = rows_2[1](i)
+        eight = pl.ds(pl.multiple_of((e - 1) * 8, 8), 8)
         spreads = [spread[eight, h * LANES : (h + 1) * LANES] for h in range(half)]
-        found = [jnp.zeros((8, LANES), F32) for h in range(half)]
-
-        def store(v, h, out):
-            q = (r - 1) * nv + v
-            mean = jnp.sum(out, axis=0, keepdims=True) * (1.0 / k)
-            found[h] = jnp.where(sub == v, mean, found[h])
-            part = out - mean
-            s2 = spreads[h][v : v + 1]
-            s1 = spreads[h][nv + v : nv + v + 1]
-            at = pl.ds(pl.multiple_of(q * cy + h * LANES, LANES), LANES)
-            high, low = split_2(part)
-            anomalies[0:k, at] = high
-            anomalies[k : 2 * k, at] = low
-            high, low = split_2(part * (s2 * (factor * factor)))
-            moved[0:k, at] = high
-            moved[k : 2 * k, at] = low
-            pull = jnp.broadcast_to((s1 - mean * s2) * factor, (16, LANES))
-            high, low = split_2(pull)
-            moved[2 * k : 2 * k + 16, at] = high
-            moved[2 * k + 16 : 2 * k + 32, at] = low
-
-        advance(first_view(), first_columns, r, store)
+
+        def store(v, j, h, out):
+            kept[pl.ds(v * k + j, 8), h * LANES : (h + 1) * LANES] = out
+
+        advance(dims, mixing, kext, loader(first, e * block), first_side, e, lane, store)
         for h in range(half):
-            means[eight, h * LANES : (h + 1) * LANES] = found[h]
+            found = jnp.zeros((8, LANES), F32)
+            for v in range(nv):
+                lanes = slice(h * LANES, (h + 1) * LANES)
+                out = kept[v * k : (v + 1) * k, lanes]
+                mean = jnp.sum(out, axis=0, keepdims=True) * (1.0 / k)
+                found = jnp.where(sub == v, mean, found)
+                s2 = spreads[h][v : v + 1]
+                s1 = spreads[h][nv + v : nv + v + 1]
+                at = pl.ds(pl.multiple_of((i * nv + v) * cy + h * LANES, LANES), LANES)
+                scale = s2 * (factor * factor)
+                for j in range(0, k, 16):
+                    part = out[j : j + 16] - mean
+                    high, low = split_2(part)
+                    anomalies[j : j + 16, at] = high
+                    anomalies[k + j : k + j + 16, at] = low
+                    high, low = split_2(part * scale)
+                    moved[j : j + 16, at] = high
+                    moved[k + j : k + j + 16, at] = low
+                pull = jnp.broadcast_to((s1 - mean * s2) * factor, (16, LANES))
+                high, low = split_2(pull)
+                moved[2 * k : 2 * k + 16, at] = high
+                moved[2 * k + 16 : 2 * k + 32, at] = low
+            means[pl.ds(pl.multiple_of(i * 8, 8), 8), h * LANES : (h + 1) * LANES] = found
         return carry
 
-    class first_view:
-        def __getitem__(self, index):
-            return first[pl.ds(pl.multiple_of(index[0].start - block, k), k), index[1]]
-
-    lax.fori_loop(1, cx + 1, step_2, 0)
-
-    got = nt(moved[...], anomalies[...])
+    lax.fori_loop(0, rows_2[0], step_2, 0)
+    return nt(moved[...], anomalies[...])
+
+
+def set_rows(dims, kappa, cells, kext, spread):
+    k, nv, cx, cy = dims
+    for v in range(nv):
+        for r in range(cx):
+            kext[pl.ds((r + 1) * 8 + v, 1), :] = kappa[v, r : r + 1, :]
+            spread[pl.ds(r * 8 + v, 1), :] = cells[pl.ds(r * nv + v, 1), :]
+            spread[pl.ds(r * 8 + nv + v, 1), :] = cells[pl.ds(32 + r * nv + v, 1), :]
+
+
+def inner_kernel(
+    dims, factor, mixing, state, sides, halo, kappa, cells,
+    first, anomalies, means, partial, kext, spread, first_side, moved, kept,
+):
+    k, nv, cx, cy = dims
+    set_rows(dims, kappa, cells, kext, spread)
+    lane = lax.broadcasted_iota(jnp.int32, (1, LANES), 1)
+    first_side[...] = first_columns_of(
+        dims, mixing, halo[0:k, :], halo[k : k + 1, :], sides[0:k, :], lane
+    )
+    partial[...] = rows_forecast(
+        dims, factor, mixing, kext, spread, state, first, halo, first_side,
+        (cx - 2, lambda i: i + 2), (cx - 4, lambda i: i + 3),
+        (anomalies, means, moved, kept), lane,
+    )
+
+
+def edge_kernel(
+    dims, factor, mixing, state_in, first_in, partial, recv_a, recv_b, sides, halo, corner_a, corner_b, kappa, cells,
+    state, first, anomalies, means, gram, kext, spread, side, first_side, moved, kept,
+):
+    k, nv, cx, cy = dims
+    block = nv * k
+    gx = lax.axis_index("gx")
+    nx = lax.axis_size("gx")
+    even_x = gx % 2 == 0
+    has_up = gx > 0
+    has_down = gx < nx - 1
+    up_is_a = jnp.logical_not(even_x)
+
+    def pick(ref_is_a, has, a, b):
+        return jnp.where(has, jnp.where(ref_is_a, a, b), 0.0)
+
+    for j in range(0, 2 * block, 32):
+        a = recv_a[pl.ds(j, 32), :]
+        b = recv_b[pl.ds(j, 32), :]
+        up_at = (block if j < block else -block) + j
+        state[pl.ds(up_at, 32), :] = pick(up_is_a, has_up, a, b)
+        state[pl.ds((cx + 2) * block + j, 32), :] = pick(even_x, has_down, a, b)
+    set_rows(dims, kappa, cells, kext, spread)
+    for v in range(nv):
+        a = recv_a[pl.ds(2 * block + v, 1), :]
+        b = recv_b[pl.ds(2 * block + v, 1), :]
+        kext[pl.ds(v, 1), :] = pick(up_is_a, has_up, a, b)
+        kext[pl.ds((cx + 1) * 8 + v, 1), :] = pick(even_x, has_down, a, b)
+
+    lane = lax.broadcasted_iota(jnp.int32, (1, LANES), 1)
+    slot = lane % 64
+    up_corner = pick(up_is_a, has_up, corner_a[...], corner_b[...])
+    down_corner = pick(even_x, has_down, corner_a[...], corner_b[...])
+    far = 2 * nv * cx
+    columns = jnp.where(slot < 2 * nv, pltpu.roll(up_corner, LANES - far, 1), halo[...])
+    columns = jnp.where(
+        (slot >= 2 * nv * (cx + 1)) & (slot < 2 * nv * (cx + 2)), pltpu.roll(down_corner, far, 1), columns
+    )
+    side[...] = columns[0:k, :]
+    first_side[...] = first_columns_of(dims, mixing, columns[0:k, :], columns[k : k + 1, :], sides[0:k, :], lane)
+    got = partial[...] + rows_forecast(
+        dims, factor, mixing, kext, spread, state, first, side, first_side,
+        (4, lambda i: jnp.where(i < 2, i, i + cx - 2)), (4, lambda i: jnp.where(i < 2, i + 1, i + cx - 3)),
+        (anomalies, means, moved, kept), lane,
+    )
     whole = got[:, 0:k] + got[:, k : 2 * k]
     matrix = whole[0:k] + whole[k : 2 * k]
     pull = whole[2 * k : 2 * k + 8] + whole[2 * k + 16 : 2 * k + 24]
@@ -331,7 +398,7 @@
     gram[k // 2 : k // 2 + 8, :] = jnp.concatenate([pull, pull], axis=1)
 
 
-def apply_kernel(dims, gram, anomalies, means, out, buf, sems):
+def apply_kernel(dims, gram, inner, inner_means, edge, edge_means, out, buf, sems):
     k, nv, cx, cy = dims
     rows = nv * cx
     row = lax.broadcasted_iota(jnp.int32, (k, k), 0)
@@ -360,11 +427,14 @@
     high_2 = jnp.concatenate([high, high], axis=1)
     for v in range(nv):
         for r in range(cx):
-            q = r * nv + v
-            at = slice(q * cy, (q + 1) * cy)
+            deep = 2 <= r < cx - 2
+            i = r - 2 if deep else (r if r < 2 else r - cx + 4)
+            anomalies = inner if deep else edge
+            means = inner_means if deep else edge_means
+            at = slice((i * nv + v) * cy, (i * nv + v + 1) * cy)
             value = jnp.dot(high_2, anomalies[:, at], preferred_element_type=F32)
             value = value + jnp.dot(low, anomalies[0:k, at], preferred_element_type=F32)
-            value = value + means[r * 8 + v : r * 8 + v + 1, :]
+            value = value + means[i * 8 + v : i * 8 + v + 1, :]
             for h in range(cy // LANES):
                 buf[h, pl.ds(v * cx + r, k, stride=rows), :] = value[:, h * LANES : (h + 1) * LANES]
     copies = []
@@ -384,30 +454,36 @@
     grp, nx, ny = sizes
     count = obs_cell.shape[2]
     factor = 1.0 / math.sqrt((k - 1) * count * nx * ny)
-    limits = pltpu.CompilerParams(vmem_limit_bytes=48 << 20)
+    limits = pltpu.CompilerParams(vmem_limit_bytes=16 << 20)
 
     def shape(*dims, dtype=F32):
         return jax.ShapeDtypeStruct(dims, dtype)
 
-    state, send_a, send_b, sides = pl.pallas_call(
+    small = (diffusivity, mixing) + tuple(a.reshape(1, count) for a in (obs_cell, obs_var, obs_value, obs_weight))
+    state, send_a, send_b, sides, side_a, side_b, kappa, mixing, *obs = pl.pallas_call(
         functools.partial(load_kernel, dims),
         name="load",
-        in_specs=[pl.BlockSpec(memory_space=pl.ANY), vmem()],
-        out_specs=[vmem()] * 4,
+        in_specs=[pl.BlockSpec(memory_space=pltpu.HBM)] * 7,
+        out_specs=[vmem()] * 12,
         out_shape=[
             shape((cx + 4) * block, cy),
             shape(2 * block + 8, cy),
             shape(2 * block + 8, cy),
             shape(k + 8, LANES),
-        ],
-        scratch_shapes=[pltpu.VMEM((cy // LANES, k * rows, LANES), F32), pltpu.SemaphoreType.DMA((4, cy // LANES))],
+            shape(k + 8, LANES),
+            shape(k + 8, LANES),
+        ]
+        + [shape(*a.shape, dtype=a.dtype) for a in small],
+        scratch_shapes=[pltpu.VMEM((cy // LANES, k * rows, LANES), F32), pltpu.SemaphoreType.DMA((4, cy // LANES)), pltpu.SemaphoreType.DMA((6,))],
         compiler_params=limits,
-    )(ensemble.reshape(k * rows, cy), diffusivity)
+    )(
+        *(pltpu.with_memory_space_constraint(a, pltpu.HBM) for a in (ensemble.reshape(k * rows, cy),) + small)
+    )
 
     recv_b = x_swap(1, sizes)(send_b)
+    side_a = y_swap(0, sizes)(side_a)
+    side_b = y_swap(1, sizes)(side_b)
     recv_a = x_swap(0, sizes)(send_a)
-    side_a = y_swap(0, sizes)(sides)
-    side_b = y_swap(1, sizes)(sides)
 
     cells = pl.pallas_call(
         functools.partial(scatter_kernel, dims),
@@ -416,48 +492,72 @@
         out_specs=vmem(),
         out_shape=shape(64, cy),
         compiler_params=limits,
-    )(*(a.reshape(1, count) for a in (obs_cell, obs_var, obs_value, obs_weight)))
-
-    gy = lax.axis_index("gy")
-    lane = lax.broadcasted_iota(jnp.int32, (1, LANES), 1)
-    from_a = (gy % 2 == 1) == (lane < 64)
-    there = jnp.where(lane < 64, gy > 0, gy < ny - 1)
-    halo = jnp.where(there, jnp.where(from_a, side_a, side_b), 0.0)
+    )(*obs)
+
+    side_a, side_b, cells = lax.optimization_barrier((side_a, side_b, cells))
+    halo = side_a + side_b
     corner_b = x_swap(1, sizes)(halo)
     corner_a = x_swap(0, sizes)(halo)
 
-    _, anomalies, means, gram = pl.pallas_call(
-        functools.partial(forecast_kernel, dims, factor),
-        name="forecast",
-        in_specs=[smem()] + [vmem()] * 9,
+    inner_rows = cx - 4
+    first, inner_anomalies, inner_means, partial = pl.pallas_call(
+        functools.partial(inner_kernel, dims, factor),
+        name="inner",
+        in_specs=[smem()] + [vmem()] * 5,
         out_specs=[vmem()] * 4,
         out_shape=[
+            shape((cx + 2) * block, cy),
+            shape(2 * k, inner_rows * nv * cy, dtype=BF16),
+            shape(inner_rows * 8, cy),
+            shape(2 * k + 32, 2 * k),
+        ],
+        scratch_shapes=[
+            pltpu.VMEM(((cx + 2) * 8, cy), F32),
+            pltpu.VMEM((cx * 8, cy), F32),
+            pltpu.VMEM((k, LANES), F32),
+            pltpu.VMEM((2 * k + 32, inner_rows * nv * cy), BF16),
+            pltpu.VMEM((block, cy), F32),
+        ],
+        compiler_params=limits,
+    )(mixing, state, sides, halo, kappa, cells)
+
+    _, _, edge_anomalies, edge_means, gram = pl.pallas_call(
+        functools.partial(edge_kernel, dims, factor),
+        name="edge",
+        in_specs=[smem()] + [vmem()] * 11,
+        out_specs=[vmem()] * 5,
+        out_shape=[
             shape((cx + 4) * block, cy),
-            shape(2 * k, rows * cy, dtype=BF16),
-            shape(cx * 8, cy),
+            shape((cx + 2) * block, cy),
+            shape(2 * k, 4 * nv * cy, dtype=BF16),
+            shape(4 * 8, cy),
             shape(k // 2 + 8, 2 * k),
         ],
         scratch_shapes=[
-            pltpu.VMEM(((cx + 2) * block, cy), F32),
             pltpu.VMEM(((cx + 2) * 8, cy), F32),
             pltpu.VMEM((cx * 8, cy), F32),
-            pltpu.VMEM((2 * k + 32, rows * cy), BF16),
+            pltpu.VMEM((k, LANES), F32),
+            pltpu.VMEM((k, LANES), F32),
+            pltpu.VMEM((2 * k + 32, 4 * nv * cy), BF16),
+            pltpu.VMEM((block, cy), F32),
         ],
-        input_output_aliases={1: 0},
+        input_output_aliases={1: 0, 2: 1},
         compiler_params=limits,
-    )(mixing, state, recv_a, recv_b, sides, halo, corner_a, corner_b, diffusivity, cells)
+    )(
+        mixing, state, first, partial, recv_a, recv_b, sides, halo, corner_a, corner_b, kappa, cells
+    )
 
     gram = all_sum(gram, sizes)
 
     out = pl.pallas_call(
         functools.partial(apply_kernel, dims),
         name="apply",
-        in_specs=[vmem()] * 3,
-        out_specs=pl.BlockSpec(memory_space=pl.ANY),
+        in_specs=[vmem()] * 5,
+        out_specs=pl.BlockSpec(memory_space=pltpu.HBM),
         out_shape=shape(k * rows, cy),
         scratch_shapes=[pltpu.VMEM((cy // LANES, k * rows, LANES), F32), pltpu.SemaphoreType.DMA((cy // LANES,))],
         compiler_params=limits,
-    )(gram, anomalies, means)
+    )(gram, inner_anomalies, inner_means, edge_anomalies, edge_means)
     return out.reshape(k, nv, cx, cy)
 
 

time: 40.5 us -> 33.2 us (0.82)
  local copies, waits for them, and re-layouts: 4.73 us -> 0 us
  waiting for transfers between devices: 10.3 us -> 7.78 us
  Pallas kernels: 13.1 us -> 14.2 us
  starting transfers between devices: 11.9 us -> 10.9 us
    unnamed x20 -> x0, local copies, waits for them, and re-layouts: 4.73 us -> none
    ppermute x12, waiting for transfers between devices: 10.3 us -> 7.78 us  [pair_swap(): return lambda value: lax.ppermute(value, ('grp', 'gx', 'gy'), pairs)]
    ppermute x12, starting transfers between devices: 11.9 us -> 10.9 us  [pair_swap(): return lambda value: lax.ppermute(value, ('grp', 'gx', 'gy'), pairs)]
    pallas_call x1 -> x2, Pallas kernels: 6.8 us -> 7.54 us  [the longest x1 3.83 us: local(): pl.pallas_call(functools.partial(inner_kernel, dims, factor), name='inner...]
  transfers between devices with their start and end apart: 12 -> 12, of which waited for: 8 -> 6; matrix products, arithmetic and copies ran while one was open for 0% -> 0% of each run, Pallas kernels for 1% -> 13%
where the time goes in v2:
time: 33.2 us; the launch traced here: 33 us
  Pallas kernels  14.2 us (43%)
  starting transfers between devices  10.9 us (33%)
  waiting for transfers between devices  7.78 us (23%)
    ppermute x12, starting transfers between devices, pair_swap(): return lambda value: lax.ppermute(value, ('grp', 'gx', 'gy'), pairs)  10.9 us
    ppermute x12, waiting for transfers between devices, pair_swap(): return lambda value: lax.ppermute(value, ('grp', 'gx', 'gy'), pairs)  7.78 us
    pallas_call x1, Pallas kernels, local(): pl.pallas_call(functools.partial(apply_kernel, dims), name='apply', in_sp...  3.99 us
    pallas_call x1, Pallas kernels, local(): pl.pallas_call(functools.partial(inner_kernel, dims, factor), name='inner...  3.83 us
    pallas_call x1, Pallas kernels, local(): pl.pallas_call(functools.partial(edge_kernel, dims, factor), name='edge',...  3.71 us
    pallas_call x1, Pallas kernels, local(): pl.pallas_call(functools.partial(load_kernel, dims), name='load', in_spec...  2.2 us
  transfers between devices with their start and end apart: 12, of which 6 were waited for; matrix products, arithmetic and copies ran while one was open for 0% of the time, Pallas kernels for 13%

profile of v2, /device:TPU:0, one launch (start us, length us, event | category | flops | bytes accessed | tf_op | source)
XLA Modules:
  0.0 33.0 jit_solution(11888393018262633070)
XLA Ops:
  0.0 2.2 %load.1 = (f32[2304,256]{1,0:T(8,128)S(1)}, f32[392,256]{1,0:T(8,128)S(1)}, f32[392,256]{1,0:T(8,128)S(1)}, f32[72,128]{1,0:T(8,128)S(1)}, f32[72,128]{1,0:T(8,1...) custom-call(f32[1536,256]{1,0:T(8,128)} %bitcast.6, ...), custom_call_target="tpu_custom_call" | custom-call | tf_op jit(solution)/shard_map/load/pallas_call | solution.py:463
  2.2 0.5 %collective-permute-start.2 = (f32[392,256]{1,0:T(8,128)S(1)}, f32[392,256]{1,0:T(8,128)S(1)}, u32[]{:S(2)}, u32[]{:S(2)}) collective-permute-start(f32[392,256]{1,0:T(8,128)S(1)} %get-tuple-element.42), channel_id=1, source_target_pairs={{0,4},{1,5},{2,6},{3,7},{4,0},{5,1},{6,2},{7,3},{8,12},{9,13},{10,... | collective-permute-start | bytes 1204232 | tf_op jit(solution)/shard_map/ppermute | solution.py:52
  2.7 2.6 %collective-permute-start.3 = (f32[392,256]{1,0:T(8,128)S(1)}, f32[392,256]{1,0:T(8,128)S(1)}, u32[]{:S(2)}, u32[]{:S(2)}) collective-permute-start(f32[392,256]{1,0:T(8,128)S(1)} %get-tuple-element.43), channel_id=1, source_target_pairs={{0,16},{1,17},{2,18},{3,19},{4,8},{5,9},{6,10},{7,11},{8,4},{9,5},... | collective-permute-start | bytes 1204232 | tf_op jit(solution)/shard_map/ppermute | solution.py:52
  5.3 1.6 %collective-permute-start = (f32[72,128]{1,0:T(8,128)S(1)}, f32[72,128]{1,0:T(8,128)S(1)}, u32[]{:S(2)}, u32[]{:S(2)}) collective-permute-start(f32[72,128]{1,0:T(8,128)S(1)} %get-tuple-element.30), channel_id=1, source_target_pairs={{0,1},{1,0},{2,3},{3,2},{4,5},{5,4},{6,7},{7,6},{8,9},{9,8},{10,11... | collective-permute-start | bytes 110600 | tf_op jit(solution)/shard_map/ppermute | solution.py:52
  6.9 0.0 collective-permute-start.1
  6.9 0.5 %scatter.1.cells = f32[64,256]{1,0:T(8,128)S(1)} custom-call(s32[1,2048]{1,0:T(1,128)S(1)} %get-tuple-element.32.cell, s32[1,2048]{1,0:T(1,128)S(1)} %get-tuple-element.33.var, f32[1,2048]{1,0:T(1,128)S(1)} %get-tuple-element.34.value, f32[1,2048]{1,0:T(1,128)S(1)} %get-tuple-element.35.weight), custom_call_target="tpu_custom_call" | custom-call | tf_op jit(solution)/shard_map/scatter/pallas_call | solution.py:488
  7.4 1.9 %collective-permute-done = f32[72,128]{1,0:T(8,128)S(1)} collective-permute-done((f32[72,128]{1,0:T(8,128)S(1)}, f32[72,128]{1,0:T(8,128)S(1)}, u32[]{:S(2)}, u32[]{:S(2)}) %collective-permute-start) | collective-permute-done | bytes 36896 | tf_op jit(solution)/shard_map/ppermute | solution.py:52
  9.3 0.0 collective-permute-done.1
  9.3 0.1 collective-permute-start.5
  9.4 0.1 collective-permute-start.4
  9.6 3.8 %inner.1 = (f32[1920,256]{1,0:T(8,128)S(1)}, bf16[128,3072]{1,0:T(8,128)(2,1)S(1)}, f32[32,256]{1,0:T(8,128)S(1)}, f32[160,128]{1,0:T(8,128)S(1)}) custom-call(f32[3,3]{1,0:T(4,128)S(1)} %get-tuple-element.27.mixing, f32[2304,256]{1,0:T(8,128)S(1)} %get-tuple-element.28.state.state_in, f32[72,128]{1,0:T(8,128)S(1)} %get-tuple-element.29.sides, ...), custom_call_target="tpu_custom_call" | custom-call | tf_op jit(solution)/shard_map/inner/pallas_call | solution.py:503
  13.4 0.0 collective-permute-done.5.corner_b
  13.4 0.0 collective-permute-done.4.corner_a
  13.4 0.0 collective-permute-done.2.recv_a
  13.4 0.0 collective-permute-done.3.recv_b
  13.5 3.7 %edge.1 = (f32[2304,256]{1,0:T(8,128)S(1)}, f32[1920,256]{1,0:T(8,128)S(1)}, bf16[128,3072]{1,0:T(8,128)(2,1)S(1)}, f32[32,256]{1,0:T(8,128)S(1)}, f32[40,128]{1,0:T(8,128)S(1)}) custom-call(f32[3,3]{1,0:T(4,128)S(1)} %get-tuple-element.27.mixing, f32[2304,256]{1,0:T(8,128)S(1)} %get-tuple-element.28.state.state_in, ...), custom_call_target="tpu_custom_call", output_to_operand_aliasing={{0}: (1, {}), {1}: (2, {})} | custom-call | tf_op jit(solution)/shard_map/edge/pallas_call | solution.py:524
  17.2 0.4 %collective-permute-start.6 = (f32[40,128]{1,0:T(8,128)S(1)}, f32[40,128]{1,0:T(8,128)S(1)}, u32[]{:S(2)}, u32[]{:S(2)}) collective-permute-start(f32[40,128]{1,0:T(8,128)S(1)} %get-tuple-element.44), channel_id=1, source_target_pairs={{0,4},{1,5},{2,6},{3,7},{4,0},{5,1},{6,2},{7,3},{8,12},{9,13},{10,... | collective-permute-start | bytes 61448 | tf_op jit(solution)/shard_map/ppermute | solution.py:52
  17.6 0.8 %collective-permute-done.6 = f32[40,128]{1,0:T(8,128)S(1)} collective-permute-done((f32[40,128]{1,0:T(8,128)S(1)}, f32[40,128]{1,0:T(8,128)S(1)}, u32[]{:S(2)}, u32[]{:S(2)}) %collective-permute-start.6) | collective-permute-done | bytes 20512 | tf_op jit(solution)/shard_map/ppermute | solution.py:52
  18.4 4.3 %collective-permute-start.10 = (f32[40,128]{1,0:T(8,128)S(1)}, f32[40,128]{1,0:T(8,128)S(1)}, u32[]{:S(2)}, u32[]{:S(2)}) collective-permute-start(f32[40,128]{1,0:T(8,128)S(1)} %add.22), channel_id=1, source_target_pairs={{0,3},{1,2},{2,1},{3,0},{4,15},{5,14},{6,13},{7,12},{8,11},{9,10},... | collective-permute-start | bytes 61448 | tf_op jit(solution)/shard_map/ppermute | solution.py:52
  22.7 0.5 %collective-permute-start.9 = (f32[40,128]{1,0:T(8,128)S(1)}, f32[40,128]{1,0:T(8,128)S(1)}, u32[]{:S(2)}, u32[]{:S(2)}) collective-permute-start(f32[40,128]{1,0:T(8,128)S(1)} %add.22), channel_id=1, source_target_pairs={{0,2},{1,3},{2,0},{3,1},{4,14},{5,15},{6,12},{7,13},{8,10},{9,11},... | collective-permute-start | bytes 61448 | tf_op jit(solution)/shard_map/ppermute | solution.py:52
  23.2 0.5 %collective-permute-start.8 = (f32[40,128]{1,0:T(8,128)S(1)}, f32[40,128]{1,0:T(8,128)S(1)}, u32[]{:S(2)}, u32[]{:S(2)}) collective-permute-start(f32[40,128]{1,0:T(8,128)S(1)} %add.22), channel_id=1, source_target_pairs={{0,1},{1,0},{2,3},{3,2},{4,13},{5,12},{6,15},{7,14},{8,9},{9,8},{1... | collective-permute-start | bytes 61448 | tf_op jit(solution)/shard_map/ppermute | solution.py:52
  23.7 0.1 collective-permute-start.7
  23.9 0.6 %collective-permute-done.10 = f32[40,128]{1,0:T(8,128)S(1)} collective-permute-done((f32[40,128]{1,0:T(8,128)S(1)}, f32[40,128]{1,0:T(8,128)S(1)}, u32[]{:S(2)}, u32[]{:S(2)}) %collective-permute-start.10) | collective-permute-done | bytes 20512 | tf_op jit(solution)/shard_map/ppermute | solution.py:52
  24.5 3.2 %collective-permute-done.9 = f32[40,128]{1,0:T(8,128)S(1)} collective-permute-done((f32[40,128]{1,0:T(8,128)S(1)}, f32[40,128]{1,0:T(8,128)S(1)}, u32[]{:S(2)}, u32[]{:S(2)}) %collective-permute-start.9) | collective-permute-done | bytes 20512 | tf_op jit(solution)/shard_map/ppermute | solution.py:52
  27.7 0.0 collective-permute-done.8
  27.7 0.1 collective-permute-done.7
  27.8 0.1 collective-permute-start.11
  27.8 1.2 %collective-permute-done.11 = f32[40,128]{1,0:T(8,128)S(1)} collective-permute-done((f32[40,128]{1,0:T(8,128)S(1)}, f32[40,128]{1,0:T(8,128)S(1)}, u32[]{:S(2)}, u32[]{:S(2)}) %collective-permute-start.11) | collective-permute-done | bytes 20512 | tf_op jit(solution)/shard_map/ppermute | solution.py:52
  29.0 4.0 %apply.1 = f32[1536,256]{1,0:T(8,128)} custom-call(f32[40,128]{1,0:T(8,128)S(1)} %add.27.gram, bf16[128,3072]{1,0:T(8,128)(2,1)S(1)} %get-tuple-element.45.inner, f32[32,256]{1,0:T(8,128)S(1)} %get-tuple-element.46.inner_means, bf16[128,3072]{1,0:T(8,128)(2,1)S(1)} %get-tuple-element.47.edge, f32[32,256]{1,0:T(8,128)S(1)} %get-tuple-element.48.edge_means), custom_call_target="tpu_custom_call" | custom-call | tf_op jit(solution)/shard_map/apply/pallas_call | solution.py:552
  (4 shorter events, 0.0 us)
Async XLA Ops:
  2.2 11.2 %collective-permute-start.2 = (f32[392,256]{1,0:T(8,128)S(1)}, f32[392,256]{1,0:T(8,128)S(1)}, u32[]{:S(2)}, u32[]{:S(2)}) collective-permute-start(f32[392,256]{1,0:T(8,128)S(1)} %get-tuple-element.42), channel_id=1, source_target_pairs={{0,4},{1,5},{2,6},{3,7},{4,0},{5,1},{6,2},{7,3},{8,12},{9,13},{10,... | collective-permute-start | bytes 1204232 | tf_op jit(solution)/shard_map/ppermute | solution.py:52
  2.7 10.7 %collective-permute-start.3 = (f32[392,256]{1,0:T(8,128)S(1)}, f32[392,256]{1,0:T(8,128)S(1)}, u32[]{:S(2)}, u32[]{:S(2)}) collective-permute-start(f32[392,256]{1,0:T(8,128)S(1)} %get-tuple-element.43), channel_id=1, source_target_pairs={{0,16},{1,17},{2,18},{3,19},{4,8},{5,9},{6,10},{7,11},{8,4},{9,5},... | collective-permute-start | bytes 1204232 | tf_op jit(solution)/shard_map/ppermute | solution.py:52
  5.3 4.0 %collective-permute-start = (f32[72,128]{1,0:T(8,128)S(1)}, f32[72,128]{1,0:T(8,128)S(1)}, u32[]{:S(2)}, u32[]{:S(2)}) collective-permute-start(f32[72,128]{1,0:T(8,128)S(1)} %get-tuple-element.30), channel_id=1, source_target_pairs={{0,1},{1,0},{2,3},{3,2},{4,5},{5,4},{6,7},{7,6},{8,9},{9,8},{10,11... | collective-permute-start | bytes 110600 | tf_op jit(solution)/shard_map/ppermute | solution.py:52
  6.9 2.4 %collective-permute-start.1 = (f32[72,128]{1,0:T(8,128)S(1)}, f32[72,128]{1,0:T(8,128)S(1)}, u32[]{:S(2)}, u32[]{:S(2)}) collective-permute-start(f32[72,128]{1,0:T(8,128)S(1)} %get-tuple-element.31), channel_id=1, source_target_pairs={{0,4},{1,2},{2,1},{3,7},{4,0},{5,6},{6,5},{7,3},{8,12},{9,10},{10,... | collective-permute-start | bytes 110600 | tf_op jit(solution)/shard_map/ppermute | solution.py:52
  9.3 4.1 %collective-permute-start.5 = (f32[72,128]{1,0:T(8,128)S(1)}, f32[72,128]{1,0:T(8,128)S(1)}, u32[]{:S(2)}, u32[]{:S(2)}) collective-permute-start(f32[72,128]{1,0:T(8,128)S(1)} %add.21.halo), channel_id=1, source_target_pairs={{0,16},{1,17},{2,18},{3,19},{4,8},{5,9},{6,10},{7,11},{8,4},{9,5},... | collective-permute-start | bytes 110600 | tf_op jit(solution)/shard_map/ppermute | solution.py:52
  9.4 4.0 %collective-permute-start.4 = (f32[72,128]{1,0:T(8,128)S(1)}, f32[72,128]{1,0:T(8,128)S(1)}, u32[]{:S(2)}, u32[]{:S(2)}) collective-permute-start(f32[72,128]{1,0:T(8,128)S(1)} %add.21.halo), channel_id=1, source_target_pairs={{0,4},{1,5},{2,6},{3,7},{4,0},{5,1},{6,2},{7,3},{8,12},{9,13},{10,... | collective-permute-start | bytes 110600 | tf_op jit(solution)/shard_map/ppermute | solution.py:52
  17.2 1.2 %collective-permute-start.6 = (f32[40,128]{1,0:T(8,128)S(1)}, f32[40,128]{1,0:T(8,128)S(1)}, u32[]{:S(2)}, u32[]{:S(2)}) collective-permute-start(f32[40,128]{1,0:T(8,128)S(1)} %get-tuple-element.44), channel_id=1, source_target_pairs={{0,4},{1,5},{2,6},{3,7},{4,0},{5,1},{6,2},{7,3},{8,12},{9,13},{10,... | collective-permute-start | bytes 61448 | tf_op jit(solution)/shard_map/ppermute | solution.py:52
  18.4 6.1 %collective-permute-start.10 = (f32[40,128]{1,0:T(8,128)S(1)}, f32[40,128]{1,0:T(8,128)S(1)}, u32[]{:S(2)}, u32[]{:S(2)}) collective-permute-start(f32[40,128]{1,0:T(8,128)S(1)} %add.22), channel_id=1, source_target_pairs={{0,3},{1,2},{2,1},{3,0},{4,15},{5,14},{6,13},{7,12},{8,11},{9,10},... | collective-permute-start | bytes 61448 | tf_op jit(solution)/shard_map/ppermute | solution.py:52
  22.7 5.0 %collective-permute-start.9 = (f32[40,128]{1,0:T(8,128)S(1)}, f32[40,128]{1,0:T(8,128)S(1)}, u32[]{:S(2)}, u32[]{:S(2)}) collective-permute-start(f32[40,128]{1,0:T(8,128)S(1)} %add.22), channel_id=1, source_target_pairs={{0,2},{1,3},{2,0},{3,1},{4,14},{5,15},{6,12},{7,13},{8,10},{9,11},... | collective-permute-start | bytes 61448 | tf_op jit(solution)/shard_map/ppermute | solution.py:52
  23.2 4.4 %collective-permute-start.8 = (f32[40,128]{1,0:T(8,128)S(1)}, f32[40,128]{1,0:T(8,128)S(1)}, u32[]{:S(2)}, u32[]{:S(2)}) collective-permute-start(f32[40,128]{1,0:T(8,128)S(1)} %add.22), channel_id=1, source_target_pairs={{0,1},{1,0},{2,3},{3,2},{4,13},{5,12},{6,15},{7,14},{8,9},{9,8},{1... | collective-permute-start | bytes 61448 | tf_op jit(solution)/shard_map/ppermute | solution.py:52
  23.7 4.0 %collective-permute-start.7 = (f32[40,128]{1,0:T(8,128)S(1)}, f32[40,128]{1,0:T(8,128)S(1)}, u32[]{:S(2)}, u32[]{:S(2)}) collective-permute-start(f32[40,128]{1,0:T(8,128)S(1)} %add.22), channel_id=1, source_target_pairs={{0,8},{1,9},{2,10},{3,11},{4,12},{5,13},{6,14},{7,15},{8,0},{9,1},... | collective-permute-start | bytes 61448 | tf_op jit(solution)/shard_map/ppermute | solution.py:52
  27.8 1.3 %collective-permute-start.11 = (f32[40,128]{1,0:T(8,128)S(1)}, f32[40,128]{1,0:T(8,128)S(1)}, u32[]{:S(2)}, u32[]{:S(2)}) collective-permute-start(f32[40,128]{1,0:T(8,128)S(1)} %add_add_fusion), channel_id=1, source_target_pairs={{0,4},{1,5},{2,6},{3,7},{4,0},{5,1},{6,2},{7,3},{8,12},{9,13},{10,... | collective-permute-start | bytes 61448 | tf_op jit(solution)/shard_map/ppermute | solution.py:52

commit v3 on v2

--- a/solution.py
+++ b/solution.py
@@ -10,7 +10,6 @@
 
 NS_ITERS = 5
 LANES = 128
-HIGHEST = lax.Precision.HIGHEST
 F32 = jnp.float32
 BF16 = jnp.bfloat16
 
@@ -124,63 +123,72 @@
     small_copies = [pltpu.make_async_copy(a, b, small_sems.at[i]) for i, (a, b) in enumerate(zip(small_in, small))]
     for copy in small_copies:
         copy.start()
+    lane = lax.broadcasted_iota(jnp.int32, (1, LANES), 1)
+
+    def add(acc, place, right, left):
+        low = (lane >= place) & (lane < place + 2)
+        high = (lane >= 64 + place) & (lane < 64 + place + 2)
+        acc = jnp.where(low, pltpu.roll(right, (place + 2) % LANES, 1), acc)
+        return jnp.where(high, pltpu.roll(left, 64 + place, 1), acc)
+
+    gy = lax.axis_index("gy")
+    even_y = gy % 2 == 0
+    has_left = gy > 0
+    has_right = gy < lax.axis_size("gy") - 1
+    wanted = []
+    for to_right in (even_y, jnp.logical_not(even_y)):
+        start = jnp.where(jnp.where(to_right, has_right, has_left), jnp.where(to_right, 0, 64), LANES)
+        wanted.append((lane >= start) & (lane < start + 64))
+
+    def put_sides(at, total):
+        sides[at, :] = total
+        side_a[at, :] = jnp.where(wanted[0], total, 0.0)
+        side_b[at, :] = jnp.where(wanted[1], total, 0.0)
+
     for c in range(chunks):
         for h in range(half):
             copies[c * half + h].wait()
-            for r in range(cx):
-                for v in range(nv):
-                    value = buf[h, pl.ds(c * part * rows + v * cx + r, part, stride=rows), :]
-                    at = pl.ds(((r + 2) * nv + v) * k + c * part, part)
-                    state[at, h * LANES : (h + 1) * LANES] = value
+        total = jnp.zeros((part, LANES), F32)
+        for r in range(cx):
+            for v in range(nv):
+                at = pl.ds(((r + 2) * nv + v) * k + c * part, part)
+                values = [buf[h, pl.ds(c * part * rows + v * cx + r, part, stride=rows), :] for h in range(half)]
+                for h in range(half):
+                    state[at, h * LANES : (h + 1) * LANES] = values[h]
+                total = add(total, 2 * (nv * (r + 1) + v), values[-1], values[0])
+        put_sides(pl.ds(c * part, part), total)
     for copy in small_copies:
         copy.wait()
     block = nv * k
     even_x = lax.axis_index("gx") % 2 == 0
     top = 2 * block
     bottom = (cx + 1) * block
+    gx = lax.axis_index("gx")
+    has_up = gx > 0
+    has_down = gx < lax.axis_size("gx") - 1
     for ref, near_top in ((send_a, jnp.logical_not(even_x)), (send_b, even_x)):
+        has = jnp.where(near_top, has_up, has_down)
         near = jnp.where(near_top, top, bottom)
         second = jnp.where(near_top, top + block, bottom - block)
         for j in range(0, block, 64):
-            ref[pl.ds(j, 64), :] = state[pl.ds(pl.multiple_of(near + j, 64), 64), :]
-            ref[pl.ds(block + j, 64), :] = state[pl.ds(pl.multiple_of(second + j, 64), 64), :]
+            ref[pl.ds(j, 64), :] = jnp.where(has, state[pl.ds(pl.multiple_of(near + j, 64), 64), :], 0.0)
+            ref[pl.ds(block + j, 64), :] = jnp.where(has, state[pl.ds(pl.multiple_of(second + j, 64), 64), :], 0.0)
         for v in range(nv):
             edge = jnp.where(near_top, kappa[v, 0:1, :], kappa[v, cx - 1 : cx, :])
-            ref[pl.ds(2 * block + v, 1), :] = edge
+            ref[pl.ds(2 * block + v, 1), :] = jnp.where(has, edge, 0.0)
         ref[pl.ds(2 * block + nv, 8 - nv), :] = jnp.zeros((8 - nv, cy), F32)
 
-    lane = lax.broadcasted_iota(jnp.int32, (1, LANES), 1)
-    total = jnp.zeros((k, LANES), F32)
-    total_k = jnp.zeros((8, LANES), F32)
+    total = jnp.zeros((8, LANES), F32)
     for r in range(cx):
         for v in range(nv):
-            place = 2 * (nv * (r + 1) + v)
-            base = ((r + 2) * nv + v) * k
-            low = (lane >= place) & (lane < place + 2)
-            high = (lane >= 64 + place) & (lane < 64 + place + 2)
-
-            def add(acc, right, left):
-                acc = jnp.where(low, pltpu.roll(right, (place + 2) % LANES, 1), acc)
-                return jnp.where(high, pltpu.roll(left, 64 + place, 1), acc)
-
-            total = add(total, state[pl.ds(base, k), cy - LANES :], state[pl.ds(base, k), :LANES])
             row = kappa[v, r : r + 1, :]
-            total_k = add(
-                total_k,
+            total = add(
+                total,
+                2 * (nv * (r + 1) + v),
                 jnp.broadcast_to(row[:, cy - LANES :], (8, LANES)),
                 jnp.broadcast_to(row[:, :LANES], (8, LANES)),
             )
-    sides[0:k, :] = total
-    sides[k : k + 8, :] = total_k
-    gy = lax.axis_index("gy")
-    even_y = gy % 2 == 0
-    has_left = gy > 0
-    has_right = gy < lax.axis_size("gy") - 1
-    for ref, to_right in ((side_a, even_y), (side_b, jnp.logical_not(even_y))):
-        start = jnp.where(jnp.where(to_right, has_right, has_left), jnp.where(to_right, 0, 64), LANES)
-        wanted = (lane >= start) & (lane < start + 64)
-        ref[0:k, :] = jnp.where(wanted, total, 0.0)
-        ref[k : k + 8, :] = jnp.where(wanted, total_k, 0.0)
+    put_sides(pl.ds(k, 8), total)
 
 
 def scatter_kernel(dims, cell, var, value, weight, out):
@@ -231,22 +239,18 @@
     first_lane = lane == 0
     last_lane = lane == LANES - 1
     for v in range(nv):
-        at = 2 * (nv * e + v)
-        to_left = (LANES - 1 - at) & (LANES - 1)
-        to_right = (2 * LANES - 1 - 64 - at) & (LANES - 1)
+        shift = (LANES - 1 - 2 * (nv * e + v)) & (LANES - 1)
         kap = [jnp.broadcast_to(kappas[h][v : v + 1], (8, LANES)) for h in range(half)]
         own = [1.0 - 4.0 * kap[h] + mixing[v, v] for h in range(half)]
         others = [(w, mixing[v, w]) for w in range(nv) if w != v]
         for j in range(0, k, 8):
-            edge = side[pl.ds(j, 8), :]
-            left_edge = pltpu.roll(edge, to_left, 1)
-            right_edge = pltpu.roll(edge, to_right, 1)
+            edge = 0.0 if side is None else pltpu.roll(side[pl.ds(j, 8), :], shift, 1)
             center = [load(0, v, j, h) for h in range(half)]
             ahead = [pltpu.roll(c, 1, 1) for c in center]
             behind = [pltpu.roll(c, LANES - 1, 1) for c in center]
             for h in range(half):
-                left = jnp.where(first_lane, left_edge if h == 0 else ahead[h - 1], ahead[h])
-                right = jnp.where(last_lane, right_edge if h == half - 1 else behind[h + 1], behind[h])
+                left = jnp.where(first_lane, edge if h == 0 else ahead[h - 1], ahead[h])
+                right = jnp.where(last_lane, edge if h == half - 1 else behind[h + 1], behind[h])
                 around = (load(-1, v, j, h) + load(1, v, j, h)) + (left + right)
                 out = own[h] * center[h] + kap[h] * around
                 for w, factor in others:
@@ -254,42 +258,74 @@
                 store(v, j, h, out)
 
 
-def rows_forecast(
-    dims, factor, mixing, kext, spread, state, first, side, first_side, rows_1, rows_2, outs, lane
-):
+def edges_of(columns, lane):
+    return jnp.where(lane % 2 == 0, pltpu.roll(columns, 64, 1), columns)
+
+
+def loader(ref, base, k, row_size):
+    def load(row, w, j, h):
+        at = pl.multiple_of(base + row * row_size + w * k + j, 8)
+        return ref[pl.ds(at, 8), h * LANES : (h + 1) * LANES]
+
+    return load
+
+
+def first_step(dims, mixing, kext, state, first, side, count, row_of, lane):
+    k, nv, cx, cy = dims
+    block = nv * k
+
+    def step(i, carry):
+        e = row_of(i)
+
+        def store(v, j, h, out):
+            first[pl.ds(pl.multiple_of(e * block + v * k + j, 8), 8), h * LANES : (h + 1) * LANES] = out
+
+        advance(dims, mixing, kext, loader(state, (e + 1) * block, k, block), side, e, lane, store)
+        return carry
+
+    lax.fori_loop(0, count, step, 0)
+
+
+def add_sides(dims, kext, first, side, count, row_of, lane):
+    k, nv, cx, cy = dims
+    block = nv * k
+    ends = ((0, lane == 0), (cy - LANES, lane == LANES - 1))
+
+    def step(i, carry):
+        e = row_of(i)
+        eight = pl.ds(pl.multiple_of(e * 8, 8), 8)
+        for v in range(nv):
+            shift = (LANES - 1 - 2 * (nv * e + v)) & (LANES - 1)
+            kap = []
+            for at, here in ends:
+                row = jnp.where(here, kext[eight, at : at + LANES][v : v + 1], 0.0)
+                kap.append(jnp.broadcast_to(row, (8, LANES)))
+            for j in range(0, k, 8):
+                edge = pltpu.roll(side[pl.ds(j, 8), :], shift, 1)
+                rows = pl.ds(pl.multiple_of(e * block + v * k + j, 8), 8)
+                for (at, here), factor in zip(ends, kap):
+                    first[rows, at : at + LANES] += factor * edge
+        return carry
+
+    lax.fori_loop(0, count, step, 0)
+
+
+def second_step(dims, factor, mixing, kext, spread, first, first_side, count, row_of, outs, lane):
     k, nv, cx, cy = dims
     block = nv * k
     half = cy // LANES
     anomalies, means, moved, kept = outs
-
-    def loader(ref, base):
-        def load(row, w, j, h):
-            at = pl.multiple_of(base + row * block + w * k + j, 8)
-            return ref[pl.ds(at, 8), h * LANES : (h + 1) * LANES]
-
-        return load
-
-    def step_1(i, carry):
-        e = rows_1[1](i)
-
-        def store(v, j, h, out):
-            first[pl.ds(pl.multiple_of(e * block + v * k + j, 8), 8), h * LANES : (h + 1) * LANES] = out
-
-        advance(dims, mixing, kext, loader(state, (e + 1) * block), side, e, lane, store)
-        return carry
-
-    lax.fori_loop(0, rows_1[0], step_1, 0)
     sub = lax.broadcasted_iota(jnp.int32, (8, 1), 0)
 
     def step_2(i, carry):
-        e = rows_2[1](i)
+        e = row_of(i)
         eight = pl.ds(pl.multiple_of((e - 1) * 8, 8), 8)
         spreads = [spread[eight, h * LANES : (h + 1) * LANES] for h in range(half)]
 
         def store(v, j, h, out):
             kept[pl.ds(v * k + j, 8), h * LANES : (h + 1) * LANES] = out
 
-        advance(dims, mixing, kext, loader(first, e * block), first_side, e, lane, store)
+        advance(dims, mixing, kext, loader(first, e * block, k, block), first_side, e, lane, store)
         for h in range(half):
             found = jnp.zeros((8, LANES), F32)
             for v in range(nv):
@@ -316,79 +352,83 @@
             means[pl.ds(pl.multiple_of(i * 8, 8), 8), h * LANES : (h + 1) * LANES] = found
         return carry
 
-    lax.fori_loop(0, rows_2[0], step_2, 0)
+    lax.fori_loop(0, count, step_2, 0)
     return nt(moved[...], anomalies[...])
 
 
-def set_rows(dims, kappa, cells, kext, spread):
+def set_kappa(dims, kappa, kext):
     k, nv, cx, cy = dims
     for v in range(nv):
         for r in range(cx):
             kext[pl.ds((r + 1) * 8 + v, 1), :] = kappa[v, r : r + 1, :]
+
+
+def middle_kernel(dims, mixing, state, kappa, cell, var, value, weight, first, kext, spread, cells):
+    k, nv, cx, cy = dims
+    scatter_kernel(dims, cell, var, value, weight, cells)
+    for v in range(nv):
+        for r in range(cx):
             spread[pl.ds(r * 8 + v, 1), :] = cells[pl.ds(r * nv + v, 1), :]
             spread[pl.ds(r * 8 + nv + v, 1), :] = cells[pl.ds(32 + r * nv + v, 1), :]
+    set_kappa(dims, kappa, kext)
+    lane = lax.broadcasted_iota(jnp.int32, (1, LANES), 1)
+    first_step(dims, mixing, kext, state, first, None, cx - 2, lambda i: i + 2, lane)
 
 
 def inner_kernel(
-    dims, factor, mixing, state, sides, halo, kappa, cells,
-    first, anomalies, means, partial, kext, spread, first_side, moved, kept,
+    dims, factor, mixing, first_in, sides, halo, kext, spread,
+    first, anomalies, means, partial, side, first_side, moved, kept,
 ):
     k, nv, cx, cy = dims
-    set_rows(dims, kappa, cells, kext, spread)
     lane = lax.broadcasted_iota(jnp.int32, (1, LANES), 1)
-    first_side[...] = first_columns_of(
-        dims, mixing, halo[0:k, :], halo[k : k + 1, :], sides[0:k, :], lane
+    columns = first_columns_of(dims, mixing, halo[0:k, :], halo[k : k + 1, :], sides[0:k, :], lane)
+    side[...] = edges_of(halo[0:k, :], lane)
+    first_side[...] = edges_of(columns, lane)
+    add_sides(dims, kext, first, side, cx - 2, lambda i: i + 2, lane)
+    outs = (anomalies, means, moved, kept)
+    partial[...] = second_step(
+        dims, factor, mixing, kext, spread, first, first_side, cx - 4, lambda i: i + 3, outs, lane
     )
-    partial[...] = rows_forecast(
-        dims, factor, mixing, kext, spread, state, first, halo, first_side,
-        (cx - 2, lambda i: i + 2), (cx - 4, lambda i: i + 3),
-        (anomalies, means, moved, kept), lane,
-    )
 
 
 def edge_kernel(
-    dims, factor, mixing, state_in, first_in, partial, recv_a, recv_b, sides, halo, corner_a, corner_b, kappa, cells,
-    state, first, anomalies, means, gram, kext, spread, side, first_side, moved, kept,
+    dims, factor, mixing, state_in, first_in, partial, recv_a, recv_b, sides, halo, corner_a, corner_b, kext_in, spread,
+    state, first, anomalies, means, gram, kext, side, first_side, moved, kept,
 ):
     k, nv, cx, cy = dims
     block = nv * k
     gx = lax.axis_index("gx")
     nx = lax.axis_size("gx")
-    even_x = gx % 2 == 0
-    has_up = gx > 0
-    has_down = gx < nx - 1
-    up_is_a = jnp.logical_not(even_x)
-
-    def pick(ref_is_a, has, a, b):
-        return jnp.where(has, jnp.where(ref_is_a, a, b), 0.0)
+    down_is_a = gx % 2 == 0
+
+    def both(a, b):
+        return jnp.where(down_is_a, b, a), jnp.where(down_is_a, a, b)
 
     for j in range(0, 2 * block, 32):
-        a = recv_a[pl.ds(j, 32), :]
-        b = recv_b[pl.ds(j, 32), :]
-        up_at = (block if j < block else -block) + j
-        state[pl.ds(up_at, 32), :] = pick(up_is_a, has_up, a, b)
-        state[pl.ds((cx + 2) * block + j, 32), :] = pick(even_x, has_down, a, b)
-    set_rows(dims, kappa, cells, kext, spread)
-    for v in range(nv):
-        a = recv_a[pl.ds(2 * block + v, 1), :]
-        b = recv_b[pl.ds(2 * block + v, 1), :]
-        kext[pl.ds(v, 1), :] = pick(up_is_a, has_up, a, b)
-        kext[pl.ds((cx + 1) * 8 + v, 1), :] = pick(even_x, has_down, a, b)
+        up, down = both(recv_a[pl.ds(j, 32), :], recv_b[pl.ds(j, 32), :])
+        state[pl.ds((block if j < block else -block) + j, 32), :] = up
+        state[pl.ds((cx + 2) * block + j, 32), :] = down
+    up, down = both(recv_a[2 * block : 2 * block + 8, :], recv_b[2 * block : 2 * block + 8, :])
+    kext[8 : 8 * (cx + 1), :] = kext_in[8 : 8 * (cx + 1), :]
+    kext[0:8, :] = up
+    kext[8 * (cx + 1) : 8 * (cx + 2), :] = down
 
     lane = lax.broadcasted_iota(jnp.int32, (1, LANES), 1)
     slot = lane % 64
-    up_corner = pick(up_is_a, has_up, corner_a[...], corner_b[...])
-    down_corner = pick(even_x, has_down, corner_a[...], corner_b[...])
+    up, down = both(corner_a[...], corner_b[...])
+    up = jnp.where(gx > 0, up, 0.0)
+    down = jnp.where(gx < nx - 1, down, 0.0)
     far = 2 * nv * cx
-    columns = jnp.where(slot < 2 * nv, pltpu.roll(up_corner, LANES - far, 1), halo[...])
-    columns = jnp.where(
-        (slot >= 2 * nv * (cx + 1)) & (slot < 2 * nv * (cx + 2)), pltpu.roll(down_corner, far, 1), columns
+    columns = jnp.where(slot < 2 * nv, pltpu.roll(up, LANES - far, 1), halo[...])
+    columns = jnp.where((slot >= 2 * nv * (cx + 1)) & (slot < 2 * nv * (cx + 2)), pltpu.roll(down, far, 1), columns)
+    side[...] = edges_of(columns[0:k, :], lane)
+    columns = first_columns_of(dims, mixing, columns[0:k, :], columns[k : k + 1, :], sides[0:k, :], lane)
+    first_side[...] = edges_of(columns, lane)
+    first_step(
+        dims, mixing, kext, state, first, side, 4, lambda i: jnp.where(i < 2, i, i + cx - 2), lane
     )
-    side[...] = columns[0:k, :]
-    first_side[...] = first_columns_of(dims, mixing, columns[0:k, :], columns[k : k + 1, :], sides[0:k, :], lane)
-    got = partial[...] + rows_forecast(
-        dims, factor, mixing, kext, spread, state, first, side, first_side,
-        (4, lambda i: jnp.where(i < 2, i, i + cx - 2)), (4, lambda i: jnp.where(i < 2, i + 1, i + cx - 3)),
+    got = partial[...] + second_step(
+        dims, factor, mixing, kext, spread, first, first_side, 4, lambda i: jnp.where(i < 2, i + 1, i + cx - 3),
         (anomalies, means, moved, kept), lane,
     )
     whole = got[:, 0:k] + got[:, k : 2 * k]
@@ -400,7 +440,7 @@
 
 def apply_kernel(dims, gram, inner, inner_means, edge, edge_means, out, buf, sems):
     k, nv, cx, cy = dims
-    rows = nv * cx
+    half = cy // LANES
     row = lax.broadcasted_iota(jnp.int32, (k, k), 0)
     col = lax.broadcasted_iota(jnp.int32, (k, k), 1)
     eye = (row == col).astype(F32)
@@ -410,7 +450,13 @@
     norm = jnp.sqrt(jnp.sum(jnp.sum(matrix * matrix, axis=1, keepdims=True), axis=0, keepdims=True))
 
     def dot(a, b):
-        return jnp.dot(a, b, precision=HIGHEST, preferred_element_type=F32)
+        a_high, a_low = split_2(a)
+        b_high, b_low = split_2(b)
+
+        def one(x, y):
+            return jnp.dot(x, y, preferred_element_type=F32)
+
+        return one(a_high, b_high) + (one(a_high, b_low) + one(a_low, b_high))
 
     root = matrix / norm
     correction = 1.5 * eye - 0.5 * root
@@ -425,6 +471,7 @@
     weights = carried[0:k] / jnp.sqrt(norm) + shift[0:1, :]
     high, low = split_2(weights)
     high_2 = jnp.concatenate([high, high], axis=1)
+    copies = []
     for v in range(nv):
         for r in range(cx):
             deep = 2 <= r < cx - 2
@@ -435,12 +482,13 @@
             value = jnp.dot(high_2, anomalies[:, at], preferred_element_type=F32)
             value = value + jnp.dot(low, anomalies[0:k, at], preferred_element_type=F32)
             value = value + means[i * 8 + v : i * 8 + v + 1, :]
-            for h in range(cy // LANES):
-                buf[h, pl.ds(v * cx + r, k, stride=rows), :] = value[:, h * LANES : (h + 1) * LANES]
-    copies = []
-    for h in range(cy // LANES):
-        copies.append(pltpu.make_async_copy(buf.at[h], out.at[:, h * LANES : (h + 1) * LANES], sems.at[h]))
-        copies[-1].start()
+            for h in range(half):
+                buf[v * half + h, pl.ds(r, k, stride=cx), :] = value[:, h * LANES : (h + 1) * LANES]
+        for h in range(half):
+            source = buf.at[v * half + h].reshape(k, cx, LANES)
+            target = out.at[:, v, :, h * LANES : (h + 1) * LANES]
+            copies.append(pltpu.make_async_copy(source, target, sems.at[v, h]))
+            copies[-1].start()
     for copy in copies:
         copy.wait()
 
@@ -485,16 +533,16 @@
     side_b = y_swap(1, sizes)(side_b)
     recv_a = x_swap(0, sizes)(send_a)
 
-    cells = pl.pallas_call(
-        functools.partial(scatter_kernel, dims),
-        name="scatter",
-        in_specs=[vmem()] * 4,
-        out_specs=vmem(),
-        out_shape=shape(64, cy),
+    first, kext, spread = pl.pallas_call(
+        functools.partial(middle_kernel, dims),
+        name="middle",
+        in_specs=[smem()] + [vmem()] * 6,
+        out_specs=[vmem()] * 3,
+        out_shape=[shape((cx + 2) * block, cy), shape((cx + 2) * 8, cy), shape(cx * 8, cy)],
+        scratch_shapes=[pltpu.VMEM((64, cy), F32)],
         compiler_params=limits,
-    )(*obs)
-
-    side_a, side_b, cells = lax.optimization_barrier((side_a, side_b, cells))
+    )(mixing, state, kappa, *obs)
+    side_a, side_b, first = lax.optimization_barrier((side_a, side_b, first))
     halo = side_a + side_b
     corner_b = x_swap(1, sizes)(halo)
     corner_a = x_swap(0, sizes)(halo)
@@ -505,6 +553,7 @@
         name="inner",
         in_specs=[smem()] + [vmem()] * 5,
         out_specs=[vmem()] * 4,
+        input_output_aliases={1: 0},
         out_shape=[
             shape((cx + 2) * block, cy),
             shape(2 * k, inner_rows * nv * cy, dtype=BF16),
@@ -512,14 +561,13 @@
             shape(2 * k + 32, 2 * k),
         ],
         scratch_shapes=[
-            pltpu.VMEM(((cx + 2) * 8, cy), F32),
-            pltpu.VMEM((cx * 8, cy), F32),
+            pltpu.VMEM((k, LANES), F32),
             pltpu.VMEM((k, LANES), F32),
             pltpu.VMEM((2 * k + 32, inner_rows * nv * cy), BF16),
             pltpu.VMEM((block, cy), F32),
         ],
         compiler_params=limits,
-    )(mixing, state, sides, halo, kappa, cells)
+    )(mixing, first, sides, halo, kext, spread)
 
     _, _, edge_anomalies, edge_means, gram = pl.pallas_call(
         functools.partial(edge_kernel, dims, factor),
@@ -535,7 +583,6 @@
         ],
         scratch_shapes=[
             pltpu.VMEM(((cx + 2) * 8, cy), F32),
-            pltpu.VMEM((cx * 8, cy), F32),
             pltpu.VMEM((k, LANES), F32),
             pltpu.VMEM((k, LANES), F32),
             pltpu.VMEM((2 * k + 32, 4 * nv * cy), BF16),
@@ -544,21 +591,23 @@
         input_output_aliases={1: 0, 2: 1},
         compiler_params=limits,
     )(
-        mixing, state, first, partial, recv_a, recv_b, sides, halo, corner_a, corner_b, kappa, cells
+        mixing, state, first, partial, recv_a, recv_b, sides, halo, corner_a, corner_b, kext, spread
     )
 
     gram = all_sum(gram, sizes)
 
-    out = pl.pallas_call(
+    return pl.pallas_call(
         functools.partial(apply_kernel, dims),
         name="apply",
         in_specs=[vmem()] * 5,
         out_specs=pl.BlockSpec(memory_space=pltpu.HBM),
-        out_shape=shape(k * rows, cy),
-        scratch_shapes=[pltpu.VMEM((cy // LANES, k * rows, LANES), F32), pltpu.SemaphoreType.DMA((cy // LANES,))],
+        out_shape=shape(k, nv, cx, cy),
+        scratch_shapes=[
+            pltpu.VMEM((nv * (cy // LANES), k * cx, LANES), F32),
+            pltpu.SemaphoreType.DMA((nv, cy // LANES)),
+        ],
         compiler_params=limits,
     )(gram, inner_anomalies, inner_means, edge_anomalies, edge_means)
-    return out.reshape(k, nv, cx, cy)
 
 
 def solution(mesh):

time: 33.2 us -> 31.5 us (0.949)
  waiting for transfers between devices: 7.78 us -> 5.44 us
  starting transfers between devices: 10.9 us -> 11.7 us
    ppermute x12, waiting for transfers between devices: 7.78 us -> 5.44 us  [pair_swap(): return lambda value: lax.ppermute(value, ('grp', 'gx', 'gy'), pairs)]
    pallas_call x1, Pallas kernels: 0.5 us -> 2.15 us  [local(): pl.pallas_call(functools.partial(middle_kernel, dims), name='middle', in_...]
    ppermute x12, starting transfers between devices: 10.9 us -> 11.7 us  [pair_swap(): return lambda value: lax.ppermute(value, ('grp', 'gx', 'gy'), pairs)]
    pallas_call x1, Pallas kernels: 3.83 us -> 3.15 us  [local(): pl.pallas_call(functools.partial(inner_kernel, dims, factor), name='inner...]
    pallas_call x1, Pallas kernels: 3.99 us -> 3.33 us  [local(): pl.pallas_call(functools.partial(apply_kernel, dims), name='apply', in_sp...]
  transfers between devices with their start and end apart: 12 -> 12, of which waited for: 6 -> 6; matrix products, arithmetic and copies ran while one was open for 0% -> 0% of each run, Pallas kernels for 13% -> 17%
where the time goes in v3:
time: 31.5 us; the launch traced here: 31.4 us
  Pallas kernels  14.1 us (45%)
  starting transfers between devices  11.7 us (37%)
  waiting for transfers between devices  5.44 us (17%)
    ppermute x12, starting transfers between devices, pair_swap(): return lambda value: lax.ppermute(value, ('grp', 'gx', 'gy'), pairs)  11.7 us
    ppermute x12, waiting for transfers between devices, pair_swap(): return lambda value: lax.ppermute(value, ('grp', 'gx', 'gy'), pairs)  5.44 us
    pallas_call x1, Pallas kernels, local(): pl.pallas_call(functools.partial(edge_kernel, dims, factor), name='edge',...  3.47 us
    pallas_call x1, Pallas kernels, local(): pl.pallas_call(functools.partial(apply_kernel, dims), name='apply', in_sp...  3.33 us
    pallas_call x1, Pallas kernels, local(): pl.pallas_call(functools.partial(inner_kernel, dims, factor), name='inner...  3.15 us
    pallas_call x1, Pallas kernels, local(): pl.pallas_call(functools.partial(middle_kernel, dims), name='middle', in_...  2.15 us
    pallas_call x1, Pallas kernels, local(): pl.pallas_call(functools.partial(load_kernel, dims), name='load', in_spec...  2.03 us
  transfers between devices with their start and end apart: 12, of which 6 were waited for; matrix products, arithmetic and copies ran while one was open for 0% of the time, Pallas kernels for 17%

profile of v3, /device:TPU:0, one launch (start us, length us, event | category | flops | bytes accessed | tf_op | source)
XLA Modules:
  0.0 31.4 jit_solution(962341808779553160)
XLA Ops:
  0.0 2.0 %load.1 = (f32[2304,256]{1,0:T(8,128)S(1)}, f32[392,256]{1,0:T(8,128)S(1)}, f32[392,256]{1,0:T(8,128)S(1)}, f32[72,128]{1,0:T(8,128)S(1)}, f32[72,128]{1,0:T(8,1...) custom-call(f32[1536,256]{1,0:T(8,128)} %bitcast.5, ...), custom_call_target="tpu_custom_call" | custom-call | tf_op jit(solution)/shard_map/load/pallas_call | solution.py:511
  2.0 0.5 %collective-permute-start.2 = (f32[392,256]{1,0:T(8,128)S(1)}, f32[392,256]{1,0:T(8,128)S(1)}, u32[]{:S(2)}, u32[]{:S(2)}) collective-permute-start(f32[392,256]{1,0:T(8,128)S(1)} %get-tuple-element.48), channel_id=1, source_target_pairs={{0,4},{1,5},{2,6},{3,7},{4,0},{5,1},{6,2},{7,3},{8,12},{9,13},{10,... | collective-permute-start | bytes 1204232 | tf_op jit(solution)/shard_map/ppermute | solution.py:51
  2.6 2.6 %collective-permute-start.3 = (f32[392,256]{1,0:T(8,128)S(1)}, f32[392,256]{1,0:T(8,128)S(1)}, u32[]{:S(2)}, u32[]{:S(2)}) collective-permute-start(f32[392,256]{1,0:T(8,128)S(1)} %get-tuple-element.49), channel_id=1, source_target_pairs={{0,16},{1,17},{2,18},{3,19},{4,8},{5,9},{6,10},{7,11},{8,4},{9,5},... | collective-permute-start | bytes 1204232 | tf_op jit(solution)/shard_map/ppermute | solution.py:51
  5.2 1.6 %collective-permute-start = (f32[72,128]{1,0:T(8,128)S(1)}, f32[72,128]{1,0:T(8,128)S(1)}, u32[]{:S(2)}, u32[]{:S(2)}) collective-permute-start(f32[72,128]{1,0:T(8,128)S(1)} %get-tuple-element.32), channel_id=1, source_target_pairs={{0,1},{1,0},{2,3},{3,2},{4,5},{5,4},{6,7},{7,6},{8,9},{9,8},{10,11... | collective-permute-start | bytes 110600 | tf_op jit(solution)/shard_map/ppermute | solution.py:51
  6.7 0.0 collective-permute-start.1
  6.7 2.2 %middle.1 = (f32[1920,256]{1,0:T(8,128)S(1)}, f32[80,256]{1,0:T(8,128)S(1)}, f32[64,256]{1,0:T(8,128)S(1)}) custom-call(f32[3,3]{1,0:T(4,128)S(1)} %get-tuple-element.30.mixing, f32[2304,256]{1,0:T(8,128)S(1)} %get-tuple-element.31.state.state_in, f32[3,8,256]{2,1,0:T(8,128)S(1)} %get-tuple-element.34.kappa, s32[1,2048]{1,0:T(1,128)S(1)} %get-tuple-element.35.cell, ...), custom_call_target="tpu_custom_call" | custom-call | tf_op jit(solution)/shard_map/middle/pallas_call | solution.py:536
  8.9 0.2 collective-permute-done
  9.1 0.0 collective-permute-done.1
  9.1 1.2 %collective-permute-start.5 = (f32[72,128]{1,0:T(8,128)S(1)}, f32[72,128]{1,0:T(8,128)S(1)}, u32[]{:S(2)}, u32[]{:S(2)}) collective-permute-start(f32[72,128]{1,0:T(8,128)S(1)} %add.21.halo), channel_id=1, source_target_pairs={{0,16},{1,17},{2,18},{3,19},{4,8},{5,9},{6,10},{7,11},{8,4},{9,5},... | collective-permute-start | bytes 110600 | tf_op jit(solution)/shard_map/ppermute | solution.py:51
  10.3 0.2 collective-permute-start.4
  10.5 3.2 %inner.1 = (f32[1920,256]{1,0:T(8,128)S(1)}, bf16[128,3072]{1,0:T(8,128)(2,1)S(1)}, f32[32,256]{1,0:T(8,128)S(1)}, f32[160,128]{1,0:T(8,128)S(1)}) custom-call(f32[3,3]{1,0:T(4,128)S(1)} %get-tuple-element.30.mixing, f32[1920,256]{1,0:T(8,128)S(1)} %get-tuple-element.40.first_in, ...), custom_call_target="tpu_custom_call", output_to_operand_aliasing={{0}: (1, {})} | custom-call | tf_op jit(solution)/shard_map/inner/pallas_call | solution.py:551
  13.6 0.0 collective-permute-done.5.corner_b
  13.6 0.0 collective-permute-done.4.corner_a
  13.6 0.0 collective-permute-done.2.recv_a
  13.7 0.0 collective-permute-done.3.recv_b
  13.7 3.5 %edge.1 = (f32[2304,256]{1,0:T(8,128)S(1)}, f32[1920,256]{1,0:T(8,128)S(1)}, bf16[128,3072]{1,0:T(8,128)(2,1)S(1)}, f32[32,256]{1,0:T(8,128)S(1)}, f32[40,128]{1,0:T(8,128)S(1)}) custom-call(f32[3,3]{1,0:T(4,128)S(1)} %get-tuple-element.30.mixing, f32[2304,256]{1,0:T(8,128)S(1)} %get-tuple-element.31.state.state_in, ...), custom_call_target="tpu_custom_call", output_to_operand_aliasing={{0}: (1, {}), {1}: (2, {})} | custom-call | tf_op jit(solution)/shard_map/edge/pallas_call | solution.py:572
  17.1 0.4 %collective-permute-start.6 = (f32[40,128]{1,0:T(8,128)S(1)}, f32[40,128]{1,0:T(8,128)S(1)}, u32[]{:S(2)}, u32[]{:S(2)}) collective-permute-start(f32[40,128]{1,0:T(8,128)S(1)} %get-tuple-element.50), channel_id=1, source_target_pairs={{0,4},{1,5},{2,6},{3,7},{4,0},{5,1},{6,2},{7,3},{8,12},{9,13},{10,... | collective-permute-start | bytes 61448 | tf_op jit(solution)/shard_map/ppermute | solution.py:51
  17.5 0.8 %collective-permute-done.6 = f32[40,128]{1,0:T(8,128)S(1)} collective-permute-done((f32[40,128]{1,0:T(8,128)S(1)}, f32[40,128]{1,0:T(8,128)S(1)}, u32[]{:S(2)}, u32[]{:S(2)}) %collective-permute-start.6) | collective-permute-done | bytes 20512 | tf_op jit(solution)/shard_map/ppermute | solution.py:51
  18.4 3.2 %collective-permute-start.10 = (f32[40,128]{1,0:T(8,128)S(1)}, f32[40,128]{1,0:T(8,128)S(1)}, u32[]{:S(2)}, u32[]{:S(2)}) collective-permute-start(f32[40,128]{1,0:T(8,128)S(1)} %add.22), channel_id=1, source_target_pairs={{0,3},{1,2},{2,1},{3,0},{4,15},{5,14},{6,13},{7,12},{8,11},{9,10},... | collective-permute-start | bytes 61448 | tf_op jit(solution)/shard_map/ppermute | solution.py:51
  21.6 0.7 %collective-permute-start.9 = (f32[40,128]{1,0:T(8,128)S(1)}, f32[40,128]{1,0:T(8,128)S(1)}, u32[]{:S(2)}, u32[]{:S(2)}) collective-permute-start(f32[40,128]{1,0:T(8,128)S(1)} %add.22), channel_id=1, source_target_pairs={{0,2},{1,3},{2,0},{3,1},{4,14},{5,15},{6,12},{7,13},{8,10},{9,11},... | collective-permute-start | bytes 61448 | tf_op jit(solution)/shard_map/ppermute | solution.py:51
  22.3 0.5 %collective-permute-start.8 = (f32[40,128]{1,0:T(8,128)S(1)}, f32[40,128]{1,0:T(8,128)S(1)}, u32[]{:S(2)}, u32[]{:S(2)}) collective-permute-start(f32[40,128]{1,0:T(8,128)S(1)} %add.22), channel_id=1, source_target_pairs={{0,1},{1,0},{2,3},{3,2},{4,13},{5,12},{6,15},{7,14},{8,9},{9,8},{1... | collective-permute-start | bytes 61448 | tf_op jit(solution)/shard_map/ppermute | solution.py:51
  22.8 0.8 %collective-permute-start.7 = (f32[40,128]{1,0:T(8,128)S(1)}, f32[40,128]{1,0:T(8,128)S(1)}, u32[]{:S(2)}, u32[]{:S(2)}) collective-permute-start(f32[40,128]{1,0:T(8,128)S(1)} %add.22), channel_id=1, source_target_pairs={{0,8},{1,9},{2,10},{3,11},{4,12},{5,13},{6,14},{7,15},{8,0},{9,1},... | collective-permute-start | bytes 61448 | tf_op jit(solution)/shard_map/ppermute | solution.py:51
  23.6 0.4 %collective-permute-done.10 = f32[40,128]{1,0:T(8,128)S(1)} collective-permute-done((f32[40,128]{1,0:T(8,128)S(1)}, f32[40,128]{1,0:T(8,128)S(1)}, u32[]{:S(2)}, u32[]{:S(2)}) %collective-permute-start.10) | collective-permute-done | bytes 20512 | tf_op jit(solution)/shard_map/ppermute | solution.py:51
  24.0 2.6 %collective-permute-done.9 = f32[40,128]{1,0:T(8,128)S(1)} collective-permute-done((f32[40,128]{1,0:T(8,128)S(1)}, f32[40,128]{1,0:T(8,128)S(1)}, u32[]{:S(2)}, u32[]{:S(2)}) %collective-permute-start.9) | collective-permute-done | bytes 20512 | tf_op jit(solution)/shard_map/ppermute | solution.py:51
  26.6 0.0 collective-permute-done.8
  26.6 0.2 collective-permute-done.7
  26.8 0.1 collective-permute-start.11
  26.8 1.2 %collective-permute-done.11 = f32[40,128]{1,0:T(8,128)S(1)} collective-permute-done((f32[40,128]{1,0:T(8,128)S(1)}, f32[40,128]{1,0:T(8,128)S(1)}, u32[]{:S(2)}, u32[]{:S(2)}) %collective-permute-start.11) | collective-permute-done | bytes 20512 | tf_op jit(solution)/shard_map/ppermute | solution.py:51
  28.0 3.3 %apply.1 = f32[64,3,8,256]{3,2,1,0:T(8,128)} custom-call(f32[40,128]{1,0:T(8,128)S(1)} %add.27.gram, bf16[128,3072]{1,0:T(8,128)(2,1)S(1)} %get-tuple-element.51.inner, f32[32,256]{1,0:T(8,128)S(1)} %get-tuple-element.52.inner_means, bf16[128,3072]{1,0:T(8,128)(2,1)S(1)} %get-tuple-element.53.edge, f32[32,256]{1,0:T(8,128)S(1)} %get-tuple-element.54.edge_means), custom_call_target="tpu_custom_call" | custom-call | tf_op jit(solution)/shard_map/apply/pallas_call | solution.py:599
  (4 shorter events, 0.0 us)
Async XLA Ops:
  2.0 11.6 %collective-permute-start.2 = (f32[392,256]{1,0:T(8,128)S(1)}, f32[392,256]{1,0:T(8,128)S(1)}, u32[]{:S(2)}, u32[]{:S(2)}) collective-permute-start(f32[392,256]{1,0:T(8,128)S(1)} %get-tuple-element.48), channel_id=1, source_target_pairs={{0,4},{1,5},{2,6},{3,7},{4,0},{5,1},{6,2},{7,3},{8,12},{9,13},{10,... | collective-permute-start | bytes 1204232 | tf_op jit(solution)/shard_map/ppermute | solution.py:51
  2.6 11.1 %collective-permute-start.3 = (f32[392,256]{1,0:T(8,128)S(1)}, f32[392,256]{1,0:T(8,128)S(1)}, u32[]{:S(2)}, u32[]{:S(2)}) collective-permute-start(f32[392,256]{1,0:T(8,128)S(1)} %get-tuple-element.49), channel_id=1, source_target_pairs={{0,16},{1,17},{2,18},{3,19},{4,8},{5,9},{6,10},{7,11},{8,4},{9,5},... | collective-permute-start | bytes 1204232 | tf_op jit(solution)/shard_map/ppermute | solution.py:51
  5.2 4.0 %collective-permute-start = (f32[72,128]{1,0:T(8,128)S(1)}, f32[72,128]{1,0:T(8,128)S(1)}, u32[]{:S(2)}, u32[]{:S(2)}) collective-permute-start(f32[72,128]{1,0:T(8,128)S(1)} %get-tuple-element.32), channel_id=1, source_target_pairs={{0,1},{1,0},{2,3},{3,2},{4,5},{5,4},{6,7},{7,6},{8,9},{9,8},{10,11... | collective-permute-start | bytes 110600 | tf_op jit(solution)/shard_map/ppermute | solution.py:51
  6.7 2.4 %collective-permute-start.1 = (f32[72,128]{1,0:T(8,128)S(1)}, f32[72,128]{1,0:T(8,128)S(1)}, u32[]{:S(2)}, u32[]{:S(2)}) collective-permute-start(f32[72,128]{1,0:T(8,128)S(1)} %get-tuple-element.33), channel_id=1, source_target_pairs={{0,4},{1,2},{2,1},{3,7},{4,0},{5,6},{6,5},{7,3},{8,12},{9,10},{10,... | collective-permute-start | bytes 110600 | tf_op jit(solution)/shard_map/ppermute | solution.py:51
  9.1 4.5 %collective-permute-start.5 = (f32[72,128]{1,0:T(8,128)S(1)}, f32[72,128]{1,0:T(8,128)S(1)}, u32[]{:S(2)}, u32[]{:S(2)}) collective-permute-start(f32[72,128]{1,0:T(8,128)S(1)} %add.21.halo), channel_id=1, source_target_pairs={{0,16},{1,17},{2,18},{3,19},{4,8},{5,9},{6,10},{7,11},{8,4},{9,5},... | collective-permute-start | bytes 110600 | tf_op jit(solution)/shard_map/ppermute | solution.py:51
  10.3 3.3 %collective-permute-start.4 = (f32[72,128]{1,0:T(8,128)S(1)}, f32[72,128]{1,0:T(8,128)S(1)}, u32[]{:S(2)}, u32[]{:S(2)}) collective-permute-start(f32[72,128]{1,0:T(8,128)S(1)} %add.21.halo), channel_id=1, source_target_pairs={{0,4},{1,5},{2,6},{3,7},{4,0},{5,1},{6,2},{7,3},{8,12},{9,13},{10,... | collective-permute-start | bytes 110600 | tf_op jit(solution)/shard_map/ppermute | solution.py:51
  17.1 1.2 %collective-permute-start.6 = (f32[40,128]{1,0:T(8,128)S(1)}, f32[40,128]{1,0:T(8,128)S(1)}, u32[]{:S(2)}, u32[]{:S(2)}) collective-permute-start(f32[40,128]{1,0:T(8,128)S(1)} %get-tuple-element.50), channel_id=1, source_target_pairs={{0,4},{1,5},{2,6},{3,7},{4,0},{5,1},{6,2},{7,3},{8,12},{9,13},{10,... | collective-permute-start | bytes 61448 | tf_op jit(solution)/shard_map/ppermute | solution.py:51
  18.4 5.6 %collective-permute-start.10 = (f32[40,128]{1,0:T(8,128)S(1)}, f32[40,128]{1,0:T(8,128)S(1)}, u32[]{:S(2)}, u32[]{:S(2)}) collective-permute-start(f32[40,128]{1,0:T(8,128)S(1)} %add.22), channel_id=1, source_target_pairs={{0,3},{1,2},{2,1},{3,0},{4,15},{5,14},{6,13},{7,12},{8,11},{9,10},... | collective-permute-start | bytes 61448 | tf_op jit(solution)/shard_map/ppermute | solution.py:51
  21.6 5.0 %collective-permute-start.9 = (f32[40,128]{1,0:T(8,128)S(1)}, f32[40,128]{1,0:T(8,128)S(1)}, u32[]{:S(2)}, u32[]{:S(2)}) collective-permute-start(f32[40,128]{1,0:T(8,128)S(1)} %add.22), channel_id=1, source_target_pairs={{0,2},{1,3},{2,0},{3,1},{4,14},{5,15},{6,12},{7,13},{8,10},{9,11},... | collective-permute-start | bytes 61448 | tf_op jit(solution)/shard_map/ppermute | solution.py:51
  22.3 4.3 %collective-permute-start.8 = (f32[40,128]{1,0:T(8,128)S(1)}, f32[40,128]{1,0:T(8,128)S(1)}, u32[]{:S(2)}, u32[]{:S(2)}) collective-permute-start(f32[40,128]{1,0:T(8,128)S(1)} %add.22), channel_id=1, source_target_pairs={{0,1},{1,0},{2,3},{3,2},{4,13},{5,12},{6,15},{7,14},{8,9},{9,8},{1... | collective-permute-start | bytes 61448 | tf_op jit(solution)/shard_map/ppermute | solution.py:51
  22.8 4.0 %collective-permute-start.7 = (f32[40,128]{1,0:T(8,128)S(1)}, f32[40,128]{1,0:T(8,128)S(1)}, u32[]{:S(2)}, u32[]{:S(2)}) collective-permute-start(f32[40,128]{1,0:T(8,128)S(1)} %add.22), channel_id=1, source_target_pairs={{0,8},{1,9},{2,10},{3,11},{4,12},{5,13},{6,14},{7,15},{8,0},{9,1},... | collective-permute-start | bytes 61448 | tf_op jit(solution)/shard_map/ppermute | solution.py:51
  26.8 1.3 %collective-permute-start.11 = (f32[40,128]{1,0:T(8,128)S(1)}, f32[40,128]{1,0:T(8,128)S(1)}, u32[]{:S(2)}, u32[]{:S(2)}) collective-permute-start(f32[40,128]{1,0:T(8,128)S(1)} %add_add_fusion), channel_id=1, source_target_pairs={{0,4},{1,5},{2,6},{3,7},{4,0},{5,1},{6,2},{7,3},{8,12},{9,13},{10,... | collective-permute-start | bytes 61448 | tf_op jit(solution)/shard_map/ppermute | solution.py:51

commit v4 on v3

--- a/solution.py
+++ b/solution.py
@@ -104,9 +104,25 @@
     return value
 
 
+def send_rows(dims, state, kappa, ref, near_top):
+    k, nv, cx, cy = dims
+    block = nv * k
+    gx = lax.axis_index("gx")
+    has = jnp.where(near_top, gx > 0, gx < lax.axis_size("gx") - 1)
+    near = jnp.where(near_top, 2, cx + 1) * block
+    second = jnp.where(near_top, 3, cx) * block
+    for j in range(0, block, 64):
+        ref[pl.ds(j, 64), :] = jnp.where(has, state[pl.ds(pl.multiple_of(near + j, 64), 64), :], 0.0)
+        ref[pl.ds(block + j, 64), :] = jnp.where(has, state[pl.ds(pl.multiple_of(second + j, 64), 64), :], 0.0)
+    for v in range(nv):
+        edge = jnp.where(near_top, kappa[v, 0:1, :], kappa[v, cx - 1 : cx, :])
+        ref[pl.ds(2 * block + v, 1), :] = jnp.where(has, edge, 0.0)
+    ref[pl.ds(2 * block + nv, 8 - nv), :] = jnp.zeros((8 - nv, cy), F32)
+
+
 def load_kernel(dims, ens, *refs):
-    small_in, (state, send_a, send_b, sides, side_a, side_b) = refs[:6], refs[6:12]
-    small, (buf, sems, small_sems) = refs[12:18], refs[18:]
+    small_in, (state, send_b, sides, side_a, side_b) = refs[:6], refs[6:11]
+    small, (buf, sems, small_sems) = refs[11:17], refs[17:]
     kappa = small[0]
     k, nv, cx, cy = dims
     rows = nv * cx
@@ -159,25 +175,7 @@
         put_sides(pl.ds(c * part, part), total)
     for copy in small_copies:
         copy.wait()
-    block = nv * k
-    even_x = lax.axis_index("gx") % 2 == 0
-    top = 2 * block
-    bottom = (cx + 1) * block
-    gx = lax.axis_index("gx")
-    has_up = gx > 0
-    has_down = gx < lax.axis_size("gx") - 1
-    for ref, near_top in ((send_a, jnp.logical_not(even_x)), (send_b, even_x)):
-        has = jnp.where(near_top, has_up, has_down)
-        near = jnp.where(near_top, top, bottom)
-        second = jnp.where(near_top, top + block, bottom - block)
-        for j in range(0, block, 64):
-            ref[pl.ds(j, 64), :] = jnp.where(has, state[pl.ds(pl.multiple_of(near + j, 64), 64), :], 0.0)
-            ref[pl.ds(block + j, 64), :] = jnp.where(has, state[pl.ds(pl.multiple_of(second + j, 64), 64), :], 0.0)
-        for v in range(nv):
-            edge = jnp.where(near_top, kappa[v, 0:1, :], kappa[v, cx - 1 : cx, :])
-            ref[pl.ds(2 * block + v, 1), :] = jnp.where(has, edge, 0.0)
-        ref[pl.ds(2 * block + nv, 8 - nv), :] = jnp.zeros((8 - nv, cy), F32)
-
+    send_rows(dims, state, kappa, send_b, lax.axis_index("gx") % 2 == 0)
     total = jnp.zeros((8, LANES), F32)
     for r in range(cx):
         for v in range(nv):
@@ -234,27 +232,28 @@
 def advance(dims, mixing, kext, load, side, e, lane, store):
     k, nv, cx, cy = dims
     half = cy // LANES
-    eight = pl.ds(pl.multiple_of(e * 8, 8), 8)
+    eight = pl.ds(e * 8, 8)
     kappas = [kext[eight, h * LANES : (h + 1) * LANES] for h in range(half)]
     first_lane = lane == 0
     last_lane = lane == LANES - 1
-    for v in range(nv):
-        shift = (LANES - 1 - 2 * (nv * e + v)) & (LANES - 1)
-        kap = [jnp.broadcast_to(kappas[h][v : v + 1], (8, LANES)) for h in range(half)]
-        own = [1.0 - 4.0 * kap[h] + mixing[v, v] for h in range(half)]
-        others = [(w, mixing[v, w]) for w in range(nv) if w != v]
-        for j in range(0, k, 8):
+    kap = [[jnp.broadcast_to(kappas[h][v : v + 1], (8, LANES)) for h in range(half)] for v in range(nv)]
+    own = [[1.0 - 4.0 * kap[v][h] + mixing[v, v] for h in range(half)] for v in range(nv)]
+    for j in range(0, k, 8):
+        centers = [[load(0, v, j, h) for h in range(half)] for v in range(nv)]
+        for v in range(nv):
+            center = centers[v]
+            shift = (LANES - 1 - 2 * (nv * e + v)) & (LANES - 1)
             edge = 0.0 if side is None else pltpu.roll(side[pl.ds(j, 8), :], shift, 1)
-            center = [load(0, v, j, h) for h in range(half)]
             ahead = [pltpu.roll(c, 1, 1) for c in center]
             behind = [pltpu.roll(c, LANES - 1, 1) for c in center]
             for h in range(half):
                 left = jnp.where(first_lane, edge if h == 0 else ahead[h - 1], ahead[h])
                 right = jnp.where(last_lane, edge if h == half - 1 else behind[h + 1], behind[h])
                 around = (load(-1, v, j, h) + load(1, v, j, h)) + (left + right)
-                out = own[h] * center[h] + kap[h] * around
-                for w, factor in others:
-                    out = out + factor * load(0, w, j, h)
+                out = own[v][h] * center[h] + kap[v][h] * around
+                for w in range(nv):
+                    if w != v:
+                        out = out + mixing[v, w] * centers[w][h]
                 store(v, j, h, out)
 
 
@@ -264,96 +263,89 @@
 
 def loader(ref, base, k, row_size):
     def load(row, w, j, h):
-        at = pl.multiple_of(base + row * row_size + w * k + j, 8)
+        at = base + row * row_size + w * k + j
         return ref[pl.ds(at, 8), h * LANES : (h + 1) * LANES]
 
     return load
 
 
-def first_step(dims, mixing, kext, state, first, side, count, row_of, lane):
+def first_step(dims, mixing, kext, state, first, side, rows, lane, inside=False):
     k, nv, cx, cy = dims
     block = nv * k
-
-    def step(i, carry):
-        e = row_of(i)
+    for e in rows:
 
         def store(v, j, h, out):
-            first[pl.ds(pl.multiple_of(e * block + v * k + j, 8), 8), h * LANES : (h + 1) * LANES] = out
-
-        advance(dims, mixing, kext, loader(state, (e + 1) * block, k, block), side, e, lane, store)
-        return carry
-
-    lax.fori_loop(0, count, step, 0)
-
-
-def add_sides(dims, kext, first, side, count, row_of, lane):
+            first[pl.ds(e * block + v * k + j, 8), h * LANES : (h + 1) * LANES] = out
+
+        plain = loader(state, (e + 1) * block, k, block)
+
+        def load(row, w, j, h):
+            return 0.0 if inside and not 1 <= e + row <= cx else plain(row, w, j, h)
+
+        advance(dims, mixing, kext, load, side, e, lane, store)
+
+
+def add_sides(dims, kext, first, side, rows, lane):
     k, nv, cx, cy = dims
     block = nv * k
     ends = ((0, lane == 0), (cy - LANES, lane == LANES - 1))
-
-    def step(i, carry):
-        e = row_of(i)
-        eight = pl.ds(pl.multiple_of(e * 8, 8), 8)
+    for e in rows:
         for v in range(nv):
             shift = (LANES - 1 - 2 * (nv * e + v)) & (LANES - 1)
             kap = []
             for at, here in ends:
-                row = jnp.where(here, kext[eight, at : at + LANES][v : v + 1], 0.0)
+                row = jnp.where(here, kext[e * 8 + v : e * 8 + v + 1, at : at + LANES], 0.0)
                 kap.append(jnp.broadcast_to(row, (8, LANES)))
             for j in range(0, k, 8):
                 edge = pltpu.roll(side[pl.ds(j, 8), :], shift, 1)
-                rows = pl.ds(pl.multiple_of(e * block + v * k + j, 8), 8)
+                place = pl.ds(e * block + v * k + j, 8)
                 for (at, here), factor in zip(ends, kap):
-                    first[rows, at : at + LANES] += factor * edge
-        return carry
-
-    lax.fori_loop(0, count, step, 0)
-
-
-def second_step(dims, factor, mixing, kext, spread, first, first_side, count, row_of, outs, lane):
+                    first[place, at : at + LANES] += factor * edge
+
+
+def second_step(dims, mixing, kext, first, first_side, e, ref, slot, lane):
+    k, nv, cx, cy = dims
+    block = nv * k
+    sums = {}
+
+    def store(v, j, h, out):
+        ref[pl.ds(slot * block + v * k + j, 8), h * LANES : (h + 1) * LANES] = out
+        sums[v, h] = out if j == 0 else sums[v, h] + out
+
+    advance(dims, mixing, kext, loader(first, e * block, k, block), first_side, e, lane, store)
+    return sums
+
+
+def anomalies_of(dims, factor, spread, e, i, sums, kept, outs):
     k, nv, cx, cy = dims
     block = nv * k
     half = cy // LANES
-    anomalies, means, moved, kept = outs
+    anomalies, means, moved = outs
     sub = lax.broadcasted_iota(jnp.int32, (8, 1), 0)
-
-    def step_2(i, carry):
-        e = row_of(i)
-        eight = pl.ds(pl.multiple_of((e - 1) * 8, 8), 8)
-        spreads = [spread[eight, h * LANES : (h + 1) * LANES] for h in range(half)]
-
-        def store(v, j, h, out):
-            kept[pl.ds(v * k + j, 8), h * LANES : (h + 1) * LANES] = out
-
-        advance(dims, mixing, kext, loader(first, e * block, k, block), first_side, e, lane, store)
-        for h in range(half):
-            found = jnp.zeros((8, LANES), F32)
-            for v in range(nv):
-                lanes = slice(h * LANES, (h + 1) * LANES)
-                out = kept[v * k : (v + 1) * k, lanes]
-                mean = jnp.sum(out, axis=0, keepdims=True) * (1.0 / k)
-                found = jnp.where(sub == v, mean, found)
-                s2 = spreads[h][v : v + 1]
-                s1 = spreads[h][nv + v : nv + v + 1]
-                at = pl.ds(pl.multiple_of((i * nv + v) * cy + h * LANES, LANES), LANES)
-                scale = s2 * (factor * factor)
-                for j in range(0, k, 16):
-                    part = out[j : j + 16] - mean
-                    high, low = split_2(part)
-                    anomalies[j : j + 16, at] = high
-                    anomalies[k + j : k + j + 16, at] = low
-                    high, low = split_2(part * scale)
-                    moved[j : j + 16, at] = high
-                    moved[k + j : k + j + 16, at] = low
-                pull = jnp.broadcast_to((s1 - mean * s2) * factor, (16, LANES))
-                high, low = split_2(pull)
-                moved[2 * k : 2 * k + 16, at] = high
-                moved[2 * k + 16 : 2 * k + 32, at] = low
-            means[pl.ds(pl.multiple_of(i * 8, 8), 8), h * LANES : (h + 1) * LANES] = found
-        return carry
-
-    lax.fori_loop(0, count, step_2, 0)
-    return nt(moved[...], anomalies[...])
+    for h in range(half):
+        lanes = slice(h * LANES, (h + 1) * LANES)
+        spreads = spread[pl.ds((e - 1) * 8, 8), lanes]
+        found = jnp.zeros((8, LANES), F32)
+        for v in range(nv):
+            mean = jnp.sum(sums[v, h], axis=0, keepdims=True) * (1.0 / k)
+            found = jnp.where(sub == v, mean, found)
+            s2 = spreads[v : v + 1]
+            s1 = spreads[nv + v : nv + v + 1]
+            at = pl.ds((i * nv + v) * cy + h * LANES, LANES)
+            scale = s2 * (factor * factor)
+            for j in range(0, k, 16):
+                part = kept[pl.ds(i * block + v * k + j, 16), lanes] - mean
+                high, low = split_2(part)
+                anomalies[j : j + 16, at] = high
+                anomalies[k + j : k + j + 16, at] = low
+                high, low = split_2(part * scale)
+                moved[j : j + 16, at] = high
+                moved[k + j : k + j + 16, at] = low
+            pull = jnp.broadcast_to((s1 - mean * s2) * factor, (16, LANES))
+            high, low = split_2(pull)
+            moved[2 * k : 2 * k + 16, at] = high
+            moved[2 * k + 16 : 2 * k + 32, at] = low
+        means[i * 8 : i * 8 + 8, lanes] = found
 
 
 def set_kappa(dims, kappa, kext):
@@ -363,8 +355,9 @@
             kext[pl.ds((r + 1) * 8 + v, 1), :] = kappa[v, r : r + 1, :]
 
 
-def middle_kernel(dims, mixing, state, kappa, cell, var, value, weight, first, kext, spread, cells):
-    k, nv, cx, cy = dims
+def middle_kernel(dims, mixing, state, kappa, cell, var, value, weight, first, kext, spread, send_a, cells):
+    k, nv, cx, cy = dims
+    send_rows(dims, state, kappa, send_a, lax.axis_index("gx") % 2 == 1)
     scatter_kernel(dims, cell, var, value, weight, cells)
     for v in range(nv):
         for r in range(cx):
@@ -372,27 +365,30 @@
             spread[pl.ds(r * 8 + nv + v, 1), :] = cells[pl.ds(32 + r * nv + v, 1), :]
     set_kappa(dims, kappa, kext)
     lane = lax.broadcasted_iota(jnp.int32, (1, LANES), 1)
-    first_step(dims, mixing, kext, state, first, None, cx - 2, lambda i: i + 2, lane)
+    first_step(dims, mixing, kext, state, first, None, range(1, cx + 1), lane, inside=True)
 
 
 def inner_kernel(
     dims, factor, mixing, first_in, sides, halo, kext, spread,
-    first, anomalies, means, partial, side, first_side, moved, kept,
+    first, anomalies, means, partial, early, side, first_side, moved, kept,
 ):
     k, nv, cx, cy = dims
     lane = lax.broadcasted_iota(jnp.int32, (1, LANES), 1)
     columns = first_columns_of(dims, mixing, halo[0:k, :], halo[k : k + 1, :], sides[0:k, :], lane)
     side[...] = edges_of(halo[0:k, :], lane)
     first_side[...] = edges_of(columns, lane)
-    add_sides(dims, kext, first, side, cx - 2, lambda i: i + 2, lane)
-    outs = (anomalies, means, moved, kept)
-    partial[...] = second_step(
-        dims, factor, mixing, kext, spread, first, first_side, cx - 4, lambda i: i + 3, outs, lane
-    )
+    add_sides(dims, kext, first, side, range(1, cx + 1), lane)
+    outs = (anomalies, means, moved)
+    for i, e in enumerate(range(3, cx - 1)):
+        sums = second_step(dims, mixing, kext, first, first_side, e, kept, i, lane)
+        anomalies_of(dims, factor, spread, e, i, sums, kept, outs)
+    partial[...] = nt(moved[...], anomalies[...])
+    second_step(dims, mixing, kext, first, first_side, 2, early, 0, lane)
+    second_step(dims, mixing, kext, first, first_side, cx - 1, early, 1, lane)
 
 
 def edge_kernel(
-    dims, factor, mixing, state_in, first_in, partial, recv_a, recv_b, sides, halo, corner_a, corner_b, kext_in, spread,
+    dims, factor, mixing, state_in, first_in, partial, early, recv_a, recv_b, sides, halo, corner_a, corner_b, kext_in, spread,
     state, first, anomalies, means, gram, kext, side, first_side, moved, kept,
 ):
     k, nv, cx, cy = dims
@@ -424,13 +420,37 @@
     side[...] = edges_of(columns[0:k, :], lane)
     columns = first_columns_of(dims, mixing, columns[0:k, :], columns[k : k + 1, :], sides[0:k, :], lane)
     first_side[...] = edges_of(columns, lane)
-    first_step(
-        dims, mixing, kext, state, first, side, 4, lambda i: jnp.where(i < 2, i, i + cx - 2), lane
-    )
-    got = partial[...] + second_step(
-        dims, factor, mixing, kext, spread, first, first_side, 4, lambda i: jnp.where(i < 2, i + 1, i + cx - 3),
-        (anomalies, means, moved, kept), lane,
-    )
+    first_step(dims, mixing, kext, state, first, side, (0, cx + 1), lane)
+    half = cy // LANES
+    outs = (anomalies, means, moved)
+
+    def late(e, beyond, near, read, write):
+        sums = {}
+        for v in range(nv):
+            for h in range(half):
+                lanes = slice(h * LANES, (h + 1) * LANES)
+                row = kext[e * 8 + v : e * 8 + v + 1, lanes]
+                if near != e:
+                    row = row * kext[near * 8 + v : near * 8 + v + 1, lanes]
+                row = jnp.broadcast_to(row, (8, LANES))
+                for j in range(0, k, 8):
+                    out = read[0][pl.ds(read[1] + v * k + j, 8), lanes]
+                    out = out + row * state[pl.ds(beyond * block + v * k + j, 8), lanes]
+                    write[0][pl.ds(write[1] + v * k + j, 8), lanes] = out
+                    sums[v, h] = out if j == 0 else sums[v, h] + out
+        return sums
+
+    for e, beyond in ((1, 1), (cx, cx + 2)):
+        late(e, beyond, e, (first, e * block), (first, e * block))
+    for i, e in enumerate((1, 2, cx - 1, cx)):
+        if i in (0, 3):
+            sums = second_step(dims, mixing, kext, first, first_side, e, kept, i, lane)
+        elif i == 1:
+            sums = late(e, 1, 1, (early, 0), (kept, i * block))
+        else:
+            sums = late(e, cx + 2, cx, (early, block), (kept, i * block))
+        anomalies_of(dims, factor, spread, e, i, sums, kept, outs)
+    got = partial[...] + nt(moved[...], anomalies[...])
     whole = got[:, 0:k] + got[:, k : 2 * k]
     matrix = whole[0:k] + whole[k : 2 * k]
     pull = whole[2 * k : 2 * k + 8] + whole[2 * k + 16 : 2 * k + 24]
@@ -447,25 +467,28 @@
     both = gram[...]
     matrix = jnp.concatenate([both[0 : k // 2, 0:k], both[0 : k // 2, k : 2 * k]], axis=0) + eye
     pull = both[k // 2 : k // 2 + 8, 0:k]
+    pull = jnp.concatenate([pull, pull], axis=0)
     norm = jnp.sqrt(jnp.sum(jnp.sum(matrix * matrix, axis=1, keepdims=True), axis=0, keepdims=True))
+
+    def one(x, y):
+        return jnp.dot(x, y, preferred_element_type=F32)
 
     def dot(a, b):
         a_high, a_low = split_2(a)
         b_high, b_low = split_2(b)
-
-        def one(x, y):
-            return jnp.dot(x, y, preferred_element_type=F32)
-
-        return one(a_high, b_high) + (one(a_high, b_low) + one(a_low, b_high))
+        rows = a.shape[0]
+        both = one(jnp.concatenate([a_high, a_low], axis=0), b_high)
+        return both[0:rows] + (both[rows:] + one(a_high, b_low))
 
     root = matrix / norm
     correction = 1.5 * eye - 0.5 * root
-    carried = jnp.concatenate([correction, dot(pull, correction)], axis=0)
-    root = dot(root, correction)
+    stacked = dot(jnp.concatenate([root, pull], axis=0), correction)
+    root = dot(stacked[0:k], correction)
+    carried = jnp.concatenate([correction, stacked[k:]], axis=0)
     for i in range(1, NS_ITERS):
-        correction = 1.5 * eye - 0.5 * dot(carried[0:k], root)
+        correction = 1.5 * eye - 0.5 * root
         if i < NS_ITERS - 1:
-            root = dot(root, correction)
+            root = dot(dot(root, correction), correction)
         carried = dot(carried, correction)
     shift = dot(carried[k:], carried[0:k]) / norm
     weights = carried[0:k] / jnp.sqrt(norm) + shift[0:1, :]
@@ -508,14 +531,13 @@
         return jax.ShapeDtypeStruct(dims, dtype)
 
     small = (diffusivity, mixing) + tuple(a.reshape(1, count) for a in (obs_cell, obs_var, obs_value, obs_weight))
-    state, send_a, send_b, sides, side_a, side_b, kappa, mixing, *obs = pl.pallas_call(
+    state, send_b, sides, side_a, side_b, kappa, mixing, *obs = pl.pallas_call(
         functools.partial(load_kernel, dims),
         name="load",
         in_specs=[pl.BlockSpec(memory_space=pltpu.HBM)] * 7,
-        out_specs=[vmem()] * 12,
+        out_specs=[vmem()] * 11,
         out_shape=[
             shape((cx + 4) * block, cy),
-            shape(2 * block + 8, cy),
             shape(2 * block + 8, cy),
             shape(k + 8, LANES),
             shape(k + 8, LANES),
@@ -531,40 +553,46 @@
     recv_b = x_swap(1, sizes)(send_b)
     side_a = y_swap(0, sizes)(side_a)
     side_b = y_swap(1, sizes)(side_b)
-    recv_a = x_swap(0, sizes)(send_a)
-
-    first, kext, spread = pl.pallas_call(
+
+    first, kext, spread, send_a = pl.pallas_call(
         functools.partial(middle_kernel, dims),
         name="middle",
         in_specs=[smem()] + [vmem()] * 6,
-        out_specs=[vmem()] * 3,
-        out_shape=[shape((cx + 2) * block, cy), shape((cx + 2) * 8, cy), shape(cx * 8, cy)],
+        out_specs=[vmem()] * 4,
+        out_shape=[
+            shape((cx + 2) * block, cy),
+            shape((cx + 2) * 8, cy),
+            shape(cx * 8, cy),
+            shape(2 * block + 8, cy),
+        ],
         scratch_shapes=[pltpu.VMEM((64, cy), F32)],
         compiler_params=limits,
     )(mixing, state, kappa, *obs)
-    side_a, side_b, first = lax.optimization_barrier((side_a, side_b, first))
+    side_a, side_b, first, send_a = lax.optimization_barrier((side_a, side_b, first, send_a))
+    recv_a = x_swap(0, sizes)(send_a)
     halo = side_a + side_b
     corner_b = x_swap(1, sizes)(halo)
     corner_a = x_swap(0, sizes)(halo)
 
     inner_rows = cx - 4
-    first, inner_anomalies, inner_means, partial = pl.pallas_call(
+    first, inner_anomalies, inner_means, partial, early = pl.pallas_call(
         functools.partial(inner_kernel, dims, factor),
         name="inner",
         in_specs=[smem()] + [vmem()] * 5,
-        out_specs=[vmem()] * 4,
+        out_specs=[vmem()] * 5,
         input_output_aliases={1: 0},
         out_shape=[
             shape((cx + 2) * block, cy),
             shape(2 * k, inner_rows * nv * cy, dtype=BF16),
             shape(inner_rows * 8, cy),
             shape(2 * k + 32, 2 * k),
+            shape(2 * block, cy),
         ],
         scratch_shapes=[
             pltpu.VMEM((k, LANES), F32),
             pltpu.VMEM((k, LANES), F32),
             pltpu.VMEM((2 * k + 32, inner_rows * nv * cy), BF16),
-            pltpu.VMEM((block, cy), F32),
+            pltpu.VMEM((4 * block, cy), F32),
         ],
         compiler_params=limits,
     )(mixing, first, sides, halo, kext, spread)
@@ -572,7 +600,7 @@
     _, _, edge_anomalies, edge_means, gram = pl.pallas_call(
         functools.partial(edge_kernel, dims, factor),
         name="edge",
-        in_specs=[smem()] + [vmem()] * 11,
+        in_specs=[smem()] + [vmem()] * 12,
         out_specs=[vmem()] * 5,
         out_shape=[
             shape((cx + 4) * block, cy),
@@ -586,12 +614,12 @@
             pltpu.VMEM((k, LANES), F32),
             pltpu.VMEM((k, LANES), F32),
             pltpu.VMEM((2 * k + 32, 4 * nv * cy), BF16),
-            pltpu.VMEM((block, cy), F32),
+            pltpu.VMEM((4 * block, cy), F32),
         ],
         input_output_aliases={1: 0, 2: 1},
         compiler_params=limits,
     )(
-        mixing, state, first, partial, recv_a, recv_b, sides, halo, corner_a, corner_b, kext, spread
+        mixing, state, first, partial, early, recv_a, recv_b, sides, halo, corner_a, corner_b, kext, spread
     )
 
     gram = all_sum(gram, sizes)

time: 31.5 us -> 30.1 us (0.956)
  Pallas kernels: 14.1 us -> 11.7 us
  starting transfers between devices: 11.7 us -> 12.5 us
    pallas_call x1, Pallas kernels: 3.47 us -> 2.42 us  [local(): pl.pallas_call(functools.partial(edge_kernel, dims, factor), name='edge',...]
    ppermute x12, starting transfers between devices: 11.7 us -> 12.5 us  [pair_swap(): return lambda value: lax.ppermute(value, ('grp', 'gx', 'gy'), pairs)]
    pallas_call x1, Pallas kernels: 3.15 us -> 2.4 us  [local(): pl.pallas_call(functools.partial(inner_kernel, dims, factor), name='inner...]
    pallas_call x1, Pallas kernels: 2.15 us -> 1.75 us  [local(): pl.pallas_call(functools.partial(middle_kernel, dims), name='middle', in_...]
  transfers between devices with their start and end apart: 12 -> 12, of which waited for: 6 -> 5; matrix products, arithmetic and copies ran while one was open for 0% -> 0% of each run, Pallas kernels for 17% -> 14%
where the time goes in v4:
time: 30.1 us; the launch traced here: 29.9 us
  starting transfers between devices  12.5 us (42%)
  Pallas kernels  11.7 us (39%)
  waiting for transfers between devices  5.6 us (19%)
    ppermute x12, starting transfers between devices, pair_swap(): return lambda value: lax.ppermute(value, ('grp', 'gx', 'gy'), pairs)  12.5 us
    ppermute x12, waiting for transfers between devices, pair_swap(): return lambda value: lax.ppermute(value, ('grp', 'gx', 'gy'), pairs)  5.6 us
    pallas_call x1, Pallas kernels, local(): pl.pallas_call(functools.partial(apply_kernel, dims), name='apply', in_sp...  3.12 us
    pallas_call x1, Pallas kernels, local(): pl.pallas_call(functools.partial(edge_kernel, dims, factor), name='edge',...  2.42 us
    pallas_call x1, Pallas kernels, local(): pl.pallas_call(functools.partial(inner_kernel, dims, factor), name='inner...  2.4 us
    pallas_call x1, Pallas kernels, local(): pl.pallas_call(functools.partial(load_kernel, dims), name='load', in_spec...  2.01 us
    pallas_call x1, Pallas kernels, local(): pl.pallas_call(functools.partial(middle_kernel, dims), name='middle', in_...  1.75 us
  transfers between devices with their start and end apart: 12, of which 5 were waited for; matrix products, arithmetic and copies ran while one was open for 0% of the time, Pallas kernels for 14%

profile of v4, /device:TPU:0, one launch (start us, length us, event | category | flops | bytes accessed | tf_op | source)
XLA Modules:
  0.0 29.9 jit_solution(10931620227881952987)
XLA Ops:
  0.0 2.0 %load.1 = (f32[2304,256]{1,0:T(8,128)S(1)}, f32[392,256]{1,0:T(8,128)S(1)}, f32[72,128]{1,0:T(8,128)S(1)}, f32[72,128]{1,0:T(8,128)S(1)}, f32[72,128]{1,0:T(8,12...) custom-call(f32[1536,256]{1,0:T(8,128)} %bitcast.5, ...), custom_call_target="tpu_custom_call" | custom-call | tf_op jit(solution)/shard_map/load/pallas_call | solution.py:534
  2.0 3.1 %collective-permute-start = (f32[72,128]{1,0:T(8,128)S(1)}, f32[72,128]{1,0:T(8,128)S(1)}, u32[]{:S(2)}, u32[]{:S(2)}) collective-permute-start(f32[72,128]{1,0:T(8,128)S(1)} %get-tuple-element.34), channel_id=1, source_target_pairs={{0,1},{1,0},{2,3},{3,2},{4,5},{5,4},{6,7},{7,6},{8,9},{9,8},{10,11... | collective-permute-start | bytes 110600 | tf_op jit(solution)/shard_map/ppermute | solution.py:51
  5.1 0.0 collective-permute-start.1
  5.1 1.5 %collective-permute-start.3 = (f32[392,256]{1,0:T(8,128)S(1)}, f32[392,256]{1,0:T(8,128)S(1)}, u32[]{:S(2)}, u32[]{:S(2)}) collective-permute-start(f32[392,256]{1,0:T(8,128)S(1)} %get-tuple-element.53), channel_id=1, source_target_pairs={{0,16},{1,17},{2,18},{3,19},{4,8},{5,9},{6,10},{7,11},{8,4},{9,5},... | collective-permute-start | bytes 1204232 | tf_op jit(solution)/shard_map/ppermute | solution.py:51
  6.6 1.8 %middle.1 = (f32[1920,256]{1,0:T(8,128)S(1)}, f32[80,256]{1,0:T(8,128)S(1)}, f32[64,256]{1,0:T(8,128)S(1)}, f32[392,256]{1,0:T(8,128)S(1)}) custom-call(f32[3,3]{1,0:T(4,128)S(1)} %get-tuple-element.32.mixing, f32[2304,256]{1,0:T(8,128)S(1)} %get-tuple-element.33.state.state_in, f32[3,8,256]{2,1,0:T(8,128)S(1)} %get-tuple-element.36.kappa, ...), custom_call_target="tpu_custom_call" | custom-call | tf_op jit(solution)/shard_map/middle/pallas_call | solution.py:557
  8.4 0.0 collective-permute-done
  8.4 0.0 collective-permute-done.1
  8.4 0.2 collective-permute-start.2
  8.6 1.5 %collective-permute-start.5 = (f32[72,128]{1,0:T(8,128)S(1)}, f32[72,128]{1,0:T(8,128)S(1)}, u32[]{:S(2)}, u32[]{:S(2)}) collective-permute-start(f32[72,128]{1,0:T(8,128)S(1)} %add.21.halo), channel_id=1, source_target_pairs={{0,16},{1,17},{2,18},{3,19},{4,8},{5,9},{6,10},{7,11},{8,4},{9,5},... | collective-permute-start | bytes 110600 | tf_op jit(solution)/shard_map/ppermute | solution.py:51
  10.1 0.2 collective-permute-start.4
  10.3 2.4 %inner.1 = (f32[1920,256]{1,0:T(8,128)S(1)}, bf16[128,3072]{1,0:T(8,128)(2,1)S(1)}, f32[32,256]{1,0:T(8,128)S(1)}, f32[160,128]{1,0:T(8,128)S(1)}, f32[384,256]{1,0:T(8,128)S(1)}) custom-call(f32[3,3]{1,0:T(4,128)S(1)} %get-tuple-element.32.mixing, f32[1920,256]{1,0:T(8,128)S(1)} %get-tuple-element.43.first_in, ...), custom_call_target="tpu_custom_call", output_to_operand_aliasing={{0}: (1, {})} | custom-call | tf_op jit(solution)/shard_map/inner/pallas_call | solution.py:578
  12.7 0.6 %collective-permute-done.5.corner_b = f32[72,128]{1,0:T(8,128)S(1)} collective-permute-done((f32[72,128]{1,0:T(8,128)S(1)}, f32[72,128]{1,0:T(8,128)S(1)}, u32[]{:S(2)}, u32[]{:S(2)}) %collective-permute-start.5) | collective-permute-done | bytes 36896 | tf_op jit(solution)/shard_map/ppermute | solution.py:51
  13.4 0.0 collective-permute-done.4.corner_a
  13.4 0.0 collective-permute-done.3.recv_b
  13.4 0.0 collective-permute-done.2.recv_a
  13.4 2.4 %edge.1 = (f32[2304,256]{1,0:T(8,128)S(1)}, f32[1920,256]{1,0:T(8,128)S(1)}, bf16[128,3072]{1,0:T(8,128)(2,1)S(1)}, f32[32,256]{1,0:T(8,128)S(1)}, f32[40,128]{1,0:T(8,128)S(1)}) custom-call(f32[3,3]{1,0:T(4,128)S(1)} %get-tuple-element.32.mixing, f32[2304,256]{1,0:T(8,128)S(1)} %get-tuple-element.33.state.state_in, ...), custom_call_target="tpu_custom_call", output_to_operand_aliasing={{0}: (1, {}), {1}: (2, {})} | custom-call | tf_op jit(solution)/shard_map/edge/pallas_call | solution.py:600
  15.8 0.1 collective-permute-start.6
  15.9 1.1 %collective-permute-done.6 = f32[40,128]{1,0:T(8,128)S(1)} collective-permute-done((f32[40,128]{1,0:T(8,128)S(1)}, f32[40,128]{1,0:T(8,128)S(1)}, u32[]{:S(2)}, u32[]{:S(2)}) %collective-permute-start.6) | collective-permute-done | bytes 20512 | tf_op jit(solution)/shard_map/ppermute | solution.py:51
  17.0 2.5 %collective-permute-start.10 = (f32[40,128]{1,0:T(8,128)S(1)}, f32[40,128]{1,0:T(8,128)S(1)}, u32[]{:S(2)}, u32[]{:S(2)}) collective-permute-start(f32[40,128]{1,0:T(8,128)S(1)} %add.22), channel_id=1, source_target_pairs={{0,3},{1,2},{2,1},{3,0},{4,15},{5,14},{6,13},{7,12},{8,11},{9,10},... | collective-permute-start | bytes 61448 | tf_op jit(solution)/shard_map/ppermute | solution.py:51
  19.5 2.1 %collective-permute-start.9 = (f32[40,128]{1,0:T(8,128)S(1)}, f32[40,128]{1,0:T(8,128)S(1)}, u32[]{:S(2)}, u32[]{:S(2)}) collective-permute-start(f32[40,128]{1,0:T(8,128)S(1)} %add.22), channel_id=1, source_target_pairs={{0,2},{1,3},{2,0},{3,1},{4,14},{5,15},{6,12},{7,13},{8,10},{9,11},... | collective-permute-start | bytes 61448 | tf_op jit(solution)/shard_map/ppermute | solution.py:51
  21.6 0.0 collective-permute-start.8
  21.6 0.9 %collective-permute-start.7 = (f32[40,128]{1,0:T(8,128)S(1)}, f32[40,128]{1,0:T(8,128)S(1)}, u32[]{:S(2)}, u32[]{:S(2)}) collective-permute-start(f32[40,128]{1,0:T(8,128)S(1)} %add.22), channel_id=1, source_target_pairs={{0,8},{1,9},{2,10},{3,11},{4,12},{5,13},{6,14},{7,15},{8,0},{9,1},... | collective-permute-start | bytes 61448 | tf_op jit(solution)/shard_map/ppermute | solution.py:51
  22.6 0.0 collective-permute-done.10
  22.6 2.0 %collective-permute-done.9 = f32[40,128]{1,0:T(8,128)S(1)} collective-permute-done((f32[40,128]{1,0:T(8,128)S(1)}, f32[40,128]{1,0:T(8,128)S(1)}, u32[]{:S(2)}, u32[]{:S(2)}) %collective-permute-start.9) | collective-permute-done | bytes 20512 | tf_op jit(solution)/shard_map/ppermute | solution.py:51
  24.7 0.9 %collective-permute-done.8 = f32[40,128]{1,0:T(8,128)S(1)} collective-permute-done((f32[40,128]{1,0:T(8,128)S(1)}, f32[40,128]{1,0:T(8,128)S(1)}, u32[]{:S(2)}, u32[]{:S(2)}) %collective-permute-start.8) | collective-permute-done | bytes 20512 | tf_op jit(solution)/shard_map/ppermute | solution.py:51
  25.5 0.0 collective-permute-done.7
  25.5 0.4 %collective-permute-start.11 = (f32[40,128]{1,0:T(8,128)S(1)}, f32[40,128]{1,0:T(8,128)S(1)}, u32[]{:S(2)}, u32[]{:S(2)}) collective-permute-start(f32[40,128]{1,0:T(8,128)S(1)} %add_add_fusion), channel_id=1, source_target_pairs={{0,4},{1,5},{2,6},{3,7},{4,0},{5,1},{6,2},{7,3},{8,12},{9,13},{10,... | collective-permute-start | bytes 61448 | tf_op jit(solution)/shard_map/ppermute | solution.py:51
  25.9 0.9 %collective-permute-done.11 = f32[40,128]{1,0:T(8,128)S(1)} collective-permute-done((f32[40,128]{1,0:T(8,128)S(1)}, f32[40,128]{1,0:T(8,128)S(1)}, u32[]{:S(2)}, u32[]{:S(2)}) %collective-permute-start.11) | collective-permute-done | bytes 20512 | tf_op jit(solution)/shard_map/ppermute | solution.py:51
  26.8 3.1 %apply.1 = f32[64,3,8,256]{3,2,1,0:T(8,128)} custom-call(f32[40,128]{1,0:T(8,128)S(1)} %add.27.gram, bf16[128,3072]{1,0:T(8,128)(2,1)S(1)} %get-tuple-element.55.inner, f32[32,256]{1,0:T(8,128)S(1)} %get-tuple-element.56.inner_means, bf16[128,3072]{1,0:T(8,128)(2,1)S(1)} %get-tuple-element.57.edge, f32[32,256]{1,0:T(8,128)S(1)} %get-tuple-element.58.edge_means), custom_call_target="tpu_custom_call" | custom-call | tf_op jit(solution)/shard_map/apply/pallas_call | solution.py:627
  (4 shorter events, 0.0 us)
Async XLA Ops:
  2.0 6.4 %collective-permute-start = (f32[72,128]{1,0:T(8,128)S(1)}, f32[72,128]{1,0:T(8,128)S(1)}, u32[]{:S(2)}, u32[]{:S(2)}) collective-permute-start(f32[72,128]{1,0:T(8,128)S(1)} %get-tuple-element.34), channel_id=1, source_target_pairs={{0,1},{1,0},{2,3},{3,2},{4,5},{5,4},{6,7},{7,6},{8,9},{9,8},{10,11... | collective-permute-start | bytes 110600 | tf_op jit(solution)/shard_map/ppermute | solution.py:51
  5.1 3.3 %collective-permute-start.1 = (f32[72,128]{1,0:T(8,128)S(1)}, f32[72,128]{1,0:T(8,128)S(1)}, u32[]{:S(2)}, u32[]{:S(2)}) collective-permute-start(f32[72,128]{1,0:T(8,128)S(1)} %get-tuple-element.35), channel_id=1, source_target_pairs={{0,4},{1,2},{2,1},{3,7},{4,0},{5,6},{6,5},{7,3},{8,12},{9,10},{10,... | collective-permute-start | bytes 110600 | tf_op jit(solution)/shard_map/ppermute | solution.py:51
  5.1 8.3 %collective-permute-start.3 = (f32[392,256]{1,0:T(8,128)S(1)}, f32[392,256]{1,0:T(8,128)S(1)}, u32[]{:S(2)}, u32[]{:S(2)}) collective-permute-start(f32[392,256]{1,0:T(8,128)S(1)} %get-tuple-element.53), channel_id=1, source_target_pairs={{0,16},{1,17},{2,18},{3,19},{4,8},{5,9},{6,10},{7,11},{8,4},{9,5},... | collective-permute-start | bytes 1204232 | tf_op jit(solution)/shard_map/ppermute | solution.py:51
  8.4 5.0 %collective-permute-start.2 = (f32[392,256]{1,0:T(8,128)S(1)}, f32[392,256]{1,0:T(8,128)S(1)}, u32[]{:S(2)}, u32[]{:S(2)}) collective-permute-start(f32[392,256]{1,0:T(8,128)S(1)} %get-tuple-element.52), channel_id=1, source_target_pairs={{0,4},{1,5},{2,6},{3,7},{4,0},{5,1},{6,2},{7,3},{8,12},{9,13},{10,... | collective-permute-start | bytes 1204232 | tf_op jit(solution)/shard_map/ppermute | solution.py:51
  8.6 4.8 %collective-permute-start.5 = (f32[72,128]{1,0:T(8,128)S(1)}, f32[72,128]{1,0:T(8,128)S(1)}, u32[]{:S(2)}, u32[]{:S(2)}) collective-permute-start(f32[72,128]{1,0:T(8,128)S(1)} %add.21.halo), channel_id=1, source_target_pairs={{0,16},{1,17},{2,18},{3,19},{4,8},{5,9},{6,10},{7,11},{8,4},{9,5},... | collective-permute-start | bytes 110600 | tf_op jit(solution)/shard_map/ppermute | solution.py:51
  10.1 3.3 %collective-permute-start.4 = (f32[72,128]{1,0:T(8,128)S(1)}, f32[72,128]{1,0:T(8,128)S(1)}, u32[]{:S(2)}, u32[]{:S(2)}) collective-permute-start(f32[72,128]{1,0:T(8,128)S(1)} %add.21.halo), channel_id=1, source_target_pairs={{0,4},{1,5},{2,6},{3,7},{4,0},{5,1},{6,2},{7,3},{8,12},{9,13},{10,... | collective-permute-start | bytes 110600 | tf_op jit(solution)/shard_map/ppermute | solution.py:51
  15.8 1.2 %collective-permute-start.6 = (f32[40,128]{1,0:T(8,128)S(1)}, f32[40,128]{1,0:T(8,128)S(1)}, u32[]{:S(2)}, u32[]{:S(2)}) collective-permute-start(f32[40,128]{1,0:T(8,128)S(1)} %get-tuple-element.54), channel_id=1, source_target_pairs={{0,4},{1,5},{2,6},{3,7},{4,0},{5,1},{6,2},{7,3},{8,12},{9,13},{10,... | collective-permute-start | bytes 61448 | tf_op jit(solution)/shard_map/ppermute | solution.py:51
  17.0 5.6 %collective-permute-start.10 = (f32[40,128]{1,0:T(8,128)S(1)}, f32[40,128]{1,0:T(8,128)S(1)}, u32[]{:S(2)}, u32[]{:S(2)}) collective-permute-start(f32[40,128]{1,0:T(8,128)S(1)} %add.22), channel_id=1, source_target_pairs={{0,3},{1,2},{2,1},{3,0},{4,15},{5,14},{6,13},{7,12},{8,11},{9,10},... | collective-permute-start | bytes 61448 | tf_op jit(solution)/shard_map/ppermute | solution.py:51
  19.5 5.2 %collective-permute-start.9 = (f32[40,128]{1,0:T(8,128)S(1)}, f32[40,128]{1,0:T(8,128)S(1)}, u32[]{:S(2)}, u32[]{:S(2)}) collective-permute-start(f32[40,128]{1,0:T(8,128)S(1)} %add.22), channel_id=1, source_target_pairs={{0,2},{1,3},{2,0},{3,1},{4,14},{5,15},{6,12},{7,13},{8,10},{9,11},... | collective-permute-start | bytes 61448 | tf_op jit(solution)/shard_map/ppermute | solution.py:51
  21.6 3.9 %collective-permute-start.8 = (f32[40,128]{1,0:T(8,128)S(1)}, f32[40,128]{1,0:T(8,128)S(1)}, u32[]{:S(2)}, u32[]{:S(2)}) collective-permute-start(f32[40,128]{1,0:T(8,128)S(1)} %add.22), channel_id=1, source_target_pairs={{0,1},{1,0},{2,3},{3,2},{4,13},{5,12},{6,15},{7,14},{8,9},{9,8},{1... | collective-permute-start | bytes 61448 | tf_op jit(solution)/shard_map/ppermute | solution.py:51
  21.6 3.9 %collective-permute-start.7 = (f32[40,128]{1,0:T(8,128)S(1)}, f32[40,128]{1,0:T(8,128)S(1)}, u32[]{:S(2)}, u32[]{:S(2)}) collective-permute-start(f32[40,128]{1,0:T(8,128)S(1)} %add.22), channel_id=1, source_target_pairs={{0,8},{1,9},{2,10},{3,11},{4,12},{5,13},{6,14},{7,15},{8,0},{9,1},... | collective-permute-start | bytes 61448 | tf_op jit(solution)/shard_map/ppermute | solution.py:51
  25.5 1.3 %collective-permute-start.11 = (f32[40,128]{1,0:T(8,128)S(1)}, f32[40,128]{1,0:T(8,128)S(1)}, u32[]{:S(2)}, u32[]{:S(2)}) collective-permute-start(f32[40,128]{1,0:T(8,128)S(1)} %add_add_fusion), channel_id=1, source_target_pairs={{0,4},{1,5},{2,6},{3,7},{4,0},{5,1},{6,2},{7,3},{8,12},{9,13},{10,... | collective-permute-start | bytes 61448 | tf_op jit(solution)/shard_map/ppermute | solution.py:51

commit v5 on v4

--- a/solution.py
+++ b/solution.py
@@ -121,8 +121,8 @@
 
 
 def load_kernel(dims, ens, *refs):
-    small_in, (state, send_b, sides, side_a, side_b) = refs[:6], refs[6:11]
-    small, (buf, sems, small_sems) = refs[11:17], refs[17:]
+    small_in, (state, send_a, send_b, sides, side_a, side_b) = refs[:6], refs[6:12]
+    small, (buf, sems, small_sems) = refs[12:18], refs[18:]
     kappa = small[0]
     k, nv, cx, cy = dims
     rows = nv * cx
@@ -175,7 +175,9 @@
         put_sides(pl.ds(c * part, part), total)
     for copy in small_copies:
         copy.wait()
-    send_rows(dims, state, kappa, send_b, lax.axis_index("gx") % 2 == 0)
+    even_x = lax.axis_index("gx") % 2 == 0
+    send_rows(dims, state, kappa, send_a, jnp.logical_not(even_x))
+    send_rows(dims, state, kappa, send_b, even_x)
     total = jnp.zeros((8, LANES), F32)
     for r in range(cx):
         for v in range(nv):
@@ -355,9 +357,8 @@
             kext[pl.ds((r + 1) * 8 + v, 1), :] = kappa[v, r : r + 1, :]
 
 
-def middle_kernel(dims, mixing, state, kappa, cell, var, value, weight, first, kext, spread, send_a, cells):
-    k, nv, cx, cy = dims
-    send_rows(dims, state, kappa, send_a, lax.axis_index("gx") % 2 == 1)
+def middle_kernel(dims, mixing, state, kappa, cell, var, value, weight, first, kext, spread, cells):
+    k, nv, cx, cy = dims
     scatter_kernel(dims, cell, var, value, weight, cells)
     for v in range(nv):
         for r in range(cx):
@@ -531,13 +532,14 @@
         return jax.ShapeDtypeStruct(dims, dtype)
 
     small = (diffusivity, mixing) + tuple(a.reshape(1, count) for a in (obs_cell, obs_var, obs_value, obs_weight))
-    state, send_b, sides, side_a, side_b, kappa, mixing, *obs = pl.pallas_call(
+    state, send_a, send_b, sides, side_a, side_b, kappa, mixing, *obs = pl.pallas_call(
         functools.partial(load_kernel, dims),
         name="load",
         in_specs=[pl.BlockSpec(memory_space=pltpu.HBM)] * 7,
-        out_specs=[vmem()] * 11,
+        out_specs=[vmem()] * 12,
         out_shape=[
             shape((cx + 4) * block, cy),
+            shape(2 * block + 8, cy),
             shape(2 * block + 8, cy),
             shape(k + 8, LANES),
             shape(k + 8, LANES),
@@ -553,23 +555,18 @@
     recv_b = x_swap(1, sizes)(send_b)
     side_a = y_swap(0, sizes)(side_a)
     side_b = y_swap(1, sizes)(side_b)
-
-    first, kext, spread, send_a = pl.pallas_call(
+    recv_a = x_swap(0, sizes)(send_a)
+
+    first, kext, spread = pl.pallas_call(
         functools.partial(middle_kernel, dims),
         name="middle",
         in_specs=[smem()] + [vmem()] * 6,
-        out_specs=[vmem()] * 4,
-        out_shape=[
-            shape((cx + 2) * block, cy),
-            shape((cx + 2) * 8, cy),
-            shape(cx * 8, cy),
-            shape(2 * block + 8, cy),
-        ],
+        out_specs=[vmem()] * 3,
+        out_shape=[shape((cx + 2) * block, cy), shape((cx + 2) * 8, cy), shape(cx * 8, cy)],
         scratch_shapes=[pltpu.VMEM((64, cy), F32)],
         compiler_params=limits,
     )(mixing, state, kappa, *obs)
-    side_a, side_b, first, send_a = lax.optimization_barrier((side_a, side_b, first, send_a))
-    recv_a = x_swap(0, sizes)(send_a)
+    side_a, side_b, first = lax.optimization_barrier((side_a, side_b, first))
     halo = side_a + side_b
     corner_b = x_swap(1, sizes)(halo)
     corner_a = x_swap(0, sizes)(halo)

time: 30.1 us -> 29.9 us (level)
  starting transfers between devices: 12.5 us -> 10.6 us
  waiting for transfers between devices: 5.6 us -> 7.33 us
    ppermute x12, starting transfers between devices: 12.5 us -> 10.6 us  [pair_swap(): return lambda value: lax.ppermute(value, ('grp', 'gx', 'gy'), pairs)]
    ppermute x12, waiting for transfers between devices: 5.6 us -> 7.33 us  [pair_swap(): return lambda value: lax.ppermute(value, ('grp', 'gx', 'gy'), pairs)]
  transfers between devices with their start and end apart: 12 -> 12, of which waited for: 5 -> 7; matrix products, arithmetic and copies ran while one was open for 0% -> 0% of each run, Pallas kernels for 14% -> 14%
where the time goes in v5:
time: 29.9 us; the launch traced here: 29.7 us
  Pallas kernels  11.7 us (39%)
  starting transfers between devices  10.6 us (35%)
  waiting for transfers between devices  7.33 us (25%)
    ppermute x12, starting transfers between devices, pair_swap(): return lambda value: lax.ppermute(value, ('grp', 'gx', 'gy'), pairs)  10.6 us
    ppermute x12, waiting for transfers between devices, pair_swap(): return lambda value: lax.ppermute(value, ('grp', 'gx', 'gy'), pairs)  7.33 us
    pallas_call x1, Pallas kernels, local(): pl.pallas_call(functools.partial(apply_kernel, dims), name='apply', in_sp...  3.13 us
    pallas_call x1, Pallas kernels, local(): pl.pallas_call(functools.partial(edge_kernel, dims, factor), name='edge',...  2.42 us
    pallas_call x1, Pallas kernels, local(): pl.pallas_call(functools.partial(inner_kernel, dims, factor), name='inner...  2.4 us
    pallas_call x1, Pallas kernels, local(): pl.pallas_call(functools.partial(load_kernel, dims), name='load', in_spec...  2.03 us
    pallas_call x1, Pallas kernels, local(): pl.pallas_call(functools.partial(middle_kernel, dims), name='middle', in_...  1.75 us
  transfers between devices with their start and end apart: 12, of which 7 were waited for; matrix products, arithmetic and copies ran while one was open for 0% of the time, Pallas kernels for 14%

profile of v5, /device:TPU:0, one launch (start us, length us, event | category | flops | bytes accessed | tf_op | source)
XLA Modules:
  0.0 29.7 jit_solution(10992412578835698803)
XLA Ops:
  0.0 2.0 %load.1 = (f32[2304,256]{1,0:T(8,128)S(1)}, f32[392,256]{1,0:T(8,128)S(1)}, f32[392,256]{1,0:T(8,128)S(1)}, f32[72,128]{1,0:T(8,128)S(1)}, f32[72,128]{1,0:T(8,1...) custom-call(f32[1536,256]{1,0:T(8,128)} %bitcast.5, ...), custom_call_target="tpu_custom_call" | custom-call | tf_op jit(solution)/shard_map/load/pallas_call | solution.py:535
  2.0 0.5 %collective-permute-start.2 = (f32[392,256]{1,0:T(8,128)S(1)}, f32[392,256]{1,0:T(8,128)S(1)}, u32[]{:S(2)}, u32[]{:S(2)}) collective-permute-start(f32[392,256]{1,0:T(8,128)S(1)} %get-tuple-element.50), channel_id=1, source_target_pairs={{0,4},{1,5},{2,6},{3,7},{4,0},{5,1},{6,2},{7,3},{8,12},{9,13},{10,... | collective-permute-start | bytes 1204232 | tf_op jit(solution)/shard_map/ppermute | solution.py:51
  2.6 2.6 %collective-permute-start.3 = (f32[392,256]{1,0:T(8,128)S(1)}, f32[392,256]{1,0:T(8,128)S(1)}, u32[]{:S(2)}, u32[]{:S(2)}) collective-permute-start(f32[392,256]{1,0:T(8,128)S(1)} %get-tuple-element.51), channel_id=1, source_target_pairs={{0,16},{1,17},{2,18},{3,19},{4,8},{5,9},{6,10},{7,11},{8,4},{9,5},... | collective-permute-start | bytes 1204232 | tf_op jit(solution)/shard_map/ppermute | solution.py:51
  5.1 1.6 %collective-permute-start = (f32[72,128]{1,0:T(8,128)S(1)}, f32[72,128]{1,0:T(8,128)S(1)}, u32[]{:S(2)}, u32[]{:S(2)}) collective-permute-start(f32[72,128]{1,0:T(8,128)S(1)} %get-tuple-element.33), channel_id=1, source_target_pairs={{0,1},{1,0},{2,3},{3,2},{4,5},{5,4},{6,7},{7,6},{8,9},{9,8},{10,11... | collective-permute-start | bytes 110600 | tf_op jit(solution)/shard_map/ppermute | solution.py:51
  6.7 0.0 collective-permute-start.1
  6.7 1.7 %middle.1 = (f32[1920,256]{1,0:T(8,128)S(1)}, f32[80,256]{1,0:T(8,128)S(1)}, f32[64,256]{1,0:T(8,128)S(1)}) custom-call(f32[3,3]{1,0:T(4,128)S(1)} %get-tuple-element.31.mixing, f32[2304,256]{1,0:T(8,128)S(1)} %get-tuple-element.32.state.state_in, f32[3,8,256]{2,1,0:T(8,128)S(1)} %get-tuple-element.35.kappa, s32[1,2048]{1,0:T(1,128)S(1)} %get-tuple-element.36.cell, ...), custom_call_target="tpu_custom_call" | custom-call | tf_op jit(solution)/shard_map/middle/pallas_call | solution.py:560
  8.5 0.6 %collective-permute-done = f32[72,128]{1,0:T(8,128)S(1)} collective-permute-done((f32[72,128]{1,0:T(8,128)S(1)}, f32[72,128]{1,0:T(8,128)S(1)}, u32[]{:S(2)}, u32[]{:S(2)}) %collective-permute-start) | collective-permute-done | bytes 36896 | tf_op jit(solution)/shard_map/ppermute | solution.py:51
  9.1 0.0 collective-permute-done.1
  9.1 0.8 %collective-permute-start.5 = (f32[72,128]{1,0:T(8,128)S(1)}, f32[72,128]{1,0:T(8,128)S(1)}, u32[]{:S(2)}, u32[]{:S(2)}) collective-permute-start(f32[72,128]{1,0:T(8,128)S(1)} %add.21.halo), channel_id=1, source_target_pairs={{0,16},{1,17},{2,18},{3,19},{4,8},{5,9},{6,10},{7,11},{8,4},{9,5},... | collective-permute-start | bytes 110600 | tf_op jit(solution)/shard_map/ppermute | solution.py:51
  9.9 0.2 collective-permute-start.4
  10.1 2.4 %inner.1 = (f32[1920,256]{1,0:T(8,128)S(1)}, bf16[128,3072]{1,0:T(8,128)(2,1)S(1)}, f32[32,256]{1,0:T(8,128)S(1)}, f32[160,128]{1,0:T(8,128)S(1)}, f32[384,256]{1,0:T(8,128)S(1)}) custom-call(f32[3,3]{1,0:T(4,128)S(1)} %get-tuple-element.31.mixing, f32[1920,256]{1,0:T(8,128)S(1)} %get-tuple-element.41.first_in, ...), custom_call_target="tpu_custom_call", output_to_operand_aliasing={{0}: (1, {})} | custom-call | tf_op jit(solution)/shard_map/inner/pallas_call | solution.py:575
  12.5 0.7 %collective-permute-done.5.corner_b = f32[72,128]{1,0:T(8,128)S(1)} collective-permute-done((f32[72,128]{1,0:T(8,128)S(1)}, f32[72,128]{1,0:T(8,128)S(1)}, u32[]{:S(2)}, u32[]{:S(2)}) %collective-permute-start.5) | collective-permute-done | bytes 36896 | tf_op jit(solution)/shard_map/ppermute | solution.py:51
  13.1 0.0 collective-permute-done.4.corner_a
  13.1 0.0 collective-permute-done.2.recv_a
  13.2 0.0 collective-permute-done.3.recv_b
  13.2 2.4 %edge.1 = (f32[2304,256]{1,0:T(8,128)S(1)}, f32[1920,256]{1,0:T(8,128)S(1)}, bf16[128,3072]{1,0:T(8,128)(2,1)S(1)}, f32[32,256]{1,0:T(8,128)S(1)}, f32[40,128]{1,0:T(8,128)S(1)}) custom-call(f32[3,3]{1,0:T(4,128)S(1)} %get-tuple-element.31.mixing, f32[2304,256]{1,0:T(8,128)S(1)} %get-tuple-element.32.state.state_in, ...), custom_call_target="tpu_custom_call", output_to_operand_aliasing={{0}: (1, {}), {1}: (2, {})} | custom-call | tf_op jit(solution)/shard_map/edge/pallas_call | solution.py:597
  15.6 0.0 collective-permute-start.6
  15.6 1.2 %collective-permute-done.6 = f32[40,128]{1,0:T(8,128)S(1)} collective-permute-done((f32[40,128]{1,0:T(8,128)S(1)}, f32[40,128]{1,0:T(8,128)S(1)}, u32[]{:S(2)}, u32[]{:S(2)}) %collective-permute-start.6) | collective-permute-done | bytes 20512 | tf_op jit(solution)/shard_map/ppermute | solution.py:51
  16.8 3.6 %collective-permute-start.10 = (f32[40,128]{1,0:T(8,128)S(1)}, f32[40,128]{1,0:T(8,128)S(1)}, u32[]{:S(2)}, u32[]{:S(2)}) collective-permute-start(f32[40,128]{1,0:T(8,128)S(1)} %add.22), channel_id=1, source_target_pairs={{0,3},{1,2},{2,1},{3,0},{4,15},{5,14},{6,13},{7,12},{8,11},{9,10},... | collective-permute-start | bytes 61448 | tf_op jit(solution)/shard_map/ppermute | solution.py:51
  20.4 0.6 %collective-permute-start.9 = (f32[40,128]{1,0:T(8,128)S(1)}, f32[40,128]{1,0:T(8,128)S(1)}, u32[]{:S(2)}, u32[]{:S(2)}) collective-permute-start(f32[40,128]{1,0:T(8,128)S(1)} %add.22), channel_id=1, source_target_pairs={{0,2},{1,3},{2,0},{3,1},{4,14},{5,15},{6,12},{7,13},{8,10},{9,11},... | collective-permute-start | bytes 61448 | tf_op jit(solution)/shard_map/ppermute | solution.py:51
  21.0 0.5 %collective-permute-start.8 = (f32[40,128]{1,0:T(8,128)S(1)}, f32[40,128]{1,0:T(8,128)S(1)}, u32[]{:S(2)}, u32[]{:S(2)}) collective-permute-start(f32[40,128]{1,0:T(8,128)S(1)} %add.22), channel_id=1, source_target_pairs={{0,1},{1,0},{2,3},{3,2},{4,13},{5,12},{6,15},{7,14},{8,9},{9,8},{1... | collective-permute-start | bytes 61448 | tf_op jit(solution)/shard_map/ppermute | solution.py:51
  21.5 0.2 collective-permute-start.7
  21.7 0.7 %collective-permute-done.10 = f32[40,128]{1,0:T(8,128)S(1)} collective-permute-done((f32[40,128]{1,0:T(8,128)S(1)}, f32[40,128]{1,0:T(8,128)S(1)}, u32[]{:S(2)}, u32[]{:S(2)}) %collective-permute-start.10) | collective-permute-done | bytes 20512 | tf_op jit(solution)/shard_map/ppermute | solution.py:51
  22.4 2.8 %collective-permute-done.9 = f32[40,128]{1,0:T(8,128)S(1)} collective-permute-done((f32[40,128]{1,0:T(8,128)S(1)}, f32[40,128]{1,0:T(8,128)S(1)}, u32[]{:S(2)}, u32[]{:S(2)}) %collective-permute-start.9) | collective-permute-done | bytes 20512 | tf_op jit(solution)/shard_map/ppermute | solution.py:51
  25.2 0.0 collective-permute-done.8
  25.2 0.1 collective-permute-done.7
  25.3 0.1 collective-permute-start.11
  25.4 1.2 %collective-permute-done.11 = f32[40,128]{1,0:T(8,128)S(1)} collective-permute-done((f32[40,128]{1,0:T(8,128)S(1)}, f32[40,128]{1,0:T(8,128)S(1)}, u32[]{:S(2)}, u32[]{:S(2)}) %collective-permute-start.11) | collective-permute-done | bytes 20512 | tf_op jit(solution)/shard_map/ppermute | solution.py:51
  26.6 3.1 %apply.1 = f32[64,3,8,256]{3,2,1,0:T(8,128)} custom-call(f32[40,128]{1,0:T(8,128)S(1)} %add.27.gram, bf16[128,3072]{1,0:T(8,128)(2,1)S(1)} %get-tuple-element.53.inner, f32[32,256]{1,0:T(8,128)S(1)} %get-tuple-element.54.inner_means, bf16[128,3072]{1,0:T(8,128)(2,1)S(1)} %get-tuple-element.55.edge, f32[32,256]{1,0:T(8,128)S(1)} %get-tuple-element.56.edge_means), custom_call_target="tpu_custom_call" | custom-call | tf_op jit(solution)/shard_map/apply/pallas_call | solution.py:624
  (4 shorter events, 0.0 us)
Async XLA Ops:
  2.0 11.1 %collective-permute-start.2 = (f32[392,256]{1,0:T(8,128)S(1)}, f32[392,256]{1,0:T(8,128)S(1)}, u32[]{:S(2)}, u32[]{:S(2)}) collective-permute-start(f32[392,256]{1,0:T(8,128)S(1)} %get-tuple-element.50), channel_id=1, source_target_pairs={{0,4},{1,5},{2,6},{3,7},{4,0},{5,1},{6,2},{7,3},{8,12},{9,13},{10,... | collective-permute-start | bytes 1204232 | tf_op jit(solution)/shard_map/ppermute | solution.py:51
  2.6 10.6 %collective-permute-start.3 = (f32[392,256]{1,0:T(8,128)S(1)}, f32[392,256]{1,0:T(8,128)S(1)}, u32[]{:S(2)}, u32[]{:S(2)}) collective-permute-start(f32[392,256]{1,0:T(8,128)S(1)} %get-tuple-element.51), channel_id=1, source_target_pairs={{0,16},{1,17},{2,18},{3,19},{4,8},{5,9},{6,10},{7,11},{8,4},{9,5},... | collective-permute-start | bytes 1204232 | tf_op jit(solution)/shard_map/ppermute | solution.py:51
  5.1 4.0 %collective-permute-start = (f32[72,128]{1,0:T(8,128)S(1)}, f32[72,128]{1,0:T(8,128)S(1)}, u32[]{:S(2)}, u32[]{:S(2)}) collective-permute-start(f32[72,128]{1,0:T(8,128)S(1)} %get-tuple-element.33), channel_id=1, source_target_pairs={{0,1},{1,0},{2,3},{3,2},{4,5},{5,4},{6,7},{7,6},{8,9},{9,8},{10,11... | collective-permute-start | bytes 110600 | tf_op jit(solution)/shard_map/ppermute | solution.py:51
  6.7 2.4 %collective-permute-start.1 = (f32[72,128]{1,0:T(8,128)S(1)}, f32[72,128]{1,0:T(8,128)S(1)}, u32[]{:S(2)}, u32[]{:S(2)}) collective-permute-start(f32[72,128]{1,0:T(8,128)S(1)} %get-tuple-element.34), channel_id=1, source_target_pairs={{0,4},{1,2},{2,1},{3,7},{4,0},{5,6},{6,5},{7,3},{8,12},{9,10},{10,... | collective-permute-start | bytes 110600 | tf_op jit(solution)/shard_map/ppermute | solution.py:51
  9.1 4.0 %collective-permute-start.5 = (f32[72,128]{1,0:T(8,128)S(1)}, f32[72,128]{1,0:T(8,128)S(1)}, u32[]{:S(2)}, u32[]{:S(2)}) collective-permute-start(f32[72,128]{1,0:T(8,128)S(1)} %add.21.halo), channel_id=1, source_target_pairs={{0,16},{1,17},{2,18},{3,19},{4,8},{5,9},{6,10},{7,11},{8,4},{9,5},... | collective-permute-start | bytes 110600 | tf_op jit(solution)/shard_map/ppermute | solution.py:51
  9.9 3.2 %collective-permute-start.4 = (f32[72,128]{1,0:T(8,128)S(1)}, f32[72,128]{1,0:T(8,128)S(1)}, u32[]{:S(2)}, u32[]{:S(2)}) collective-permute-start(f32[72,128]{1,0:T(8,128)S(1)} %add.21.halo), channel_id=1, source_target_pairs={{0,4},{1,5},{2,6},{3,7},{4,0},{5,1},{6,2},{7,3},{8,12},{9,13},{10,... | collective-permute-start | bytes 110600 | tf_op jit(solution)/shard_map/ppermute | solution.py:51
  15.6 1.2 %collective-permute-start.6 = (f32[40,128]{1,0:T(8,128)S(1)}, f32[40,128]{1,0:T(8,128)S(1)}, u32[]{:S(2)}, u32[]{:S(2)}) collective-permute-start(f32[40,128]{1,0:T(8,128)S(1)} %get-tuple-element.52), channel_id=1, source_target_pairs={{0,4},{1,5},{2,6},{3,7},{4,0},{5,1},{6,2},{7,3},{8,12},{9,13},{10,... | collective-permute-start | bytes 61448 | tf_op jit(solution)/shard_map/ppermute | solution.py:51
  16.8 5.6 %collective-permute-start.10 = (f32[40,128]{1,0:T(8,128)S(1)}, f32[40,128]{1,0:T(8,128)S(1)}, u32[]{:S(2)}, u32[]{:S(2)}) collective-permute-start(f32[40,128]{1,0:T(8,128)S(1)} %add.22), channel_id=1, source_target_pairs={{0,3},{1,2},{2,1},{3,0},{4,15},{5,14},{6,13},{7,12},{8,11},{9,10},... | collective-permute-start | bytes 61448 | tf_op jit(solution)/shard_map/ppermute | solution.py:51
  20.4 4.8 %collective-permute-start.9 = (f32[40,128]{1,0:T(8,128)S(1)}, f32[40,128]{1,0:T(8,128)S(1)}, u32[]{:S(2)}, u32[]{:S(2)}) collective-permute-start(f32[40,128]{1,0:T(8,128)S(1)} %add.22), channel_id=1, source_target_pairs={{0,2},{1,3},{2,0},{3,1},{4,14},{5,15},{6,12},{7,13},{8,10},{9,11},... | collective-permute-start | bytes 61448 | tf_op jit(solution)/shard_map/ppermute | solution.py:51
  21.0 4.2 %collective-permute-start.8 = (f32[40,128]{1,0:T(8,128)S(1)}, f32[40,128]{1,0:T(8,128)S(1)}, u32[]{:S(2)}, u32[]{:S(2)}) collective-permute-start(f32[40,128]{1,0:T(8,128)S(1)} %add.22), channel_id=1, source_target_pairs={{0,1},{1,0},{2,3},{3,2},{4,13},{5,12},{6,15},{7,14},{8,9},{9,8},{1... | collective-permute-start | bytes 61448 | tf_op jit(solution)/shard_map/ppermute | solution.py:51
  21.5 3.9 %collective-permute-start.7 = (f32[40,128]{1,0:T(8,128)S(1)}, f32[40,128]{1,0:T(8,128)S(1)}, u32[]{:S(2)}, u32[]{:S(2)}) collective-permute-start(f32[40,128]{1,0:T(8,128)S(1)} %add.22), channel_id=1, source_target_pairs={{0,8},{1,9},{2,10},{3,11},{4,12},{5,13},{6,14},{7,15},{8,0},{9,1},... | collective-permute-start | bytes 61448 | tf_op jit(solution)/shard_map/ppermute | solution.py:51
  25.3 1.3 %collective-permute-start.11 = (f32[40,128]{1,0:T(8,128)S(1)}, f32[40,128]{1,0:T(8,128)S(1)}, u32[]{:S(2)}, u32[]{:S(2)}) collective-permute-start(f32[40,128]{1,0:T(8,128)S(1)} %add_add_fusion), channel_id=1, source_target_pairs={{0,4},{1,5},{2,6},{3,7},{4,0},{5,1},{6,2},{7,3},{8,12},{9,13},{10,... | collective-permute-start | bytes 61448 | tf_op jit(solution)/shard_map/ppermute | solution.py:51

commit v6 on v5

--- a/solution.py
+++ b/solution.py
@@ -94,8 +94,8 @@
     chips = nx // 2 * ny
     value = value + core_swap(value)
     if chips == 8:
-        parts = [chip_swap(a, b)(value) for a, b in ((4, 4), (1, 5), (2, 6), (3, 7))]
-        value = 0.5 * (value + parts[0]) + parts[1] + parts[2] + parts[3]
+        parts = [chip_swap(a, b)(value) for a, b in ((2, 6), (1, 5), (4, 4), (3, 7))]
+        value = parts[0] + parts[1] + 0.5 * (value + parts[2]) + parts[3]
         return value + core_swap(value)
     step = 1
     while step < chips:
@@ -208,6 +208,20 @@
     out[rows : 2 * rows, :] = piece[3] + piece[4] + piece[5]
 
 
+def mixed_columns(dims, mixing, columns, lane):
+    k, nv, cx, cy = dims
+    which = lane % 64 // 2 % nv
+    mixed = jnp.zeros((k, LANES), F32)
+    for shift in range(1 - nv, nv):
+        coef = jnp.zeros((1, LANES), F32)
+        for v in range(nv):
+            if 0 <= v + shift < nv:
+                coef = jnp.where(which == v, mixing[v, v + shift], coef)
+        source = pltpu.roll(columns, (-2 * shift) % LANES, 1) if shift else columns
+        mixed = mixed + coef * source
+    return mixed
+
+
 def first_columns_of(dims, mixing, columns, kcol, own, lane):
     k, nv, cx, cy = dims
     slot = lane % 64
@@ -219,16 +233,26 @@
     )
     step = 2 * nv
     beside = beside + pltpu.roll(columns, step, 1) + pltpu.roll(columns, LANES - step, 1)
-    which = slot // 2 % nv
-    mixed = jnp.zeros((k, LANES), F32)
-    for shift in range(1 - nv, nv):
-        coef = jnp.zeros((1, LANES), F32)
-        for v in range(nv):
-            if 0 <= v + shift < nv:
-                coef = jnp.where(which == v, mixing[v, v + shift], coef)
-        source = pltpu.roll(columns, (-2 * shift) % LANES, 1) if shift else columns
-        mixed = mixed + coef * source
+    mixed = mixed_columns(dims, mixing, columns, lane)
     return jnp.where(inside, columns + kcol * (beside - 4.0 * columns) + mixed, 0.0)
+
+
+def late_columns_of(dims, mixing, columns, first_columns, kown, lane):
+    k, nv, cx, cy = dims
+    slot = lane % 64
+    inside = (slot >= 2 * nv) & (slot < 2 * nv * (cx + 1))
+    parity = jnp.where(lane < 64, 1, 0)
+    outermost = inside & (lane % 2 == parity)
+
+    def moved(x):
+        return jnp.where(lane < 64, pltpu.roll(x, 65, 1), pltpu.roll(x, 63, 1))
+
+    added = jnp.where(outermost, kown * moved(columns), 0.0)
+    step = 2 * nv
+    beside = pltpu.roll(added, step, 1) + pltpu.roll(added, LANES - step, 1) + moved(first_columns)
+    outer = added + kown * (beside - 4.0 * added) + mixed_columns(dims, mixing, added, lane)
+    inner = kown * jnp.where(lane < 64, pltpu.roll(added, LANES - 1, 1), pltpu.roll(added, 1, 1))
+    return jnp.where(outermost, outer, jnp.where(inside, inner, 0.0))
 
 
 def advance(dims, mixing, kext, load, side, e, lane, store):
@@ -357,7 +381,7 @@
             kext[pl.ds((r + 1) * 8 + v, 1), :] = kappa[v, r : r + 1, :]
 
 
-def middle_kernel(dims, mixing, state, kappa, cell, var, value, weight, first, kext, spread, cells):
+def middle_kernel(dims, mixing, state, kappa, cell, var, value, weight, first, kext, spread, early, cells):
     k, nv, cx, cy = dims
     scatter_kernel(dims, cell, var, value, weight, cells)
     for v in range(nv):
@@ -367,36 +391,58 @@
     set_kappa(dims, kappa, kext)
     lane = lax.broadcasted_iota(jnp.int32, (1, LANES), 1)
     first_step(dims, mixing, kext, state, first, None, range(1, cx + 1), lane, inside=True)
+    for e in range(2, cx):
+        second_step(dims, mixing, kext, first, None, e, early, e - 2, lane)
 
 
 def inner_kernel(
-    dims, factor, mixing, first_in, sides, halo, kext, spread,
-    first, anomalies, means, partial, early, side, first_side, moved, kept,
+    dims, factor, mixing, first_in, early, sides, halo, kext, spread,
+    first, anomalies, means, partial, late, side, late_side, moved, kept,
 ):
     k, nv, cx, cy = dims
+    block = nv * k
+    half = cy // LANES
     lane = lax.broadcasted_iota(jnp.int32, (1, LANES), 1)
-    columns = first_columns_of(dims, mixing, halo[0:k, :], halo[k : k + 1, :], sides[0:k, :], lane)
-    side[...] = edges_of(halo[0:k, :], lane)
-    first_side[...] = edges_of(columns, lane)
-    add_sides(dims, kext, first, side, range(1, cx + 1), lane)
+    columns = halo[0:k, :]
+    first_columns = first_columns_of(dims, mixing, columns, halo[k : k + 1, :], sides[0:k, :], lane)
+    side[...] = edges_of(columns, lane)
+    late_side[...] = late_columns_of(dims, mixing, columns, first_columns, sides[k : k + 1, :], lane)
+
+    def with_sides(e, ref, slot):
+        sums = {}
+        for v in range(nv):
+            at = 2 * (nv * e + v)
+            for j in range(0, k, 8):
+                extra = late_side[pl.ds(j, 8), :]
+                for h in range(half):
+                    lanes = slice(h * LANES, (h + 1) * LANES)
+                    out = early[pl.ds((e - 2) * block + v * k + j, 8), lanes]
+                    if h == 0:
+                        out = out + jnp.where(lane < 2, pltpu.roll(extra, 64 - at, 1), 0.0)
+                    if h == half - 1:
+                        out = out + jnp.where(lane >= LANES - 2, pltpu.roll(extra, LANES - 2 - at, 1), 0.0)
+                    ref[pl.ds(slot * block + v * k + j, 8), lanes] = out
+                    sums[v, h] = out if j == 0 else sums[v, h] + out
+        return sums
+
     outs = (anomalies, means, moved)
     for i, e in enumerate(range(3, cx - 1)):
-        sums = second_step(dims, mixing, kext, first, first_side, e, kept, i, lane)
+        sums = with_sides(e, kept, i)
         anomalies_of(dims, factor, spread, e, i, sums, kept, outs)
     partial[...] = nt(moved[...], anomalies[...])
-    second_step(dims, mixing, kext, first, first_side, 2, early, 0, lane)
-    second_step(dims, mixing, kext, first, first_side, cx - 1, early, 1, lane)
-
-
-def edge_kernel(
-    dims, factor, mixing, state_in, first_in, partial, early, recv_a, recv_b, sides, halo, corner_a, corner_b, kext_in, spread,
-    state, first, anomalies, means, gram, kext, side, first_side, moved, kept,
+    with_sides(2, late, 0)
+    with_sides(cx - 1, late, 1)
+    add_sides(dims, kext, first, side, (1, 2, cx - 1, cx), lane)
+
+
+def rows_kernel(
+    dims, factor, mixing, state_in, first_in, partial, late_in, recv_a, recv_b, sides, halo, kext_in, spread,
+    state, first, anomalies, means, more, outer, kext, side, first_side, moved, kept,
 ):
     k, nv, cx, cy = dims
     block = nv * k
-    gx = lax.axis_index("gx")
-    nx = lax.axis_size("gx")
-    down_is_a = gx % 2 == 0
+    half = cy // LANES
+    down_is_a = lax.axis_index("gx") % 2 == 0
 
     def both(a, b):
         return jnp.where(down_is_a, b, a), jnp.where(down_is_a, a, b)
@@ -411,19 +457,11 @@
     kext[8 * (cx + 1) : 8 * (cx + 2), :] = down
 
     lane = lax.broadcasted_iota(jnp.int32, (1, LANES), 1)
-    slot = lane % 64
-    up, down = both(corner_a[...], corner_b[...])
-    up = jnp.where(gx > 0, up, 0.0)
-    down = jnp.where(gx < nx - 1, down, 0.0)
-    far = 2 * nv * cx
-    columns = jnp.where(slot < 2 * nv, pltpu.roll(up, LANES - far, 1), halo[...])
-    columns = jnp.where((slot >= 2 * nv * (cx + 1)) & (slot < 2 * nv * (cx + 2)), pltpu.roll(down, far, 1), columns)
-    side[...] = edges_of(columns[0:k, :], lane)
-    columns = first_columns_of(dims, mixing, columns[0:k, :], columns[k : k + 1, :], sides[0:k, :], lane)
+    columns = halo[0:k, :]
+    side[...] = edges_of(columns, lane)
+    columns = first_columns_of(dims, mixing, columns, halo[k : k + 1, :], sides[0:k, :], lane)
     first_side[...] = edges_of(columns, lane)
     first_step(dims, mixing, kext, state, first, side, (0, cx + 1), lane)
-    half = cy // LANES
-    outs = (anomalies, means, moved)
 
     def late(e, beyond, near, read, write):
         sums = {}
@@ -441,16 +479,55 @@
                     sums[v, h] = out if j == 0 else sums[v, h] + out
         return sums
 
-    for e, beyond in ((1, 1), (cx, cx + 2)):
+    for i, (e, beyond) in enumerate(((1, 1), (cx, cx + 2))):
         late(e, beyond, e, (first, e * block), (first, e * block))
-    for i, e in enumerate((1, 2, cx - 1, cx)):
-        if i in (0, 3):
-            sums = second_step(dims, mixing, kext, first, first_side, e, kept, i, lane)
-        elif i == 1:
-            sums = late(e, 1, 1, (early, 0), (kept, i * block))
-        else:
-            sums = late(e, cx + 2, cx, (early, block), (kept, i * block))
-        anomalies_of(dims, factor, spread, e, i, sums, kept, outs)
+        second_step(dims, mixing, kext, first, first_side, e, outer, i, lane)
+    for i, (e, beyond, near) in enumerate(((2, 1, 1), (cx - 1, cx + 2, cx))):
+        sums = late(e, beyond, near, (late_in, i * block), (kept, i * block))
+        anomalies_of(dims, factor, spread, e, i, sums, kept, (anomalies, means, moved))
+    more[...] = partial[...] + nt(moved[...], anomalies[...])
+
+
+def corner_kernel(
+    dims, factor, outer, partial, halo, corner_a, corner_b, kext, spread,
+    anomalies, means, gram, side_up, side_down, moved, kept,
+):
+    k, nv, cx, cy = dims
+    block = nv * k
+    half = cy // LANES
+    gx = lax.axis_index("gx")
+    down_is_a = gx % 2 == 0
+    lane = lax.broadcasted_iota(jnp.int32, (1, LANES), 1)
+    a = corner_a[0:k, :]
+    b = corner_b[0:k, :]
+    side_up[...] = edges_of(jnp.where(gx > 0, jnp.where(down_is_a, b, a), 0.0), lane)
+    side_down[...] = edges_of(jnp.where(gx < lax.axis_size("gx") - 1, jnp.where(down_is_a, a, b), 0.0), lane)
+    kside = edges_of(halo[k : k + 8, :], lane)
+
+    def to_ends(x, e, v):
+        return pltpu.roll(x, (LANES - 1 - 2 * (nv * e + v)) & (LANES - 1), 1)
+
+    for i, (e, beyond, source, there) in enumerate(((1, 0, side_up, cx), (cx, cx + 1, side_down, 1))):
+        sums = {}
+        for v in range(nv):
+            kend = to_ends(kside, e, v)[0:1]
+            factors = {}
+            for h in (0, half - 1):
+                lanes = slice(h * LANES, (h + 1) * LANES)
+                here = (lane == 0) if h == 0 else (lane == LANES - 1)
+                row = kext[e * 8 + v : e * 8 + v + 1, lanes] * (kext[beyond * 8 + v : beyond * 8 + v + 1, lanes] + kend)
+                factors[h] = jnp.broadcast_to(jnp.where(here, row, 0.0), (8, LANES))
+            for j in range(0, k, 8):
+                corner = to_ends(source[pl.ds(j, 8), :], there, v)
+                for h in range(half):
+                    lanes = slice(h * LANES, (h + 1) * LANES)
+                    place = pl.ds(i * block + v * k + j, 8)
+                    out = outer[place, lanes]
+                    if h in factors:
+                        out = out + factors[h] * corner
+                    kept[place, lanes] = out
+                    sums[v, h] = out if j == 0 else sums[v, h] + out
+        anomalies_of(dims, factor, spread, e, i, sums, kept, (anomalies, means, moved))
     got = partial[...] + nt(moved[...], anomalies[...])
     whole = got[:, 0:k] + got[:, k : 2 * k]
     matrix = whole[0:k] + whole[k : 2 * k]
@@ -459,7 +536,7 @@
     gram[k // 2 : k // 2 + 8, :] = jnp.concatenate([pull, pull], axis=1)
 
 
-def apply_kernel(dims, gram, inner, inner_means, edge, edge_means, out, buf, sems):
+def apply_kernel(dims, gram, inner, inner_means, near, near_means, edge, edge_means, out, buf, sems):
     k, nv, cx, cy = dims
     half = cy // LANES
     row = lax.broadcasted_iota(jnp.int32, (k, k), 0)
@@ -498,10 +575,12 @@
     copies = []
     for v in range(nv):
         for r in range(cx):
-            deep = 2 <= r < cx - 2
-            i = r - 2 if deep else (r if r < 2 else r - cx + 4)
-            anomalies = inner if deep else edge
-            means = inner_means if deep else edge_means
+            if 2 <= r < cx - 2:
+                anomalies, means, i = inner, inner_means, r - 2
+            elif r in (1, cx - 2):
+                anomalies, means, i = near, near_means, int(r > 1)
+            else:
+                anomalies, means, i = edge, edge_means, int(r > 0)
             at = slice((i * nv + v) * cy, (i * nv + v + 1) * cy)
             value = jnp.dot(high_2, anomalies[:, at], preferred_element_type=F32)
             value = value + jnp.dot(low, anomalies[0:k, at], preferred_element_type=F32)
@@ -557,12 +636,17 @@
     side_b = y_swap(1, sizes)(side_b)
     recv_a = x_swap(0, sizes)(send_a)
 
-    first, kext, spread = pl.pallas_call(
+    first, kext, spread, early = pl.pallas_call(
         functools.partial(middle_kernel, dims),
         name="middle",
         in_specs=[smem()] + [vmem()] * 6,
-        out_specs=[vmem()] * 3,
-        out_shape=[shape((cx + 2) * block, cy), shape((cx + 2) * 8, cy), shape(cx * 8, cy)],
+        out_specs=[vmem()] * 4,
+        out_shape=[
+            shape((cx + 2) * block, cy),
+            shape((cx + 2) * 8, cy),
+            shape(cx * 8, cy),
+            shape((cx - 2) * block, cy),
+        ],
         scratch_shapes=[pltpu.VMEM((64, cy), F32)],
         compiler_params=limits,
     )(mixing, state, kappa, *obs)
@@ -572,10 +656,10 @@
     corner_a = x_swap(0, sizes)(halo)
 
     inner_rows = cx - 4
-    first, inner_anomalies, inner_means, partial, early = pl.pallas_call(
+    first, inner_anomalies, inner_means, partial, late = pl.pallas_call(
         functools.partial(inner_kernel, dims, factor),
         name="inner",
-        in_specs=[smem()] + [vmem()] * 5,
+        in_specs=[smem()] + [vmem()] * 6,
         out_specs=[vmem()] * 5,
         input_output_aliases={1: 0},
         out_shape=[
@@ -592,39 +676,57 @@
             pltpu.VMEM((4 * block, cy), F32),
         ],
         compiler_params=limits,
-    )(mixing, first, sides, halo, kext, spread)
-
-    _, _, edge_anomalies, edge_means, gram = pl.pallas_call(
-        functools.partial(edge_kernel, dims, factor),
-        name="edge",
-        in_specs=[smem()] + [vmem()] * 12,
-        out_specs=[vmem()] * 5,
+    )(mixing, first, early, sides, halo, kext, spread)
+
+    _, _, near_anomalies, near_means, partial, outer, kext = pl.pallas_call(
+        functools.partial(rows_kernel, dims, factor),
+        name="rows",
+        in_specs=[smem()] + [vmem()] * 10,
+        out_specs=[vmem()] * 7,
         out_shape=[
             shape((cx + 4) * block, cy),
             shape((cx + 2) * block, cy),
-            shape(2 * k, 4 * nv * cy, dtype=BF16),
-            shape(4 * 8, cy),
+            shape(2 * k, 2 * nv * cy, dtype=BF16),
+            shape(2 * 8, cy),
+            shape(2 * k + 32, 2 * k),
+            shape(2 * block, cy),
+            shape((cx + 2) * 8, cy),
+        ],
+        scratch_shapes=[
+            pltpu.VMEM((k, LANES), F32),
+            pltpu.VMEM((k, LANES), F32),
+            pltpu.VMEM((2 * k + 32, 2 * nv * cy), BF16),
+            pltpu.VMEM((2 * block, cy), F32),
+        ],
+        input_output_aliases={1: 0, 2: 1},
+        compiler_params=limits,
+    )(mixing, state, first, partial, late, recv_a, recv_b, sides, halo, kext, spread)
+
+    edge_anomalies, edge_means, gram = pl.pallas_call(
+        functools.partial(corner_kernel, dims, factor),
+        name="corner",
+        in_specs=[vmem()] * 7,
+        out_specs=[vmem()] * 3,
+        out_shape=[
+            shape(2 * k, 2 * nv * cy, dtype=BF16),
+            shape(2 * 8, cy),
             shape(k // 2 + 8, 2 * k),
         ],
         scratch_shapes=[
-            pltpu.VMEM(((cx + 2) * 8, cy), F32),
             pltpu.VMEM((k, LANES), F32),
             pltpu.VMEM((k, LANES), F32),
-            pltpu.VMEM((2 * k + 32, 4 * nv * cy), BF16),
-            pltpu.VMEM((4 * block, cy), F32),
+            pltpu.VMEM((2 * k + 32, 2 * nv * cy), BF16),
+            pltpu.VMEM((2 * block, cy), F32),
         ],
-        input_output_aliases={1: 0, 2: 1},
         compiler_params=limits,
-    )(
-        mixing, state, first, partial, early, recv_a, recv_b, sides, halo, corner_a, corner_b, kext, spread
-    )
+    )(outer, partial, halo, corner_a, corner_b, kext, spread)
 
     gram = all_sum(gram, sizes)
 
     return pl.pallas_call(
         functools.partial(apply_kernel, dims),
         name="apply",
-        in_specs=[vmem()] * 5,
+        in_specs=[vmem()] * 7,
         out_specs=pl.BlockSpec(memory_space=pltpu.HBM),
         out_shape=shape(k, nv, cx, cy),
         scratch_shapes=[
@@ -632,7 +734,7 @@
             pltpu.SemaphoreType.DMA((nv, cy // LANES)),
         ],
         compiler_params=limits,
-    )(gram, inner_anomalies, inner_means, edge_anomalies, edge_means)
+    )(gram, inner_anomalies, inner_means, near_anomalies, near_means, edge_anomalies, edge_means)
 
 
 def solution(mesh):

time: 29.9 us -> 29.1 us (0.973)
  waiting for transfers between devices: 7.33 us -> 4.91 us
  starting transfers between devices: 10.6 us -> 12.2 us
    ppermute x12, waiting for transfers between devices: 7.33 us -> 4.91 us  [pair_swap(): return lambda value: lax.ppermute(value, ('grp', 'gx', 'gy'), pairs)]
    ppermute x12, starting transfers between devices: 10.6 us -> 12.2 us  [pair_swap(): return lambda value: lax.ppermute(value, ('grp', 'gx', 'gy'), pairs)]
    pallas_call x1, Pallas kernels: 2.4 us -> 1.82 us  [local(): pl.pallas_call(functools.partial(inner_kernel, dims, factor), name='inner...]
    pallas_call x1, Pallas kernels: 1.75 us -> 2.33 us  [local(): pl.pallas_call(functools.partial(middle_kernel, dims), name='middle', in_...]
    pallas_call x1 -> x2, Pallas kernels: 2.42 us -> 2.47 us  [the longest x1 1.74 us: local(): pl.pallas_call(functools.partial(rows_kernel, dims, factor), name='rows',...]
  transfers between devices with their start and end apart: 12 -> 12, of which waited for: 7 -> 4; matrix products, arithmetic and copies ran while one was open for 0% -> 0% of each run, Pallas kernels for 14% -> 20%
where the time goes in v6:
time: 29.1 us; the launch traced here: 29 us
  starting transfers between devices  12.2 us (42%)
  Pallas kernels  11.8 us (41%)
  waiting for transfers between devices  4.91 us (17%)
    ppermute x12, starting transfers between devices, pair_swap(): return lambda value: lax.ppermute(value, ('grp', 'gx', 'gy'), pairs)  12.2 us
    ppermute x12, waiting for transfers between devices, pair_swap(): return lambda value: lax.ppermute(value, ('grp', 'gx', 'gy'), pairs)  4.91 us
    pallas_call x1, Pallas kernels, local(): pl.pallas_call(functools.partial(apply_kernel, dims), name='apply', in_sp...  3.12 us
    pallas_call x1, Pallas kernels, local(): pl.pallas_call(functools.partial(middle_kernel, dims), name='middle', in_...  2.33 us
    pallas_call x1, Pallas kernels, local(): pl.pallas_call(functools.partial(load_kernel, dims), name='load', in_spec...  2.03 us
    pallas_call x1, Pallas kernels, local(): pl.pallas_call(functools.partial(inner_kernel, dims, factor), name='inner...  1.82 us
    pallas_call x1, Pallas kernels, local(): pl.pallas_call(functools.partial(rows_kernel, dims, factor), name='rows',...  1.74 us
    pallas_call x1, Pallas kernels, local(): pl.pallas_call(functools.partial(corner_kernel, dims, factor), name='corn...  0.74 us
  transfers between devices with their start and end apart: 12, of which 4 were waited for; matrix products, arithmetic and copies ran while one was open for 0% of the time, Pallas kernels for 20%

profile of v6, /device:TPU:0, one launch (start us, length us, event | category | flops | bytes accessed | tf_op | source)
XLA Modules:
  0.0 29.0 jit_solution(8452928067156958567)
XLA Ops:
  0.0 2.0 %load.1 = (f32[2304,256]{1,0:T(8,128)S(1)}, f32[392,256]{1,0:T(8,128)S(1)}, f32[392,256]{1,0:T(8,128)S(1)}, f32[72,128]{1,0:T(8,128)S(1)}, f32[72,128]{1,0:T(8,1...) custom-call(f32[1536,256]{1,0:T(8,128)} %bitcast.5, ...), custom_call_target="tpu_custom_call" | custom-call | tf_op jit(solution)/shard_map/load/pallas_call | solution.py:614
  2.0 0.5 %collective-permute-start.2 = (f32[392,256]{1,0:T(8,128)S(1)}, f32[392,256]{1,0:T(8,128)S(1)}, u32[]{:S(2)}, u32[]{:S(2)}) collective-permute-start(f32[392,256]{1,0:T(8,128)S(1)} %get-tuple-element.57), channel_id=1, source_target_pairs={{0,4},{1,5},{2,6},{3,7},{4,0},{5,1},{6,2},{7,3},{8,12},{9,13},{10,... | collective-permute-start | bytes 1204232 | tf_op jit(solution)/shard_map/ppermute | solution.py:51
  2.6 2.6 %collective-permute-start.3 = (f32[392,256]{1,0:T(8,128)S(1)}, f32[392,256]{1,0:T(8,128)S(1)}, u32[]{:S(2)}, u32[]{:S(2)}) collective-permute-start(f32[392,256]{1,0:T(8,128)S(1)} %get-tuple-element.58), channel_id=1, source_target_pairs={{0,16},{1,17},{2,18},{3,19},{4,8},{5,9},{6,10},{7,11},{8,4},{9,5},... | collective-permute-start | bytes 1204232 | tf_op jit(solution)/shard_map/ppermute | solution.py:51
  5.1 1.6 %collective-permute-start = (f32[72,128]{1,0:T(8,128)S(1)}, f32[72,128]{1,0:T(8,128)S(1)}, u32[]{:S(2)}, u32[]{:S(2)}) collective-permute-start(f32[72,128]{1,0:T(8,128)S(1)} %get-tuple-element.39), channel_id=1, source_target_pairs={{0,1},{1,0},{2,3},{3,2},{4,5},{5,4},{6,7},{7,6},{8,9},{9,8},{10,11... | collective-permute-start | bytes 110600 | tf_op jit(solution)/shard_map/ppermute | solution.py:51
  6.7 0.0 collective-permute-start.1
  6.7 2.3 %middle.1 = (f32[1920,256]{1,0:T(8,128)S(1)}, f32[80,256]{1,0:T(8,128)S(1)}, f32[64,256]{1,0:T(8,128)S(1)}, f32[1152,256]{1,0:T(8,128)S(1)}) custom-call(f32[3,3]{1,0:T(4,128)S(1)} %get-tuple-element.37.mixing, f32[2304,256]{1,0:T(8,128)S(1)} %get-tuple-element.38.state.state_in, f32[3,8,256]{2,1,0:T(8,128)S(1)} %get-tuple-element.41.kappa, ...), custom_call_target="tpu_custom_call" | custom-call | tf_op jit(solution)/shard_map/middle/pallas_call | solution.py:639
  9.1 0.0 collective-permute-done
  9.1 0.0 collective-permute-done.1
  9.1 0.6 %collective-permute-start.4 = (f32[72,128]{1,0:T(8,128)S(1)}, f32[72,128]{1,0:T(8,128)S(1)}, u32[]{:S(2)}, u32[]{:S(2)}) collective-permute-start(f32[72,128]{1,0:T(8,128)S(1)} %add.21.halo), channel_id=1, source_target_pairs={{0,4},{1,5},{2,6},{3,7},{4,0},{5,1},{6,2},{7,3},{8,12},{9,13},{10,... | collective-permute-start | bytes 110600 | tf_op jit(solution)/shard_map/ppermute | solution.py:51
  9.7 0.9 %collective-permute-start.5 = (f32[72,128]{1,0:T(8,128)S(1)}, f32[72,128]{1,0:T(8,128)S(1)}, u32[]{:S(2)}, u32[]{:S(2)}) collective-permute-start(f32[72,128]{1,0:T(8,128)S(1)} %add.21.halo), channel_id=1, source_target_pairs={{0,16},{1,17},{2,18},{3,19},{4,8},{5,9},{6,10},{7,11},{8,4},{9,5},... | collective-permute-start | bytes 110600 | tf_op jit(solution)/shard_map/ppermute | solution.py:51
  10.6 1.8 %inner.1 = (f32[1920,256]{1,0:T(8,128)S(1)}, bf16[128,3072]{1,0:T(8,128)(2,1)S(1)}, f32[32,256]{1,0:T(8,128)S(1)}, f32[160,128]{1,0:T(8,128)S(1)}, f32[384,256]{1,0:T(8,128)S(1)}) custom-call(f32[3,3]{1,0:T(4,128)S(1)} %get-tuple-element.37.mixing, f32[1920,256]{1,0:T(8,128)S(1)} %get-tuple-element.47.first_in, ...), custom_call_target="tpu_custom_call", output_to_operand_aliasing={{0}: (1, {})} | custom-call | tf_op jit(solution)/shard_map/inner/pallas_call | solution.py:659
  12.4 0.0 collective-permute-done.2.recv_a
  12.4 0.0 collective-permute-done.3.recv_b
  12.4 1.7 %rows.1 = (f32[2304,256]{1,0:T(8,128)S(1)}, f32[1920,256]{1,0:T(8,128)S(1)}, bf16[128,1536]{1,0:T(8,128)(2,1)S(1)}, f32[16,256]{1,0:T(8,128)S(1)}, f32[160,128]{...) custom-call(f32[3,3]{1,0:T(4,128)S(1)} %get-tuple-element.37.mixing,, ...), custom_call_target="tpu_custom_call", output_to_operand_aliasing={{0}: (1, {}), {1}: (2, {})} | custom-call | tf_op jit(solution)/shard_map/rows/pallas_call | solution.py:681
  14.2 0.0 collective-permute-done.4.corner_a
  14.2 0.0 collective-permute-done.5.corner_b
  14.2 0.7 %corner.1 = (bf16[128,1536]{1,0:T(8,128)(2,1)S(1)}, f32[16,256]{1,0:T(8,128)S(1)}, f32[40,128]{1,0:T(8,128)S(1)}) custom-call(f32[384,256]{1,0:T(8,128)S(1)} %get-tuple-element.59.outer, f32[160,128]{1,0:T(8,128)S(1)} %get-tuple-element.60.partial, f32[72,128]{1,0:T(8,128)S(1)} %add.21.halo, f32[72,128]{1,0:T(8,128)S(1)} %collective-permute-done.4.corner_a, ...), custom_call_target="tpu_custom_call" | custom-call | tf_op jit(solution)/shard_map/corner/pallas_call | solution.py:705
  14.9 0.2 collective-permute-start.6
  15.1 1.0 %collective-permute-done.6 = f32[40,128]{1,0:T(8,128)S(1)} collective-permute-done((f32[40,128]{1,0:T(8,128)S(1)}, f32[40,128]{1,0:T(8,128)S(1)}, u32[]{:S(2)}, u32[]{:S(2)}) %collective-permute-start.6) | collective-permute-done | bytes 20512 | tf_op jit(solution)/shard_map/ppermute | solution.py:51
  16.1 3.2 %collective-permute-start.10 = (f32[40,128]{1,0:T(8,128)S(1)}, f32[40,128]{1,0:T(8,128)S(1)}, u32[]{:S(2)}, u32[]{:S(2)}) collective-permute-start(f32[40,128]{1,0:T(8,128)S(1)} %add.22), channel_id=1, source_target_pairs={{0,3},{1,2},{2,1},{3,0},{4,15},{5,14},{6,13},{7,12},{8,11},{9,10},... | collective-permute-start | bytes 61448 | tf_op jit(solution)/shard_map/ppermute | solution.py:51
  19.4 1.0 %collective-permute-start.7 = (f32[40,128]{1,0:T(8,128)S(1)}, f32[40,128]{1,0:T(8,128)S(1)}, u32[]{:S(2)}, u32[]{:S(2)}) collective-permute-start(f32[40,128]{1,0:T(8,128)S(1)} %add.22), channel_id=1, source_target_pairs={{0,2},{1,3},{2,0},{3,1},{4,14},{5,15},{6,12},{7,13},{8,10},{9,11},... | collective-permute-start | bytes 61448 | tf_op jit(solution)/shard_map/ppermute | solution.py:51
  20.4 0.1 collective-permute-start.8
  20.5 1.0 %collective-permute-start.9 = (f32[40,128]{1,0:T(8,128)S(1)}, f32[40,128]{1,0:T(8,128)S(1)}, u32[]{:S(2)}, u32[]{:S(2)}) collective-permute-start(f32[40,128]{1,0:T(8,128)S(1)} %add.22), channel_id=1, source_target_pairs={{0,8},{1,9},{2,10},{3,11},{4,12},{5,13},{6,14},{7,15},{8,0},{9,1},... | collective-permute-start | bytes 61448 | tf_op jit(solution)/shard_map/ppermute | solution.py:51
  21.6 0.2 collective-permute-done.10
  21.7 2.8 %collective-permute-done.7 = f32[40,128]{1,0:T(8,128)S(1)} collective-permute-done((f32[40,128]{1,0:T(8,128)S(1)}, f32[40,128]{1,0:T(8,128)S(1)}, u32[]{:S(2)}, u32[]{:S(2)}) %collective-permute-start.7) | collective-permute-done | bytes 20512 | tf_op jit(solution)/shard_map/ppermute | solution.py:51
  24.5 0.0 collective-permute-done.8
  24.5 0.0 collective-permute-done.9
  24.5 0.4 %collective-permute-start.11 = (f32[40,128]{1,0:T(8,128)S(1)}, f32[40,128]{1,0:T(8,128)S(1)}, u32[]{:S(2)}, u32[]{:S(2)}) collective-permute-start(f32[40,128]{1,0:T(8,128)S(1)} %add_add_fusion), channel_id=1, source_target_pairs={{0,4},{1,5},{2,6},{3,7},{4,0},{5,1},{6,2},{7,3},{8,12},{9,13},{10,... | collective-permute-start | bytes 61448 | tf_op jit(solution)/shard_map/ppermute | solution.py:51
  25.0 0.8 %collective-permute-done.11 = f32[40,128]{1,0:T(8,128)S(1)} collective-permute-done((f32[40,128]{1,0:T(8,128)S(1)}, f32[40,128]{1,0:T(8,128)S(1)}, u32[]{:S(2)}, u32[]{:S(2)}) %collective-permute-start.11) | collective-permute-done | bytes 20512 | tf_op jit(solution)/shard_map/ppermute | solution.py:51
  25.8 3.1 %apply.1 = f32[64,3,8,256]{3,2,1,0:T(8,128)} custom-call(f32[40,128]{1,0:T(8,128)S(1)} %add.27.gram, bf16[128,3072]{1,0:T(8,128)(2,1)S(1)} %get-tuple-element.63.inner, f32[32,256]{1,0:T(8,128)S(1)} %get-tuple-element.64.inner_means, bf16[128,1536]{1,0:T(8,128)(2,1)S(1)} %get-tuple-element.65.near, f32[16,256]{1,0:T(8,128)S(1)} %get-tuple-element.66.near_means, ...), custom_call_target="tpu_custom_call" | custom-call | tf_op jit(solution)/shard_map/apply/pallas_call | solution.py:726
  (4 shorter events, 0.0 us)
Async XLA Ops:
  2.0 10.4 %collective-permute-start.2 = (f32[392,256]{1,0:T(8,128)S(1)}, f32[392,256]{1,0:T(8,128)S(1)}, u32[]{:S(2)}, u32[]{:S(2)}) collective-permute-start(f32[392,256]{1,0:T(8,128)S(1)} %get-tuple-element.57), channel_id=1, source_target_pairs={{0,4},{1,5},{2,6},{3,7},{4,0},{5,1},{6,2},{7,3},{8,12},{9,13},{10,... | collective-permute-start | bytes 1204232 | tf_op jit(solution)/shard_map/ppermute | solution.py:51
  2.6 9.9 %collective-permute-start.3 = (f32[392,256]{1,0:T(8,128)S(1)}, f32[392,256]{1,0:T(8,128)S(1)}, u32[]{:S(2)}, u32[]{:S(2)}) collective-permute-start(f32[392,256]{1,0:T(8,128)S(1)} %get-tuple-element.58), channel_id=1, source_target_pairs={{0,16},{1,17},{2,18},{3,19},{4,8},{5,9},{6,10},{7,11},{8,4},{9,5},... | collective-permute-start | bytes 1204232 | tf_op jit(solution)/shard_map/ppermute | solution.py:51
  5.1 4.0 %collective-permute-start = (f32[72,128]{1,0:T(8,128)S(1)}, f32[72,128]{1,0:T(8,128)S(1)}, u32[]{:S(2)}, u32[]{:S(2)}) collective-permute-start(f32[72,128]{1,0:T(8,128)S(1)} %get-tuple-element.39), channel_id=1, source_target_pairs={{0,1},{1,0},{2,3},{3,2},{4,5},{5,4},{6,7},{7,6},{8,9},{9,8},{10,11... | collective-permute-start | bytes 110600 | tf_op jit(solution)/shard_map/ppermute | solution.py:51
  6.7 2.4 %collective-permute-start.1 = (f32[72,128]{1,0:T(8,128)S(1)}, f32[72,128]{1,0:T(8,128)S(1)}, u32[]{:S(2)}, u32[]{:S(2)}) collective-permute-start(f32[72,128]{1,0:T(8,128)S(1)} %get-tuple-element.40), channel_id=1, source_target_pairs={{0,4},{1,2},{2,1},{3,7},{4,0},{5,6},{6,5},{7,3},{8,12},{9,10},{10,... | collective-permute-start | bytes 110600 | tf_op jit(solution)/shard_map/ppermute | solution.py:51
  9.1 5.0 %collective-permute-start.4 = (f32[72,128]{1,0:T(8,128)S(1)}, f32[72,128]{1,0:T(8,128)S(1)}, u32[]{:S(2)}, u32[]{:S(2)}) collective-permute-start(f32[72,128]{1,0:T(8,128)S(1)} %add.21.halo), channel_id=1, source_target_pairs={{0,4},{1,5},{2,6},{3,7},{4,0},{5,1},{6,2},{7,3},{8,12},{9,13},{10,... | collective-permute-start | bytes 110600 | tf_op jit(solution)/shard_map/ppermute | solution.py:51
  9.7 4.5 %collective-permute-start.5 = (f32[72,128]{1,0:T(8,128)S(1)}, f32[72,128]{1,0:T(8,128)S(1)}, u32[]{:S(2)}, u32[]{:S(2)}) collective-permute-start(f32[72,128]{1,0:T(8,128)S(1)} %add.21.halo), channel_id=1, source_target_pairs={{0,16},{1,17},{2,18},{3,19},{4,8},{5,9},{6,10},{7,11},{8,4},{9,5},... | collective-permute-start | bytes 110600 | tf_op jit(solution)/shard_map/ppermute | solution.py:51
  14.9 1.2 %collective-permute-start.6 = (f32[40,128]{1,0:T(8,128)S(1)}, f32[40,128]{1,0:T(8,128)S(1)}, u32[]{:S(2)}, u32[]{:S(2)}) collective-permute-start(f32[40,128]{1,0:T(8,128)S(1)} %get-tuple-element.62), channel_id=1, source_target_pairs={{0,4},{1,5},{2,6},{3,7},{4,0},{5,1},{6,2},{7,3},{8,12},{9,13},{10,... | collective-permute-start | bytes 61448 | tf_op jit(solution)/shard_map/ppermute | solution.py:51
  16.1 5.6 %collective-permute-start.10 = (f32[40,128]{1,0:T(8,128)S(1)}, f32[40,128]{1,0:T(8,128)S(1)}, u32[]{:S(2)}, u32[]{:S(2)}) collective-permute-start(f32[40,128]{1,0:T(8,128)S(1)} %add.22), channel_id=1, source_target_pairs={{0,3},{1,2},{2,1},{3,0},{4,15},{5,14},{6,13},{7,12},{8,11},{9,10},... | collective-permute-start | bytes 61448 | tf_op jit(solution)/shard_map/ppermute | solution.py:51
  19.4 5.2 %collective-permute-start.7 = (f32[40,128]{1,0:T(8,128)S(1)}, f32[40,128]{1,0:T(8,128)S(1)}, u32[]{:S(2)}, u32[]{:S(2)}) collective-permute-start(f32[40,128]{1,0:T(8,128)S(1)} %add.22), channel_id=1, source_target_pairs={{0,2},{1,3},{2,0},{3,1},{4,14},{5,15},{6,12},{7,13},{8,10},{9,11},... | collective-permute-start | bytes 61448 | tf_op jit(solution)/shard_map/ppermute | solution.py:51
  20.4 4.1 %collective-permute-start.8 = (f32[40,128]{1,0:T(8,128)S(1)}, f32[40,128]{1,0:T(8,128)S(1)}, u32[]{:S(2)}, u32[]{:S(2)}) collective-permute-start(f32[40,128]{1,0:T(8,128)S(1)} %add.22), channel_id=1, source_target_pairs={{0,1},{1,0},{2,3},{3,2},{4,13},{5,12},{6,15},{7,14},{8,9},{9,8},{1... | collective-permute-start | bytes 61448 | tf_op jit(solution)/shard_map/ppermute | solution.py:51
  20.5 4.0 %collective-permute-start.9 = (f32[40,128]{1,0:T(8,128)S(1)}, f32[40,128]{1,0:T(8,128)S(1)}, u32[]{:S(2)}, u32[]{:S(2)}) collective-permute-start(f32[40,128]{1,0:T(8,128)S(1)} %add.22), channel_id=1, source_target_pairs={{0,8},{1,9},{2,10},{3,11},{4,12},{5,13},{6,14},{7,15},{8,0},{9,1},... | collective-permute-start | bytes 61448 | tf_op jit(solution)/shard_map/ppermute | solution.py:51
  24.5 1.3 %collective-permute-start.11 = (f32[40,128]{1,0:T(8,128)S(1)}, f32[40,128]{1,0:T(8,128)S(1)}, u32[]{:S(2)}, u32[]{:S(2)}) collective-permute-start(f32[40,128]{1,0:T(8,128)S(1)} %add_add_fusion), channel_id=1, source_target_pairs={{0,4},{1,5},{2,6},{3,7},{4,0},{5,1},{6,2},{7,3},{8,12},{9,13},{10,... | collective-permute-start | bytes 61448 | tf_op jit(solution)/shard_map/ppermute | solution.py:51

commit v7 on v6

--- a/solution.py
+++ b/solution.py
@@ -126,7 +126,7 @@
     kappa = small[0]
     k, nv, cx, cy = dims
     rows = nv * cx
-    chunks = 4
+    chunks = 2
     part = k // chunks
     copies = []
     half = cy // LANES
@@ -546,7 +546,7 @@
     matrix = jnp.concatenate([both[0 : k // 2, 0:k], both[0 : k // 2, k : 2 * k]], axis=0) + eye
     pull = both[k // 2 : k // 2 + 8, 0:k]
     pull = jnp.concatenate([pull, pull], axis=0)
-    norm = jnp.sqrt(jnp.sum(jnp.sum(matrix * matrix, axis=1, keepdims=True), axis=0, keepdims=True))
+    norm = jnp.sqrt(jnp.sum(jnp.sum(matrix * matrix, axis=0, keepdims=True), axis=1, keepdims=True))
 
     def one(x, y):
         return jnp.dot(x, y, preferred_element_type=F32)
@@ -558,7 +558,8 @@
         both = one(jnp.concatenate([a_high, a_low], axis=0), b_high)
         return both[0:rows] + (both[rows:] + one(a_high, b_low))
 
-    root = matrix / norm
+    scale = 1.0 / norm
+    root = matrix * scale
     correction = 1.5 * eye - 0.5 * root
     stacked = dot(jnp.concatenate([root, pull], axis=0), correction)
     root = dot(stacked[0:k], correction)
@@ -568,8 +569,8 @@
         if i < NS_ITERS - 1:
             root = dot(dot(root, correction), correction)
         carried = dot(carried, correction)
-    shift = dot(carried[k:], carried[0:k]) / norm
-    weights = carried[0:k] / jnp.sqrt(norm) + shift[0:1, :]
+    shift = dot(carried[k:], carried[0:k]) * scale
+    weights = carried[0:k] * jnp.sqrt(scale) + shift[0:1, :]
     high, low = split_2(weights)
     high_2 = jnp.concatenate([high, high], axis=1)
     copies = []
@@ -625,7 +626,7 @@
             shape(k + 8, LANES),
         ]
         + [shape(*a.shape, dtype=a.dtype) for a in small],
-        scratch_shapes=[pltpu.VMEM((cy // LANES, k * rows, LANES), F32), pltpu.SemaphoreType.DMA((4, cy // LANES)), pltpu.SemaphoreType.DMA((6,))],
+        scratch_shapes=[pltpu.VMEM((cy // LANES, k * rows, LANES), F32), pltpu.SemaphoreType.DMA((2, cy // LANES)), pltpu.SemaphoreType.DMA((6,))],
         compiler_params=limits,
     )(
         *(pltpu.with_memory_space_constraint(a, pltpu.HBM) for a in (ensemble.reshape(k * rows, cy),) + small)

time: 29.1 us -> 29.1 us (level)
  no operation moved by 1% of the time
where the time goes in v7:
time: 29.1 us; the launch traced here: 28.9 us
  starting transfers between devices  12.2 us (42%)
  Pallas kernels  11.8 us (41%)
  waiting for transfers between devices  4.91 us (17%)
    ppermute x12, starting transfers between devices, pair_swap(): return lambda value: lax.ppermute(value, ('grp', 'gx', 'gy'), pairs)  12.2 us
    ppermute x12, waiting for transfers between devices, pair_swap(): return lambda value: lax.ppermute(value, ('grp', 'gx', 'gy'), pairs)  4.91 us
    pallas_call x1, Pallas kernels, local(): pl.pallas_call(functools.partial(apply_kernel, dims), name='apply', in_sp...  3.12 us
    pallas_call x1, Pallas kernels, local(): pl.pallas_call(functools.partial(middle_kernel, dims), name='middle', in_...  2.33 us
    pallas_call x1, Pallas kernels, local(): pl.pallas_call(functools.partial(load_kernel, dims), name='load', in_spec...  2.02 us
    pallas_call x1, Pallas kernels, local(): pl.pallas_call(functools.partial(inner_kernel, dims, factor), name='inner...  1.82 us
    pallas_call x1, Pallas kernels, local(): pl.pallas_call(functools.partial(rows_kernel, dims, factor), name='rows',...  1.74 us
    pallas_call x1, Pallas kernels, local(): pl.pallas_call(functools.partial(corner_kernel, dims, factor), name='corn...  0.74 us
  transfers between devices with their start and end apart: 12, of which 4 were waited for; matrix products, arithmetic and copies ran while one was open for 0% of the time, Pallas kernels for 20%

profile of v7, /device:TPU:0, one launch (start us, length us, event | category | flops | bytes accessed | tf_op | source)
XLA Modules:
  0.0 28.9 jit_solution(14364392479936942698)
XLA Ops:
  0.0 2.0 %load.1 = (f32[2304,256]{1,0:T(8,128)S(1)}, f32[392,256]{1,0:T(8,128)S(1)}, f32[392,256]{1,0:T(8,128)S(1)}, f32[72,128]{1,0:T(8,128)S(1)}, f32[72,128]{1,0:T(8,1...) custom-call(f32[1536,256]{1,0:T(8,128)} %bitcast.5, ...), custom_call_target="tpu_custom_call" | custom-call | tf_op jit(solution)/shard_map/load/pallas_call | solution.py:615
  2.0 0.5 %collective-permute-start.2 = (f32[392,256]{1,0:T(8,128)S(1)}, f32[392,256]{1,0:T(8,128)S(1)}, u32[]{:S(2)}, u32[]{:S(2)}) collective-permute-start(f32[392,256]{1,0:T(8,128)S(1)} %get-tuple-element.57), channel_id=1, source_target_pairs={{0,4},{1,5},{2,6},{3,7},{4,0},{5,1},{6,2},{7,3},{8,12},{9,13},{10,... | collective-permute-start | bytes 1204232 | tf_op jit(solution)/shard_map/ppermute | solution.py:51
  2.5 2.6 %collective-permute-start.3 = (f32[392,256]{1,0:T(8,128)S(1)}, f32[392,256]{1,0:T(8,128)S(1)}, u32[]{:S(2)}, u32[]{:S(2)}) collective-permute-start(f32[392,256]{1,0:T(8,128)S(1)} %get-tuple-element.58), channel_id=1, source_target_pairs={{0,16},{1,17},{2,18},{3,19},{4,8},{5,9},{6,10},{7,11},{8,4},{9,5},... | collective-permute-start | bytes 1204232 | tf_op jit(solution)/shard_map/ppermute | solution.py:51
  5.1 1.6 %collective-permute-start = (f32[72,128]{1,0:T(8,128)S(1)}, f32[72,128]{1,0:T(8,128)S(1)}, u32[]{:S(2)}, u32[]{:S(2)}) collective-permute-start(f32[72,128]{1,0:T(8,128)S(1)} %get-tuple-element.39), channel_id=1, source_target_pairs={{0,1},{1,0},{2,3},{3,2},{4,5},{5,4},{6,7},{7,6},{8,9},{9,8},{10,11... | collective-permute-start | bytes 110600 | tf_op jit(solution)/shard_map/ppermute | solution.py:51
  6.7 0.0 collective-permute-start.1
  6.7 2.3 %middle.1 = (f32[1920,256]{1,0:T(8,128)S(1)}, f32[80,256]{1,0:T(8,128)S(1)}, f32[64,256]{1,0:T(8,128)S(1)}, f32[1152,256]{1,0:T(8,128)S(1)}) custom-call(f32[3,3]{1,0:T(4,128)S(1)} %get-tuple-element.37.mixing, f32[2304,256]{1,0:T(8,128)S(1)} %get-tuple-element.38.state.state_in, f32[3,8,256]{2,1,0:T(8,128)S(1)} %get-tuple-element.41.kappa, ...), custom_call_target="tpu_custom_call" | custom-call | tf_op jit(solution)/shard_map/middle/pallas_call | solution.py:640
  9.1 0.0 collective-permute-done
  9.1 0.0 collective-permute-done.1
  9.1 0.6 %collective-permute-start.4 = (f32[72,128]{1,0:T(8,128)S(1)}, f32[72,128]{1,0:T(8,128)S(1)}, u32[]{:S(2)}, u32[]{:S(2)}) collective-permute-start(f32[72,128]{1,0:T(8,128)S(1)} %add.21.halo), channel_id=1, source_target_pairs={{0,4},{1,5},{2,6},{3,7},{4,0},{5,1},{6,2},{7,3},{8,12},{9,13},{10,... | collective-permute-start | bytes 110600 | tf_op jit(solution)/shard_map/ppermute | solution.py:51
  9.7 0.9 %collective-permute-start.5 = (f32[72,128]{1,0:T(8,128)S(1)}, f32[72,128]{1,0:T(8,128)S(1)}, u32[]{:S(2)}, u32[]{:S(2)}) collective-permute-start(f32[72,128]{1,0:T(8,128)S(1)} %add.21.halo), channel_id=1, source_target_pairs={{0,16},{1,17},{2,18},{3,19},{4,8},{5,9},{6,10},{7,11},{8,4},{9,5},... | collective-permute-start | bytes 110600 | tf_op jit(solution)/shard_map/ppermute | solution.py:51
  10.6 1.8 %inner.1 = (f32[1920,256]{1,0:T(8,128)S(1)}, bf16[128,3072]{1,0:T(8,128)(2,1)S(1)}, f32[32,256]{1,0:T(8,128)S(1)}, f32[160,128]{1,0:T(8,128)S(1)}, f32[384,256]{1,0:T(8,128)S(1)}) custom-call(f32[3,3]{1,0:T(4,128)S(1)} %get-tuple-element.37.mixing, f32[1920,256]{1,0:T(8,128)S(1)} %get-tuple-element.47.first_in, ...), custom_call_target="tpu_custom_call", output_to_operand_aliasing={{0}: (1, {})} | custom-call | tf_op jit(solution)/shard_map/inner/pallas_call | solution.py:660
  12.4 0.0 collective-permute-done.2.recv_a
  12.4 0.0 collective-permute-done.3.recv_b
  12.4 1.7 %rows.1 = (f32[2304,256]{1,0:T(8,128)S(1)}, f32[1920,256]{1,0:T(8,128)S(1)}, bf16[128,1536]{1,0:T(8,128)(2,1)S(1)}, f32[16,256]{1,0:T(8,128)S(1)}, f32[160,128]{...) custom-call(f32[3,3]{1,0:T(4,128)S(1)} %get-tuple-element.37.mixing,, ...), custom_call_target="tpu_custom_call", output_to_operand_aliasing={{0}: (1, {}), {1}: (2, {})} | custom-call | tf_op jit(solution)/shard_map/rows/pallas_call | solution.py:682
  14.1 0.0 collective-permute-done.4.corner_a
  14.2 0.0 collective-permute-done.5.corner_b
  14.2 0.7 %corner.1 = (bf16[128,1536]{1,0:T(8,128)(2,1)S(1)}, f32[16,256]{1,0:T(8,128)S(1)}, f32[40,128]{1,0:T(8,128)S(1)}) custom-call(f32[384,256]{1,0:T(8,128)S(1)} %get-tuple-element.59.outer, f32[160,128]{1,0:T(8,128)S(1)} %get-tuple-element.60.partial, f32[72,128]{1,0:T(8,128)S(1)} %add.21.halo, f32[72,128]{1,0:T(8,128)S(1)} %collective-permute-done.4.corner_a, ...), custom_call_target="tpu_custom_call" | custom-call | tf_op jit(solution)/shard_map/corner/pallas_call | solution.py:706
  14.9 0.2 collective-permute-start.6
  15.1 1.0 %collective-permute-done.6 = f32[40,128]{1,0:T(8,128)S(1)} collective-permute-done((f32[40,128]{1,0:T(8,128)S(1)}, f32[40,128]{1,0:T(8,128)S(1)}, u32[]{:S(2)}, u32[]{:S(2)}) %collective-permute-start.6) | collective-permute-done | bytes 20512 | tf_op jit(solution)/shard_map/ppermute | solution.py:51
  16.1 3.2 %collective-permute-start.10 = (f32[40,128]{1,0:T(8,128)S(1)}, f32[40,128]{1,0:T(8,128)S(1)}, u32[]{:S(2)}, u32[]{:S(2)}) collective-permute-start(f32[40,128]{1,0:T(8,128)S(1)} %add.22), channel_id=1, source_target_pairs={{0,3},{1,2},{2,1},{3,0},{4,15},{5,14},{6,13},{7,12},{8,11},{9,10},... | collective-permute-start | bytes 61448 | tf_op jit(solution)/shard_map/ppermute | solution.py:51
  19.4 1.0 %collective-permute-start.7 = (f32[40,128]{1,0:T(8,128)S(1)}, f32[40,128]{1,0:T(8,128)S(1)}, u32[]{:S(2)}, u32[]{:S(2)}) collective-permute-start(f32[40,128]{1,0:T(8,128)S(1)} %add.22), channel_id=1, source_target_pairs={{0,2},{1,3},{2,0},{3,1},{4,14},{5,15},{6,12},{7,13},{8,10},{9,11},... | collective-permute-start | bytes 61448 | tf_op jit(solution)/shard_map/ppermute | solution.py:51
  20.4 0.1 collective-permute-start.8
  20.5 1.0 %collective-permute-start.9 = (f32[40,128]{1,0:T(8,128)S(1)}, f32[40,128]{1,0:T(8,128)S(1)}, u32[]{:S(2)}, u32[]{:S(2)}) collective-permute-start(f32[40,128]{1,0:T(8,128)S(1)} %add.22), channel_id=1, source_target_pairs={{0,8},{1,9},{2,10},{3,11},{4,12},{5,13},{6,14},{7,15},{8,0},{9,1},... | collective-permute-start | bytes 61448 | tf_op jit(solution)/shard_map/ppermute | solution.py:51
  21.5 0.2 collective-permute-done.10
  21.7 2.8 %collective-permute-done.7 = f32[40,128]{1,0:T(8,128)S(1)} collective-permute-done((f32[40,128]{1,0:T(8,128)S(1)}, f32[40,128]{1,0:T(8,128)S(1)}, u32[]{:S(2)}, u32[]{:S(2)}) %collective-permute-start.7) | collective-permute-done | bytes 20512 | tf_op jit(solution)/shard_map/ppermute | solution.py:51
  24.5 0.0 collective-permute-done.8
  24.5 0.0 collective-permute-done.9
  24.5 0.4 %collective-permute-start.11 = (f32[40,128]{1,0:T(8,128)S(1)}, f32[40,128]{1,0:T(8,128)S(1)}, u32[]{:S(2)}, u32[]{:S(2)}) collective-permute-start(f32[40,128]{1,0:T(8,128)S(1)} %add_add_fusion), channel_id=1, source_target_pairs={{0,4},{1,5},{2,6},{3,7},{4,0},{5,1},{6,2},{7,3},{8,12},{9,13},{10,... | collective-permute-start | bytes 61448 | tf_op jit(solution)/shard_map/ppermute | solution.py:51
  25.0 0.8 %collective-permute-done.11 = f32[40,128]{1,0:T(8,128)S(1)} collective-permute-done((f32[40,128]{1,0:T(8,128)S(1)}, f32[40,128]{1,0:T(8,128)S(1)}, u32[]{:S(2)}, u32[]{:S(2)}) %collective-permute-start.11) | collective-permute-done | bytes 20512 | tf_op jit(solution)/shard_map/ppermute | solution.py:51
  25.8 3.1 %apply.1 = f32[64,3,8,256]{3,2,1,0:T(8,128)} custom-call(f32[40,128]{1,0:T(8,128)S(1)} %add.27.gram, bf16[128,3072]{1,0:T(8,128)(2,1)S(1)} %get-tuple-element.63.inner, f32[32,256]{1,0:T(8,128)S(1)} %get-tuple-element.64.inner_means, bf16[128,1536]{1,0:T(8,128)(2,1)S(1)} %get-tuple-element.65.near, f32[16,256]{1,0:T(8,128)S(1)} %get-tuple-element.66.near_means, ...), custom_call_target="tpu_custom_call" | custom-call | tf_op jit(solution)/shard_map/apply/pallas_call | solution.py:727
  (4 shorter events, 0.0 us)
Async XLA Ops:
  2.0 10.4 %collective-permute-start.2 = (f32[392,256]{1,0:T(8,128)S(1)}, f32[392,256]{1,0:T(8,128)S(1)}, u32[]{:S(2)}, u32[]{:S(2)}) collective-permute-start(f32[392,256]{1,0:T(8,128)S(1)} %get-tuple-element.57), channel_id=1, source_target_pairs={{0,4},{1,5},{2,6},{3,7},{4,0},{5,1},{6,2},{7,3},{8,12},{9,13},{10,... | collective-permute-start | bytes 1204232 | tf_op jit(solution)/shard_map/ppermute | solution.py:51
  2.5 9.9 %collective-permute-start.3 = (f32[392,256]{1,0:T(8,128)S(1)}, f32[392,256]{1,0:T(8,128)S(1)}, u32[]{:S(2)}, u32[]{:S(2)}) collective-permute-start(f32[392,256]{1,0:T(8,128)S(1)} %get-tuple-element.58), channel_id=1, source_target_pairs={{0,16},{1,17},{2,18},{3,19},{4,8},{5,9},{6,10},{7,11},{8,4},{9,5},... | collective-permute-start | bytes 1204232 | tf_op jit(solution)/shard_map/ppermute | solution.py:51
  5.1 4.0 %collective-permute-start = (f32[72,128]{1,0:T(8,128)S(1)}, f32[72,128]{1,0:T(8,128)S(1)}, u32[]{:S(2)}, u32[]{:S(2)}) collective-permute-start(f32[72,128]{1,0:T(8,128)S(1)} %get-tuple-element.39), channel_id=1, source_target_pairs={{0,1},{1,0},{2,3},{3,2},{4,5},{5,4},{6,7},{7,6},{8,9},{9,8},{10,11... | collective-permute-start | bytes 110600 | tf_op jit(solution)/shard_map/ppermute | solution.py:51
  6.7 2.4 %collective-permute-start.1 = (f32[72,128]{1,0:T(8,128)S(1)}, f32[72,128]{1,0:T(8,128)S(1)}, u32[]{:S(2)}, u32[]{:S(2)}) collective-permute-start(f32[72,128]{1,0:T(8,128)S(1)} %get-tuple-element.40), channel_id=1, source_target_pairs={{0,4},{1,2},{2,1},{3,7},{4,0},{5,6},{6,5},{7,3},{8,12},{9,10},{10,... | collective-permute-start | bytes 110600 | tf_op jit(solution)/shard_map/ppermute | solution.py:51
  9.1 5.0 %collective-permute-start.4 = (f32[72,128]{1,0:T(8,128)S(1)}, f32[72,128]{1,0:T(8,128)S(1)}, u32[]{:S(2)}, u32[]{:S(2)}) collective-permute-start(f32[72,128]{1,0:T(8,128)S(1)} %add.21.halo), channel_id=1, source_target_pairs={{0,4},{1,5},{2,6},{3,7},{4,0},{5,1},{6,2},{7,3},{8,12},{9,13},{10,... | collective-permute-start | bytes 110600 | tf_op jit(solution)/shard_map/ppermute | solution.py:51
  9.7 4.5 %collective-permute-start.5 = (f32[72,128]{1,0:T(8,128)S(1)}, f32[72,128]{1,0:T(8,128)S(1)}, u32[]{:S(2)}, u32[]{:S(2)}) collective-permute-start(f32[72,128]{1,0:T(8,128)S(1)} %add.21.halo), channel_id=1, source_target_pairs={{0,16},{1,17},{2,18},{3,19},{4,8},{5,9},{6,10},{7,11},{8,4},{9,5},... | collective-permute-start | bytes 110600 | tf_op jit(solution)/shard_map/ppermute | solution.py:51
  14.9 1.2 %collective-permute-start.6 = (f32[40,128]{1,0:T(8,128)S(1)}, f32[40,128]{1,0:T(8,128)S(1)}, u32[]{:S(2)}, u32[]{:S(2)}) collective-permute-start(f32[40,128]{1,0:T(8,128)S(1)} %get-tuple-element.62), channel_id=1, source_target_pairs={{0,4},{1,5},{2,6},{3,7},{4,0},{5,1},{6,2},{7,3},{8,12},{9,13},{10,... | collective-permute-start | bytes 61448 | tf_op jit(solution)/shard_map/ppermute | solution.py:51
  16.1 5.6 %collective-permute-start.10 = (f32[40,128]{1,0:T(8,128)S(1)}, f32[40,128]{1,0:T(8,128)S(1)}, u32[]{:S(2)}, u32[]{:S(2)}) collective-permute-start(f32[40,128]{1,0:T(8,128)S(1)} %add.22), channel_id=1, source_target_pairs={{0,3},{1,2},{2,1},{3,0},{4,15},{5,14},{6,13},{7,12},{8,11},{9,10},... | collective-permute-start | bytes 61448 | tf_op jit(solution)/shard_map/ppermute | solution.py:51
  19.4 5.2 %collective-permute-start.7 = (f32[40,128]{1,0:T(8,128)S(1)}, f32[40,128]{1,0:T(8,128)S(1)}, u32[]{:S(2)}, u32[]{:S(2)}) collective-permute-start(f32[40,128]{1,0:T(8,128)S(1)} %add.22), channel_id=1, source_target_pairs={{0,2},{1,3},{2,0},{3,1},{4,14},{5,15},{6,12},{7,13},{8,10},{9,11},... | collective-permute-start | bytes 61448 | tf_op jit(solution)/shard_map/ppermute | solution.py:51
  20.4 4.1 %collective-permute-start.8 = (f32[40,128]{1,0:T(8,128)S(1)}, f32[40,128]{1,0:T(8,128)S(1)}, u32[]{:S(2)}, u32[]{:S(2)}) collective-permute-start(f32[40,128]{1,0:T(8,128)S(1)} %add.22), channel_id=1, source_target_pairs={{0,1},{1,0},{2,3},{3,2},{4,13},{5,12},{6,15},{7,14},{8,9},{9,8},{1... | collective-permute-start | bytes 61448 | tf_op jit(solution)/shard_map/ppermute | solution.py:51
  20.5 4.0 %collective-permute-start.9 = (f32[40,128]{1,0:T(8,128)S(1)}, f32[40,128]{1,0:T(8,128)S(1)}, u32[]{:S(2)}, u32[]{:S(2)}) collective-permute-start(f32[40,128]{1,0:T(8,128)S(1)} %add.22), channel_id=1, source_target_pairs={{0,8},{1,9},{2,10},{3,11},{4,12},{5,13},{6,14},{7,15},{8,0},{9,1},... | collective-permute-start | bytes 61448 | tf_op jit(solution)/shard_map/ppermute | solution.py:51
  24.5 1.3 %collective-permute-start.11 = (f32[40,128]{1,0:T(8,128)S(1)}, f32[40,128]{1,0:T(8,128)S(1)}, u32[]{:S(2)}, u32[]{:S(2)}) collective-permute-start(f32[40,128]{1,0:T(8,128)S(1)} %add_add_fusion), channel_id=1, source_target_pairs={{0,4},{1,5},{2,6},{3,7},{4,0},{5,1},{6,2},{7,3},{8,12},{9,13},{10,... | collective-permute-start | bytes 61448 | tf_op jit(solution)/shard_map/ppermute | solution.py:51

commit v8 on v6

--- a/solution.py
+++ b/solution.py
@@ -369,8 +369,8 @@
                 moved[k + j : k + j + 16, at] = low
             pull = jnp.broadcast_to((s1 - mean * s2) * factor, (16, LANES))
             high, low = split_2(pull)
-            moved[2 * k : 2 * k + 16, at] = high
-            moved[2 * k + 16 : 2 * k + 32, at] = low
+            upper = lax.broadcasted_iota(jnp.int32, (16, 1), 0) < 8
+            moved[2 * k : 2 * k + 16, at] = jnp.where(upper, high.astype(F32), low.astype(F32)).astype(BF16)
         means[i * 8 : i * 8 + 8, lanes] = found
 
 
@@ -531,7 +531,7 @@
     got = partial[...] + nt(moved[...], anomalies[...])
     whole = got[:, 0:k] + got[:, k : 2 * k]
     matrix = whole[0:k] + whole[k : 2 * k]
-    pull = whole[2 * k : 2 * k + 8] + whole[2 * k + 16 : 2 * k + 24]
+    pull = whole[2 * k : 2 * k + 8] + whole[2 * k + 8 : 2 * k + 16]
     gram[0 : k // 2, :] = jnp.concatenate([matrix[0 : k // 2], matrix[k // 2 :]], axis=1)
     gram[k // 2 : k // 2 + 8, :] = jnp.concatenate([pull, pull], axis=1)
 
@@ -666,13 +666,13 @@
             shape((cx + 2) * block, cy),
             shape(2 * k, inner_rows * nv * cy, dtype=BF16),
             shape(inner_rows * 8, cy),
-            shape(2 * k + 32, 2 * k),
+            shape(2 * k + 16, 2 * k),
             shape(2 * block, cy),
         ],
         scratch_shapes=[
             pltpu.VMEM((k, LANES), F32),
             pltpu.VMEM((k, LANES), F32),
-            pltpu.VMEM((2 * k + 32, inner_rows * nv * cy), BF16),
+            pltpu.VMEM((2 * k + 16, inner_rows * nv * cy), BF16),
             pltpu.VMEM((4 * block, cy), F32),
         ],
         compiler_params=limits,
@@ -688,14 +688,14 @@
             shape((cx + 2) * block, cy),
             shape(2 * k, 2 * nv * cy, dtype=BF16),
             shape(2 * 8, cy),
-            shape(2 * k + 32, 2 * k),
+            shape(2 * k + 16, 2 * k),
             shape(2 * block, cy),
             shape((cx + 2) * 8, cy),
         ],
         scratch_shapes=[
             pltpu.VMEM((k, LANES), F32),
             pltpu.VMEM((k, LANES), F32),
-            pltpu.VMEM((2 * k + 32, 2 * nv * cy), BF16),
+            pltpu.VMEM((2 * k + 16, 2 * nv * cy), BF16),
             pltpu.VMEM((2 * block, cy), F32),
         ],
         input_output_aliases={1: 0, 2: 1},
@@ -715,7 +715,7 @@
         scratch_shapes=[
             pltpu.VMEM((k, LANES), F32),
             pltpu.VMEM((k, LANES), F32),
-            pltpu.VMEM((2 * k + 32, 2 * nv * cy), BF16),
+            pltpu.VMEM((2 * k + 16, 2 * nv * cy), BF16),
             pltpu.VMEM((2 * block, cy), F32),
         ],
         compiler_params=limits,

time: 29.1 us -> 29.1 us (level)
  no operation moved by 1% of the time
where the time goes in v8:
time: 29.1 us; the launch traced here: 29 us
  starting transfers between devices  12.2 us (42%)
  Pallas kernels  11.8 us (41%)
  waiting for transfers between devices  4.91 us (17%)
    ppermute x12, starting transfers between devices, pair_swap(): return lambda value: lax.ppermute(value, ('grp', 'gx', 'gy'), pairs)  12.2 us
    ppermute x12, waiting for transfers between devices, pair_swap(): return lambda value: lax.ppermute(value, ('grp', 'gx', 'gy'), pairs)  4.91 us
    pallas_call x1, Pallas kernels, local(): pl.pallas_call(functools.partial(apply_kernel, dims), name='apply', in_sp...  3.12 us
    pallas_call x1, Pallas kernels, local(): pl.pallas_call(functools.partial(middle_kernel, dims), name='middle', in_...  2.33 us
    pallas_call x1, Pallas kernels, local(): pl.pallas_call(functools.partial(load_kernel, dims), name='load', in_spec...  2.03 us
    pallas_call x1, Pallas kernels, local(): pl.pallas_call(functools.partial(inner_kernel, dims, factor), name='inner...  1.83 us
    pallas_call x1, Pallas kernels, local(): pl.pallas_call(functools.partial(rows_kernel, dims, factor), name='rows',...  1.75 us
    pallas_call x1, Pallas kernels, local(): pl.pallas_call(functools.partial(corner_kernel, dims, factor), name='corn...  0.74 us
  transfers between devices with their start and end apart: 12, of which 4 were waited for; matrix products, arithmetic and copies ran while one was open for 0% of the time, Pallas kernels for 20%

profile of v8, /device:TPU:0, one launch (start us, length us, event | category | flops | bytes accessed | tf_op | source)
XLA Modules:
  0.0 29.0 jit_solution(14604407503042557525)
XLA Ops:
  0.0 2.0 %load.1 = (f32[2304,256]{1,0:T(8,128)S(1)}, f32[392,256]{1,0:T(8,128)S(1)}, f32[392,256]{1,0:T(8,128)S(1)}, f32[72,128]{1,0:T(8,128)S(1)}, f32[72,128]{1,0:T(8,1...) custom-call(f32[1536,256]{1,0:T(8,128)} %bitcast.5, ...), custom_call_target="tpu_custom_call" | custom-call | tf_op jit(solution)/shard_map/load/pallas_call | solution.py:614
  2.0 0.5 %collective-permute-start.2 = (f32[392,256]{1,0:T(8,128)S(1)}, f32[392,256]{1,0:T(8,128)S(1)}, u32[]{:S(2)}, u32[]{:S(2)}) collective-permute-start(f32[392,256]{1,0:T(8,128)S(1)} %get-tuple-element.57), channel_id=1, source_target_pairs={{0,4},{1,5},{2,6},{3,7},{4,0},{5,1},{6,2},{7,3},{8,12},{9,13},{10,... | collective-permute-start | bytes 1204232 | tf_op jit(solution)/shard_map/ppermute | solution.py:51
  2.6 2.6 %collective-permute-start.3 = (f32[392,256]{1,0:T(8,128)S(1)}, f32[392,256]{1,0:T(8,128)S(1)}, u32[]{:S(2)}, u32[]{:S(2)}) collective-permute-start(f32[392,256]{1,0:T(8,128)S(1)} %get-tuple-element.58), channel_id=1, source_target_pairs={{0,16},{1,17},{2,18},{3,19},{4,8},{5,9},{6,10},{7,11},{8,4},{9,5},... | collective-permute-start | bytes 1204232 | tf_op jit(solution)/shard_map/ppermute | solution.py:51
  5.1 1.6 %collective-permute-start = (f32[72,128]{1,0:T(8,128)S(1)}, f32[72,128]{1,0:T(8,128)S(1)}, u32[]{:S(2)}, u32[]{:S(2)}) collective-permute-start(f32[72,128]{1,0:T(8,128)S(1)} %get-tuple-element.39), channel_id=1, source_target_pairs={{0,1},{1,0},{2,3},{3,2},{4,5},{5,4},{6,7},{7,6},{8,9},{9,8},{10,11... | collective-permute-start | bytes 110600 | tf_op jit(solution)/shard_map/ppermute | solution.py:51
  6.7 0.0 collective-permute-start.1
  6.7 2.3 %middle.1 = (f32[1920,256]{1,0:T(8,128)S(1)}, f32[80,256]{1,0:T(8,128)S(1)}, f32[64,256]{1,0:T(8,128)S(1)}, f32[1152,256]{1,0:T(8,128)S(1)}) custom-call(f32[3,3]{1,0:T(4,128)S(1)} %get-tuple-element.37.mixing, f32[2304,256]{1,0:T(8,128)S(1)} %get-tuple-element.38.state.state_in, f32[3,8,256]{2,1,0:T(8,128)S(1)} %get-tuple-element.41.kappa, ...), custom_call_target="tpu_custom_call" | custom-call | tf_op jit(solution)/shard_map/middle/pallas_call | solution.py:639
  9.1 0.0 collective-permute-done
  9.1 0.0 collective-permute-done.1
  9.1 0.6 %collective-permute-start.4 = (f32[72,128]{1,0:T(8,128)S(1)}, f32[72,128]{1,0:T(8,128)S(1)}, u32[]{:S(2)}, u32[]{:S(2)}) collective-permute-start(f32[72,128]{1,0:T(8,128)S(1)} %add.21.halo), channel_id=1, source_target_pairs={{0,4},{1,5},{2,6},{3,7},{4,0},{5,1},{6,2},{7,3},{8,12},{9,13},{10,... | collective-permute-start | bytes 110600 | tf_op jit(solution)/shard_map/ppermute | solution.py:51
  9.7 0.9 %collective-permute-start.5 = (f32[72,128]{1,0:T(8,128)S(1)}, f32[72,128]{1,0:T(8,128)S(1)}, u32[]{:S(2)}, u32[]{:S(2)}) collective-permute-start(f32[72,128]{1,0:T(8,128)S(1)} %add.21.halo), channel_id=1, source_target_pairs={{0,16},{1,17},{2,18},{3,19},{4,8},{5,9},{6,10},{7,11},{8,4},{9,5},... | collective-permute-start | bytes 110600 | tf_op jit(solution)/shard_map/ppermute | solution.py:51
  10.6 1.8 %inner.1 = (f32[1920,256]{1,0:T(8,128)S(1)}, bf16[128,3072]{1,0:T(8,128)(2,1)S(1)}, f32[32,256]{1,0:T(8,128)S(1)}, f32[144,128]{1,0:T(8,128)S(1)}, f32[384,256]{1,0:T(8,128)S(1)}) custom-call(f32[3,3]{1,0:T(4,128)S(1)} %get-tuple-element.37.mixing, f32[1920,256]{1,0:T(8,128)S(1)} %get-tuple-element.47.first_in, ...), custom_call_target="tpu_custom_call", output_to_operand_aliasing={{0}: (1, {})} | custom-call | tf_op jit(solution)/shard_map/inner/pallas_call | solution.py:659
  12.4 0.0 collective-permute-done.2.recv_a
  12.4 0.0 collective-permute-done.3.recv_b
  12.4 1.8 %rows.1 = (f32[2304,256]{1,0:T(8,128)S(1)}, f32[1920,256]{1,0:T(8,128)S(1)}, bf16[128,1536]{1,0:T(8,128)(2,1)S(1)}, f32[16,256]{1,0:T(8,128)S(1)}, f32[144,128]{...) custom-call(f32[3,3]{1,0:T(4,128)S(1)} %get-tuple-element.37.mixing,, ...), custom_call_target="tpu_custom_call", output_to_operand_aliasing={{0}: (1, {}), {1}: (2, {})} | custom-call | tf_op jit(solution)/shard_map/rows/pallas_call | solution.py:681
  14.2 0.0 collective-permute-done.4.corner_a
  14.2 0.0 collective-permute-done.5.corner_b
  14.2 0.7 %corner.1 = (bf16[128,1536]{1,0:T(8,128)(2,1)S(1)}, f32[16,256]{1,0:T(8,128)S(1)}, f32[40,128]{1,0:T(8,128)S(1)}) custom-call(f32[384,256]{1,0:T(8,128)S(1)} %get-tuple-element.59.outer, f32[144,128]{1,0:T(8,128)S(1)} %get-tuple-element.60.partial, f32[72,128]{1,0:T(8,128)S(1)} %add.21.halo, f32[72,128]{1,0:T(8,128)S(1)} %collective-permute-done.4.corner_a, ...), custom_call_target="tpu_custom_call" | custom-call | tf_op jit(solution)/shard_map/corner/pallas_call | solution.py:705
  14.9 0.2 collective-permute-start.6
  15.1 1.0 %collective-permute-done.6 = f32[40,128]{1,0:T(8,128)S(1)} collective-permute-done((f32[40,128]{1,0:T(8,128)S(1)}, f32[40,128]{1,0:T(8,128)S(1)}, u32[]{:S(2)}, u32[]{:S(2)}) %collective-permute-start.6) | collective-permute-done | bytes 20512 | tf_op jit(solution)/shard_map/ppermute | solution.py:51
  16.2 3.2 %collective-permute-start.10 = (f32[40,128]{1,0:T(8,128)S(1)}, f32[40,128]{1,0:T(8,128)S(1)}, u32[]{:S(2)}, u32[]{:S(2)}) collective-permute-start(f32[40,128]{1,0:T(8,128)S(1)} %add.22), channel_id=1, source_target_pairs={{0,3},{1,2},{2,1},{3,0},{4,15},{5,14},{6,13},{7,12},{8,11},{9,10},... | collective-permute-start | bytes 61448 | tf_op jit(solution)/shard_map/ppermute | solution.py:51
  19.4 1.0 %collective-permute-start.7 = (f32[40,128]{1,0:T(8,128)S(1)}, f32[40,128]{1,0:T(8,128)S(1)}, u32[]{:S(2)}, u32[]{:S(2)}) collective-permute-start(f32[40,128]{1,0:T(8,128)S(1)} %add.22), channel_id=1, source_target_pairs={{0,2},{1,3},{2,0},{3,1},{4,14},{5,15},{6,12},{7,13},{8,10},{9,11},... | collective-permute-start | bytes 61448 | tf_op jit(solution)/shard_map/ppermute | solution.py:51
  20.4 0.1 collective-permute-start.8
  20.5 1.0 %collective-permute-start.9 = (f32[40,128]{1,0:T(8,128)S(1)}, f32[40,128]{1,0:T(8,128)S(1)}, u32[]{:S(2)}, u32[]{:S(2)}) collective-permute-start(f32[40,128]{1,0:T(8,128)S(1)} %add.22), channel_id=1, source_target_pairs={{0,8},{1,9},{2,10},{3,11},{4,12},{5,13},{6,14},{7,15},{8,0},{9,1},... | collective-permute-start | bytes 61448 | tf_op jit(solution)/shard_map/ppermute | solution.py:51
  21.6 0.2 collective-permute-done.10
  21.7 2.8 %collective-permute-done.7 = f32[40,128]{1,0:T(8,128)S(1)} collective-permute-done((f32[40,128]{1,0:T(8,128)S(1)}, f32[40,128]{1,0:T(8,128)S(1)}, u32[]{:S(2)}, u32[]{:S(2)}) %collective-permute-start.7) | collective-permute-done | bytes 20512 | tf_op jit(solution)/shard_map/ppermute | solution.py:51
  24.5 0.0 collective-permute-done.8
  24.5 0.0 collective-permute-done.9
  24.6 0.4 %collective-permute-start.11 = (f32[40,128]{1,0:T(8,128)S(1)}, f32[40,128]{1,0:T(8,128)S(1)}, u32[]{:S(2)}, u32[]{:S(2)}) collective-permute-start(f32[40,128]{1,0:T(8,128)S(1)} %add_add_fusion), channel_id=1, source_target_pairs={{0,4},{1,5},{2,6},{3,7},{4,0},{5,1},{6,2},{7,3},{8,12},{9,13},{10,... | collective-permute-start | bytes 61448 | tf_op jit(solution)/shard_map/ppermute | solution.py:51
  25.0 0.8 %collective-permute-done.11 = f32[40,128]{1,0:T(8,128)S(1)} collective-permute-done((f32[40,128]{1,0:T(8,128)S(1)}, f32[40,128]{1,0:T(8,128)S(1)}, u32[]{:S(2)}, u32[]{:S(2)}) %collective-permute-start.11) | collective-permute-done | bytes 20512 | tf_op jit(solution)/shard_map/ppermute | solution.py:51
  25.9 3.1 %apply.1 = f32[64,3,8,256]{3,2,1,0:T(8,128)} custom-call(f32[40,128]{1,0:T(8,128)S(1)} %add.27.gram, bf16[128,3072]{1,0:T(8,128)(2,1)S(1)} %get-tuple-element.63.inner, f32[32,256]{1,0:T(8,128)S(1)} %get-tuple-element.64.inner_means, bf16[128,1536]{1,0:T(8,128)(2,1)S(1)} %get-tuple-element.65.near, f32[16,256]{1,0:T(8,128)S(1)} %get-tuple-element.66.near_means, ...), custom_call_target="tpu_custom_call" | custom-call | tf_op jit(solution)/shard_map/apply/pallas_call | solution.py:726
  (4 shorter events, 0.0 us)
Async XLA Ops:
  2.0 10.4 %collective-permute-start.2 = (f32[392,256]{1,0:T(8,128)S(1)}, f32[392,256]{1,0:T(8,128)S(1)}, u32[]{:S(2)}, u32[]{:S(2)}) collective-permute-start(f32[392,256]{1,0:T(8,128)S(1)} %get-tuple-element.57), channel_id=1, source_target_pairs={{0,4},{1,5},{2,6},{3,7},{4,0},{5,1},{6,2},{7,3},{8,12},{9,13},{10,... | collective-permute-start | bytes 1204232 | tf_op jit(solution)/shard_map/ppermute | solution.py:51
  2.6 9.9 %collective-permute-start.3 = (f32[392,256]{1,0:T(8,128)S(1)}, f32[392,256]{1,0:T(8,128)S(1)}, u32[]{:S(2)}, u32[]{:S(2)}) collective-permute-start(f32[392,256]{1,0:T(8,128)S(1)} %get-tuple-element.58), channel_id=1, source_target_pairs={{0,16},{1,17},{2,18},{3,19},{4,8},{5,9},{6,10},{7,11},{8,4},{9,5},... | collective-permute-start | bytes 1204232 | tf_op jit(solution)/shard_map/ppermute | solution.py:51
  5.1 4.0 %collective-permute-start = (f32[72,128]{1,0:T(8,128)S(1)}, f32[72,128]{1,0:T(8,128)S(1)}, u32[]{:S(2)}, u32[]{:S(2)}) collective-permute-start(f32[72,128]{1,0:T(8,128)S(1)} %get-tuple-element.39), channel_id=1, source_target_pairs={{0,1},{1,0},{2,3},{3,2},{4,5},{5,4},{6,7},{7,6},{8,9},{9,8},{10,11... | collective-permute-start | bytes 110600 | tf_op jit(solution)/shard_map/ppermute | solution.py:51
  6.7 2.4 %collective-permute-start.1 = (f32[72,128]{1,0:T(8,128)S(1)}, f32[72,128]{1,0:T(8,128)S(1)}, u32[]{:S(2)}, u32[]{:S(2)}) collective-permute-start(f32[72,128]{1,0:T(8,128)S(1)} %get-tuple-element.40), channel_id=1, source_target_pairs={{0,4},{1,2},{2,1},{3,7},{4,0},{5,6},{6,5},{7,3},{8,12},{9,10},{10,... | collective-permute-start | bytes 110600 | tf_op jit(solution)/shard_map/ppermute | solution.py:51
  9.1 5.1 %collective-permute-start.4 = (f32[72,128]{1,0:T(8,128)S(1)}, f32[72,128]{1,0:T(8,128)S(1)}, u32[]{:S(2)}, u32[]{:S(2)}) collective-permute-start(f32[72,128]{1,0:T(8,128)S(1)} %add.21.halo), channel_id=1, source_target_pairs={{0,4},{1,5},{2,6},{3,7},{4,0},{5,1},{6,2},{7,3},{8,12},{9,13},{10,... | collective-permute-start | bytes 110600 | tf_op jit(solution)/shard_map/ppermute | solution.py:51
  9.7 4.5 %collective-permute-start.5 = (f32[72,128]{1,0:T(8,128)S(1)}, f32[72,128]{1,0:T(8,128)S(1)}, u32[]{:S(2)}, u32[]{:S(2)}) collective-permute-start(f32[72,128]{1,0:T(8,128)S(1)} %add.21.halo), channel_id=1, source_target_pairs={{0,16},{1,17},{2,18},{3,19},{4,8},{5,9},{6,10},{7,11},{8,4},{9,5},... | collective-permute-start | bytes 110600 | tf_op jit(solution)/shard_map/ppermute | solution.py:51
  14.9 1.2 %collective-permute-start.6 = (f32[40,128]{1,0:T(8,128)S(1)}, f32[40,128]{1,0:T(8,128)S(1)}, u32[]{:S(2)}, u32[]{:S(2)}) collective-permute-start(f32[40,128]{1,0:T(8,128)S(1)} %get-tuple-element.62), channel_id=1, source_target_pairs={{0,4},{1,5},{2,6},{3,7},{4,0},{5,1},{6,2},{7,3},{8,12},{9,13},{10,... | collective-permute-start | bytes 61448 | tf_op jit(solution)/shard_map/ppermute | solution.py:51
  16.2 5.6 %collective-permute-start.10 = (f32[40,128]{1,0:T(8,128)S(1)}, f32[40,128]{1,0:T(8,128)S(1)}, u32[]{:S(2)}, u32[]{:S(2)}) collective-permute-start(f32[40,128]{1,0:T(8,128)S(1)} %add.22), channel_id=1, source_target_pairs={{0,3},{1,2},{2,1},{3,0},{4,15},{5,14},{6,13},{7,12},{8,11},{9,10},... | collective-permute-start | bytes 61448 | tf_op jit(solution)/shard_map/ppermute | solution.py:51
  19.4 5.2 %collective-permute-start.7 = (f32[40,128]{1,0:T(8,128)S(1)}, f32[40,128]{1,0:T(8,128)S(1)}, u32[]{:S(2)}, u32[]{:S(2)}) collective-permute-start(f32[40,128]{1,0:T(8,128)S(1)} %add.22), channel_id=1, source_target_pairs={{0,2},{1,3},{2,0},{3,1},{4,14},{5,15},{6,12},{7,13},{8,10},{9,11},... | collective-permute-start | bytes 61448 | tf_op jit(solution)/shard_map/ppermute | solution.py:51
  20.4 4.1 %collective-permute-start.8 = (f32[40,128]{1,0:T(8,128)S(1)}, f32[40,128]{1,0:T(8,128)S(1)}, u32[]{:S(2)}, u32[]{:S(2)}) collective-permute-start(f32[40,128]{1,0:T(8,128)S(1)} %add.22), channel_id=1, source_target_pairs={{0,1},{1,0},{2,3},{3,2},{4,13},{5,12},{6,15},{7,14},{8,9},{9,8},{1... | collective-permute-start | bytes 61448 | tf_op jit(solution)/shard_map/ppermute | solution.py:51
  20.5 4.0 %collective-permute-start.9 = (f32[40,128]{1,0:T(8,128)S(1)}, f32[40,128]{1,0:T(8,128)S(1)}, u32[]{:S(2)}, u32[]{:S(2)}) collective-permute-start(f32[40,128]{1,0:T(8,128)S(1)} %add.22), channel_id=1, source_target_pairs={{0,8},{1,9},{2,10},{3,11},{4,12},{5,13},{6,14},{7,15},{8,0},{9,1},... | collective-permute-start | bytes 61448 | tf_op jit(solution)/shard_map/ppermute | solution.py:51
  24.6 1.3 %collective-permute-start.11 = (f32[40,128]{1,0:T(8,128)S(1)}, f32[40,128]{1,0:T(8,128)S(1)}, u32[]{:S(2)}, u32[]{:S(2)}) collective-permute-start(f32[40,128]{1,0:T(8,128)S(1)} %add_add_fusion), channel_id=1, source_target_pairs={{0,4},{1,5},{2,6},{3,7},{4,0},{5,1},{6,2},{7,3},{8,12},{9,13},{10,... | collective-permute-start | bytes 61448 | tf_op jit(solution)/shard_map/ppermute | solution.py:51
